TPU v7x, 512 devices: a whole 4x4x16 slice. The times are simulated.
512 devices in a mesh: tok: 32 (over x, z_lo), exp: 16 (over y, z_hi, core).
Axes of the slice: x: 4, y: 4, z: 16 (z_hi: 2, z_lo: 8; z = z_hi * 8 + z_lo), core: 2. Of those that a mesh axis runs over, the one named last changes fastest.
Arguments:
- tokens_x: bfloat16 [5120, 4096], P('tok', 'exp'), may hold values from -6 to 6
- out_grad: bfloat16 [5120, 4096], P('tok', 'exp'), may hold values from -12 to 12
- expert_ids: int32 [5120, 8], P('tok'), may hold values from 0 to 127, as said below
- route_q: int32 [5120, 8], P('tok'), may hold values from 1 to 255
- gate_w: bfloat16 [16, 1536, 4096], P('exp', 'tok'), may hold values from -0.09375 to 0.09375
- up_w: bfloat16 [16, 1536, 4096], P('exp', 'tok'), may hold values from -0.09375 to 0.09375
- down_w: bfloat16 [16, 1536, 4096], P('exp', 'tok'), may hold values from -0.15625 to 0.15625
Outputs:
- input_factor: float32 [16, 4096, 4096], P('exp', 'tok')
- grad_factor: float32 [16, 1536, 1536], P('exp', 'tok')
Inputs may be any that keep to these rules, and one draw needn't show every extreme that they name: `expert_ids`: each token names exactly one expert from each range of 16 ids that starts at a multiple of 16, in varying positions of its row. Within the rows of one index of tok (aligned blocks of 160 rows) no expert below 16 is named by more than 20 rows, and in every draw one expert below 16 is named by exactly 20 rows in every block.
All inputs are finite; a program needn't handle non-finite values.
Results may differ from a plain program's by a relative error of at most 0.0056.
Values may be sent and summed in bfloat16 or wider, within the bound.
No kernel may reach another device: no remote copies, remote signals or barrier semaphores. Data moves between devices by JAX's collectives and lax.ppermute only.
A program may use at most 64 MiB of HBM per device.

v0:
```python
import jax
import jax.numpy as jnp
from jax import lax
from jax.sharding import Mesh, PartitionSpec as P


F32 = jnp.float32
BF16 = jnp.bfloat16


def silu_slope(values):
    sigma = jax.nn.sigmoid(values)
    return sigma * (1.0 + values * (1.0 - sigma))


def dot_nt(a, b):
    return lax.dot_general(a, b, (((1,), (1,)), ((), ())), preferred_element_type=F32)


def dot_tn(a, b):
    return lax.dot_general(a, b, (((0,), (0,)), ((), ())), preferred_element_type=F32)


def body(tokens_x, out_grad, expert_ids, route_q, gate_w, up_w, down_w):
    nx = lax.axis_size("x")
    nz = lax.axis_size("zl")
    owners = lax.axis_size("y") * lax.axis_size("zh") * lax.axis_size("c")
    xi = lax.axis_index("x")
    zi = lax.axis_index("zl")
    tok_rows, local_width = tokens_x.shape
    capacity = 2 * tok_rows // owners
    slot_count = capacity * nx * nz
    full_width = local_width * owners
    hid = gate_w.shape[1]

    fitted = expert_ids < owners
    fitted_id = jnp.sum(jnp.where(fitted, expert_ids, 0), axis=1)
    route_weight = jnp.sum(jnp.where(fitted, route_q, 0), axis=1).astype(F32) / 256.0
    onehot = (fitted_id[:, None] == jnp.arange(owners, dtype=jnp.int32)[None, :]).astype(jnp.int32)
    running = jnp.cumsum(onehot, axis=0)
    rank_in = jnp.sum(running * onehot, axis=1) - 1
    row_ids = fitted_id * (2 * capacity) + rank_in
    scaled = (route_weight[:, None] * out_grad.astype(F32)).astype(BF16)
    both_ids = jnp.concatenate([row_ids, row_ids + capacity])
    packer = (both_ids[None, :] == jnp.arange(owners * 2 * capacity, dtype=jnp.int32)[:, None]).astype(BF16)
    both = jnp.concatenate([tokens_x, scaled], axis=0)
    packed = jnp.dot(packer, both, preferred_element_type=F32).astype(BF16)
    packed = packed.reshape(owners, 2 * capacity, local_width)
    recv = lax.all_to_all(packed, ("y", "zh", "c"), split_axis=0, concat_axis=0, tiled=True)
    own = recv.transpose(1, 0, 2).reshape(2 * capacity, full_width)

    def swap_x(v, k):
        return lax.ppermute(v, "x", [(i, i ^ k) for i in range(nx)])

    zero = (recv[0, :1, :1] * 0).reshape(1, 1)
    w_own = jnp.concatenate([gate_w[0], up_w[0], down_w[0]], axis=0) + zero
    weights = [w_own] + [swap_x(w_own, k) for k in range(1, nx)]

    order = list(range(0, nz, 2)) + list(range(nz - 1, 0, -2))
    pairs = [(order[i], order[(i + 1) % nz]) for i in range(nz)]
    parts = [own]
    for _ in range(1, nz):
        parts.append(lax.ppermute(parts[-1], "zl", pairs))

    half = nz // 2
    group = nx * hid
    slots = nz * capacity
    place = jnp.where(zi % 2 == 0, zi // 2, nz - 1 - zi // 2)
    unit = jnp.arange(group, dtype=jnp.int32)
    from_unit = ((unit // hid) ^ xi) * hid + unit % hid
    unit_perm = (from_unit[:, None] == unit[None, :]).astype(BF16)
    column = jnp.arange(half * 2 * capacity, dtype=jnp.int32)
    slot = jnp.arange(slots, dtype=jnp.int32)

    sorted_f32 = 0.0
    x_half = []
    for h in range(2):
        rows = jnp.concatenate(parts[h * half : (h + 1) * half], axis=0)
        x_half.append(
            rows.reshape(half, 2 * capacity, full_width)[:, :capacity].reshape(half * capacity, full_width)
        )
        pre = []
        for w in weights:
            pre.append(dot_nt(w, rows))
        pre = jnp.stack(pre)
        gate_pre, up_pre = pre[:, :hid], pre[:, hid : 2 * hid]
        hidden_grad = jnp.roll(pre[:, 2 * hid :], -capacity, axis=2)
        gate_grad = (hidden_grad * up_pre * silu_slope(gate_pre)).astype(BF16).reshape(group, -1)
        arrival = h * half + column // (2 * capacity)
        within = column % (2 * capacity)
        target = jnp.where(within < capacity, ((place - arrival + nz) % nz) * capacity + within, -1)
        slot_perm = (slot[:, None] == target[None, :]).astype(BF16)
        sorted_f32 = sorted_f32 + dot_nt(slot_perm, gate_grad)
    g_sorted = jnp.dot(sorted_f32.astype(BF16), unit_perm, preferred_element_type=F32).astype(BF16)

    wide = jnp.concatenate([g_sorted[: slots // 2], g_sorted[slots // 2 :]], axis=1)
    spread = jnp.broadcast_to(wide[None], (nz,) + wide.shape)
    spread = lax.all_to_all(spread, "zl", split_axis=0, concat_axis=0, tiled=True)
    spread = spread.reshape(nz, slots // 2, 2, nx, hid).transpose(2, 1, 3, 0, 4)
    spread = spread.reshape(slots, nx * nz * hid)
    part_sent = dot_tn(g_sorted, spread).astype(BF16).reshape(nx, hid, nx * nz * hid)
    part = lax.all_to_all(part_sent, "x", split_axis=0, concat_axis=0, tiled=True)
    grad_rows = jnp.sum(part.astype(F32), axis=0) / float(slot_count)

    strip_width = full_width // (nx * nz)
    late = (part_sent[0, :1, :1] * 0).reshape(1, 1)
    input_rows = 0.0
    for name, piece in zip(("xa", "xb"), x_half):
        own_piece = piece if name == "xa" else piece + late
        gathered = [own_piece] + [swap_x(piece, k) for k in range(1, nx)]
        rows = jnp.concatenate(gathered, axis=0)
        strip = lax.dynamic_slice_in_dim(rows, (xi * nz + zi) * strip_width, strip_width, 1)
        input_rows = input_rows + dot_tn(strip, rows) / float(slot_count)
    return (input_rows[None], grad_rows[None])


def solution(mesh):
    fine = Mesh(mesh.devices.reshape(4, 8, 4, 2, 2), ("x", "zl", "y", "zh", "c"))
    tok, exp = ("x", "zl"), ("y", "zh", "c")
    placed = (
        P(tok, exp),
        P(tok, exp),
        P(tok, None),
        P(tok, None),
        P(exp, tok, None),
        P(exp, tok, None),
        P(exp, tok, None),
    )
    return jax.shard_map(
        body,
        mesh=fine,
        in_specs=placed,
        out_specs=(P(exp, tok, None), P(exp, tok, None)),
        check_vma=False,
    )
```

profile of v0, /device:TPU:2, one launch (start us, length us, event | category | flops | bytes accessed | tf_op | source)
XLA Modules:
  0.0 219.3 jit_solution(6280583563777437558)
XLA Ops:
  0.7 0.8 fusion.23
  1.5 0.6 reduce-window.6
  2.1 0.2 slice_reduce_fusion
  2.5 1.0 multiply_convert_fusion
  3.5 1.9 convolution_convert_fusion.1
  5.5 17.8 %all-to-all-start = ((bf16[16,40,256]{2,1,0:T(8,128)(2,1)}), bf16[16,40,256]{2,1,0:T(8,128)(2,1)S(1)}, u32[]{:S(2)}, u32[]{:S(2)}) async-start(bf16[16,40,256]{2,1,0:T(8,128)(2,1)} %bitcast.1), calls=%async_computation | async-start | bytes 655360 | tf_op jit(solution)/shard_map/all_to_all | solution.py:49
  23.4 17.9 %all-to-all-done = bf16[16,40,256]{2,1,0:T(8,128)(2,1)S(1)} async-done(((bf16[16,40,256]{2,1,0:T(8,128)(2,1)}), bf16[16,40,256]{2,1,0:T(8,128)(2,1)S(1)}, u32[]{:S(2)}, u32[]{:S(2)}) %all-to-all-start) | async-done | bytes 327712 | tf_op jit(solution)/shard_map/all_to_all | solution.py:49
  41.3 0.5 slice.80
  42.5 0.2 maximum_add_fusion
  42.7 3.4 %collective-permute-start.12 = (bf16[144,4096]{1,0:T(8,128)(2,1)S(1)}, bf16[144,4096]{1,0:T(8,128)(2,1)}, u32[]{:S(2)}, u32[]{:S(2)}) collective-permute-start(bf16[144,4096]{1,0:T(8,128)(2,1)S(1)} %maximum_add_fusion), channel_id=1, source_target_pairs={{0,384},{128,256},{256,128},{384,0},{1,385},{129,257},{257,129},{3... | collective-permute-start | bytes 3538952 | tf_op jit(solution)/shard_map/ppermute | solution.py:53
  46.1 3.0 %collective-permute-start.11 = (bf16[144,4096]{1,0:T(8,128)(2,1)S(1)}, bf16[144,4096]{1,0:T(8,128)(2,1)}, u32[]{:S(2)}, u32[]{:S(2)}) collective-permute-start(bf16[144,4096]{1,0:T(8,128)(2,1)S(1)} %maximum_add_fusion), channel_id=1, source_target_pairs={{0,256},{128,384},{256,0},{384,128},{1,257},{129,385},{257,1},{385... | collective-permute-start | bytes 3538952 | tf_op jit(solution)/shard_map/ppermute | solution.py:53
  49.1 3.4 %collective-permute-start.10 = (bf16[144,4096]{1,0:T(8,128)(2,1)S(1)}, bf16[144,4096]{1,0:T(8,128)(2,1)}, u32[]{:S(2)}, u32[]{:S(2)}) collective-permute-start(bf16[144,4096]{1,0:T(8,128)(2,1)S(1)} %maximum_add_fusion), channel_id=1, source_target_pairs={{0,128},{128,0},{256,384},{384,256},{1,129},{129,1},{257,385},{385... | collective-permute-start | bytes 3538952 | tf_op jit(solution)/shard_map/ppermute | solution.py:53
  52.6 9.9 %collective-permute-start = (bf16[40,4096]{1,0:T(8,128)(2,1)S(1)}, bf16[40,4096]{1,0:T(8,128)(2,1)S(1)}, u32[]{:S(2)}, u32[]{:S(2)}) collective-permute-start(bf16[40,4096]{1,0:T(8,128)(2,1)S(1)} %bitcast.77), channel_id=1, source_target_pairs={{0,32},{32,64},{64,96},{96,112},{112,80},{80,48},{48,16},{16,0},{1... | collective-permute-start | bytes 983048 | tf_op jit(solution)/shard_map/ppermute | solution.py:63
  62.5 9.3 %collective-permute-done = bf16[40,4096]{1,0:T(8,128)(2,1)S(1)} collective-permute-done((bf16[40,4096]{1,0:T(8,128)(2,1)S(1)}, bf16[40,4096]{1,0:T(8,128)(2,1)S(1)}, u32[]{:S(2)}, u32[]{:S(2)}) %collective-permute-start) | collective-permute-done | bytes 327712 | tf_op jit(solution)/shard_map/ppermute | solution.py:63
  71.9 1.9 collective-permute-start.1
  73.8 8.2 %collective-permute-done.1 = bf16[40,4096]{1,0:T(8,128)(2,1)S(1)} collective-permute-done((bf16[40,4096]{1,0:T(8,128)(2,1)S(1)}, bf16[40,4096]{1,0:T(8,128)(2,1)S(1)}, u32[]{:S(2)}, u32[]{:S(2)}) %collective-permute-start.1) | collective-permute-done | bytes 327712 | tf_op jit(solution)/shard_map/ppermute | solution.py:63
  82.0 2.5 %collective-permute-start.2 = (bf16[40,4096]{1,0:T(8,128)(2,1)S(1)}, bf16[40,4096]{1,0:T(8,128)(2,1)S(1)}, u32[]{:S(2)}, u32[]{:S(2)}) collective-permute-start(bf16[40,4096]{1,0:T(8,128)(2,1)S(1)} %collective-permute-done.1), channel_id=1, source_target_pairs={{0,32},{32,64},{64,96},{96,112},{112,80},{80,48},{48,16},{16,0},{1... | collective-permute-start | bytes 983048 | tf_op jit(solution)/shard_map/ppermute | solution.py:63
  84.5 7.1 %collective-permute-done.2 = bf16[40,4096]{1,0:T(8,128)(2,1)S(1)} collective-permute-done((bf16[40,4096]{1,0:T(8,128)(2,1)S(1)}, bf16[40,4096]{1,0:T(8,128)(2,1)S(1)}, u32[]{:S(2)}, u32[]{:S(2)}) %collective-permute-start.2) | collective-permute-done | bytes 327712 | tf_op jit(solution)/shard_map/ppermute | solution.py:63
  91.6 0.7 copy-done.4
  92.4 1.0 reshape.148
  93.4 3.5 %collective-permute-start.5 = (bf16[80,4096]{1,0:T(8,128)(2,1)}, bf16[80,4096]{1,0:T(8,128)(2,1)}, u32[]{:S(2)}, u32[]{:S(2)}) collective-permute-start(bf16[80,4096]{1,0:T(8,128)(2,1)} %reshape.148), channel_id=1, source_target_pairs={{0,384},{128,256},{256,128},{384,0},{1,385},{129,257},{257,129},{3... | collective-permute-start | bytes 1966088 | tf_op jit(solution)/shard_map/ppermute | solution.py:53
  96.9 3.0 %collective-permute-start.4 = (bf16[80,4096]{1,0:T(8,128)(2,1)}, bf16[80,4096]{1,0:T(8,128)(2,1)}, u32[]{:S(2)}, u32[]{:S(2)}) collective-permute-start(bf16[80,4096]{1,0:T(8,128)(2,1)} %reshape.148), channel_id=1, source_target_pairs={{0,256},{128,384},{256,0},{384,128},{1,257},{129,385},{257,1},{385... | collective-permute-start | bytes 1966088 | tf_op jit(solution)/shard_map/ppermute | solution.py:53
  100.0 0.5 convolution_bitcast_fusion.7
  100.5 3.5 %collective-permute-start.3 = (bf16[80,4096]{1,0:T(8,128)(2,1)S(1)}, bf16[80,4096]{1,0:T(8,128)(2,1)}, u32[]{:S(2)}, u32[]{:S(2)}) collective-permute-start(bf16[80,4096]{1,0:T(8,128)(2,1)S(1)} %copy-done), channel_id=1, source_target_pairs={{0,128},{128,0},{256,384},{384,256},{1,129},{129,1},{257,385},{385... | collective-permute-start | bytes 1966088 | tf_op jit(solution)/shard_map/ppermute | solution.py:53
  104.0 1.8 convolution_bitcast_fusion.4
  105.9 13.4 %collective-permute-start.6 = (bf16[40,4096]{1,0:T(8,128)(2,1)S(1)}, bf16[40,4096]{1,0:T(8,128)(2,1)S(1)}, u32[]{:S(2)}, u32[]{:S(2)}) collective-permute-start(bf16[40,4096]{1,0:T(8,128)(2,1)S(1)} %copy-done.5), channel_id=1, source_target_pairs={{0,32},{32,64},{64,96},{96,112},{112,80},{80,48},{48,16},{16,0},{1... | collective-permute-start | bytes 983048 | tf_op jit(solution)/shard_map/ppermute | solution.py:63
  119.2 1.8 convolution_bitcast_fusion.5
  121.0 1.8 convolution_bitcast_fusion.6
  123.1 0.2 fusion.13
  123.3 3.6 %collective-permute-done.6 = bf16[40,4096]{1,0:T(8,128)(2,1)S(1)} collective-permute-done((bf16[40,4096]{1,0:T(8,128)(2,1)S(1)}, bf16[40,4096]{1,0:T(8,128)(2,1)S(1)}, u32[]{:S(2)}, u32[]{:S(2)}) %collective-permute-start.6) | collective-permute-done | bytes 327712 | tf_op jit(solution)/shard_map/ppermute | solution.py:63
  126.9 5.3 %collective-permute-start.7 = (bf16[40,4096]{1,0:T(8,128)(2,1)S(1)}, bf16[40,4096]{1,0:T(8,128)(2,1)S(1)}, u32[]{:S(2)}, u32[]{:S(2)}) collective-permute-start(bf16[40,4096]{1,0:T(8,128)(2,1)S(1)} %collective-permute-done.6), channel_id=1, source_target_pairs={{0,32},{32,64},{64,96},{96,112},{112,80},{80,48},{48,16},{16,0},{1... | collective-permute-start | bytes 983048 | tf_op jit(solution)/shard_map/ppermute | solution.py:63
  132.2 7.3 %collective-permute-done.7 = bf16[40,4096]{1,0:T(8,128)(2,1)S(1)} collective-permute-done((bf16[40,4096]{1,0:T(8,128)(2,1)S(1)}, bf16[40,4096]{1,0:T(8,128)(2,1)S(1)}, u32[]{:S(2)}, u32[]{:S(2)}) %collective-permute-start.7) | collective-permute-done | bytes 327712 | tf_op jit(solution)/shard_map/ppermute | solution.py:63
  139.5 5.3 %collective-permute-start.8 = (bf16[40,4096]{1,0:T(8,128)(2,1)S(1)}, bf16[40,4096]{1,0:T(8,128)(2,1)S(1)}, u32[]{:S(2)}, u32[]{:S(2)}) collective-permute-start(bf16[40,4096]{1,0:T(8,128)(2,1)S(1)} %collective-permute-done.7), channel_id=1, source_target_pairs={{0,32},{32,64},{64,96},{96,112},{112,80},{80,48},{48,16},{16,0},{1... | collective-permute-start | bytes 983048 | tf_op jit(solution)/shard_map/ppermute | solution.py:63
  144.9 6.4 %collective-permute-done.8 = bf16[40,4096]{1,0:T(8,128)(2,1)S(1)} collective-permute-done((bf16[40,4096]{1,0:T(8,128)(2,1)S(1)}, bf16[40,4096]{1,0:T(8,128)(2,1)S(1)}, u32[]{:S(2)}, u32[]{:S(2)}) %collective-permute-start.8) | collective-permute-done | bytes 327712 | tf_op jit(solution)/shard_map/ppermute | solution.py:63
  151.3 5.3 %collective-permute-start.9 = (bf16[40,4096]{1,0:T(8,128)(2,1)S(1)}, bf16[40,4096]{1,0:T(8,128)(2,1)S(1)}, u32[]{:S(2)}, u32[]{:S(2)}) collective-permute-start(bf16[40,4096]{1,0:T(8,128)(2,1)S(1)} %collective-permute-done.8), channel_id=1, source_target_pairs={{0,32},{32,64},{64,96},{96,112},{112,80},{80,48},{48,16},{16,0},{1... | collective-permute-start | bytes 983048 | tf_op jit(solution)/shard_map/ppermute | solution.py:63
  156.6 4.5 %collective-permute-done.9 = bf16[40,4096]{1,0:T(8,128)(2,1)S(1)} collective-permute-done((bf16[40,4096]{1,0:T(8,128)(2,1)S(1)}, bf16[40,4096]{1,0:T(8,128)(2,1)S(1)}, u32[]{:S(2)}, u32[]{:S(2)}) %collective-permute-start.9) | collective-permute-done | bytes 327712 | tf_op jit(solution)/shard_map/ppermute | solution.py:63
  161.2 0.5 convolution_bitcast_fusion.3
  161.7 1.8 convolution_bitcast_fusion
  163.5 1.8 convolution_bitcast_fusion.1
  165.3 1.8 convolution_bitcast_fusion.2
  167.3 0.1 fusion.5
  167.4 0.3 convolution_convert_fusion.2
  167.8 0.8 broadcast_in_dim.13
  168.6 9.0 %all-to-all-start.1 = ((bf16[8,80,384]{2,1,0:T(8,128)(2,1)}), bf16[8,80,384]{2,1,0:T(8,128)(2,1)}, u32[]{:S(2)}, u32[]{:S(2)}) async-start(bf16[8,80,384]{2,1,0:T(8,128)(2,1)} %broadcast_in_dim.13), calls=%async_computation.1 | async-start | bytes 983040 | tf_op jit(solution)/shard_map/all_to_all | solution.py:98
  177.6 0.9 constant_dynamic-update-slice_fusion.7
  178.5 2.0 constant_dynamic-update-slice_fusion.6
  180.5 2.0 constant_dynamic-update-slice_fusion.5
  182.5 2.0 constant_dynamic-update-slice_fusion.4
  184.5 0.1 reshape.150
  184.7 1.9 collective-permute-start.15
  186.6 4.1 %collective-permute-start.14 = (bf16[80,4096]{1,0:T(8,128)(2,1)S(1)}, bf16[80,4096]{1,0:T(8,128)(2,1)}, u32[]{:S(2)}, u32[]{:S(2)}) collective-permute-start(bf16[80,4096]{1,0:T(8,128)(2,1)S(1)} %reshape.150), channel_id=1, source_target_pairs={{0,256},{128,384},{256,0},{384,128},{1,257},{129,385},{257,1},{385... | collective-permute-start | bytes 1966088 | tf_op jit(solution)/shard_map/ppermute | solution.py:53
  190.7 3.8 %collective-permute-start.13 = (bf16[80,4096]{1,0:T(8,128)(2,1)S(1)}, bf16[80,4096]{1,0:T(8,128)(2,1)}, u32[]{:S(2)}, u32[]{:S(2)}) collective-permute-start(bf16[80,4096]{1,0:T(8,128)(2,1)S(1)} %reshape.150), channel_id=1, source_target_pairs={{0,128},{128,0},{256,384},{384,256},{1,129},{129,1},{257,385},{385... | collective-permute-start | bytes 1966088 | tf_op jit(solution)/shard_map/ppermute | solution.py:53
  194.5 1.4 copy.18
  195.9 0.8 copy.19
  196.8 0.4 reshape.154
  197.2 1.2 convolution_convert_fusion
  198.5 1.2 slice.89
  199.7 3.6 %all-to-all-start.2 = ((bf16[4,48,1536]{2,1,0:T(8,128)(2,1)}), bf16[4,48,1536]{2,1,0:T(8,128)(2,1)S(1)}, u32[]{:S(2)}, u32[]{:S(2)}) async-start(bf16[4,48,1536]{2,1,0:T(8,128)(2,1)} %bitcast.21), calls=%async_computation.2 | async-start | bytes 1179648 | tf_op jit(solution)/shard_map/all_to_all | solution.py:102
  204.0 4.5 %collective-permute-done.15 = bf16[80,4096]{1,0:T(8,128)(2,1)S(1)} collective-permute-done((bf16[80,4096]{1,0:T(8,128)(2,1)S(1)}, bf16[80,4096]{1,0:T(8,128)(2,1)S(1)}, u32[]{:S(2)}, u32[]{:S(2)}) %collective-permute-start.15) | collective-permute-done | bytes 655392 | tf_op jit(solution)/shard_map/ppermute | solution.py:53
  208.5 3.9 %collective-permute-done.13 = bf16[80,4096]{1,0:T(8,128)(2,1)} collective-permute-done((bf16[80,4096]{1,0:T(8,128)(2,1)S(1)}, bf16[80,4096]{1,0:T(8,128)(2,1)}, u32[]{:S(2)}, u32[]{:S(2)}) %collective-permute-start.13) | collective-permute-done | bytes 655392 | tf_op jit(solution)/shard_map/ppermute | solution.py:53
  212.4 1.4 pad_maximum_fusion
  213.8 0.8 fusion.15
  214.5 3.9 %fusion.1 = f32[1,128,4096]{2,1,0:T(8,128)} fusion(f32[128,4096]{1,0:T(8,128)S(1)} %fusion.15, bf16[320,4096]{1,0:T(8,128)(2,1)} %constant_dynamic-update-slice_fusion.4, s32[]{:T(128)S(6)} %select_n.114), kind=kOutput, calls=%fused_computation.2 | convolution fusion | flops 336592896 | bytes 6897668 | tf_op jit(solution)/shard_map/dot_general | solution.py:21
  218.6 0.7 multiply_bitcast_fusion
  (52 shorter events, 1.3 us)
Async XLA Ops:
  0.6 41.8 %copy-start.1 = (bf16[1,48,4096]{2,1,0:T(8,128)(2,1)S(1)}, bf16[1,48,4096]{2,1,0:T(8,128)(2,1)}, u32[]{:S(2)}) copy-start(bf16[1,48,4096]{2,1,0:T(8,128)(2,1)} %param.13) | copy-start | bytes 1179652
  0.6 41.8 %copy-start.2 = (bf16[1,48,4096]{2,1,0:T(8,128)(2,1)S(1)}, bf16[1,48,4096]{2,1,0:T(8,128)(2,1)}, u32[]{:S(2)}) copy-start(bf16[1,48,4096]{2,1,0:T(8,128)(2,1)} %param.12) | copy-start | bytes 1179652
  0.7 41.8 %copy-start.3 = (bf16[1,48,4096]{2,1,0:T(8,128)(2,1)S(1)}, bf16[1,48,4096]{2,1,0:T(8,128)(2,1)}, u32[]{:S(2)}) copy-start(bf16[1,48,4096]{2,1,0:T(8,128)(2,1)} %param.11) | copy-start | bytes 1179652
  5.5 35.8 %all-to-all-start = ((bf16[16,40,256]{2,1,0:T(8,128)(2,1)}), bf16[16,40,256]{2,1,0:T(8,128)(2,1)S(1)}, u32[]{:S(2)}, u32[]{:S(2)}) async-start(bf16[16,40,256]{2,1,0:T(8,128)(2,1)} %bitcast.1), calls=%async_computation | async-start | bytes 655360 | tf_op jit(solution)/shard_map/all_to_all | solution.py:49
  42.7 57.8 %collective-permute-start.12 = (bf16[144,4096]{1,0:T(8,128)(2,1)S(1)}, bf16[144,4096]{1,0:T(8,128)(2,1)}, u32[]{:S(2)}, u32[]{:S(2)}) collective-permute-start(bf16[144,4096]{1,0:T(8,128)(2,1)S(1)} %maximum_add_fusion), channel_id=1, source_target_pairs={{0,384},{128,256},{256,128},{384,0},{1,385},{129,257},{257,129},{3... | collective-permute-start | bytes 3538952 | tf_op jit(solution)/shard_map/ppermute | solution.py:53
  46.1 59.8 %collective-permute-start.11 = (bf16[144,4096]{1,0:T(8,128)(2,1)S(1)}, bf16[144,4096]{1,0:T(8,128)(2,1)}, u32[]{:S(2)}, u32[]{:S(2)}) collective-permute-start(bf16[144,4096]{1,0:T(8,128)(2,1)S(1)} %maximum_add_fusion), channel_id=1, source_target_pairs={{0,256},{128,384},{256,0},{384,128},{1,257},{129,385},{257,1},{385... | collective-permute-start | bytes 3538952 | tf_op jit(solution)/shard_map/ppermute | solution.py:53
  49.1 71.9 %collective-permute-start.10 = (bf16[144,4096]{1,0:T(8,128)(2,1)S(1)}, bf16[144,4096]{1,0:T(8,128)(2,1)}, u32[]{:S(2)}, u32[]{:S(2)}) collective-permute-start(bf16[144,4096]{1,0:T(8,128)(2,1)S(1)} %maximum_add_fusion), channel_id=1, source_target_pairs={{0,128},{128,0},{256,384},{384,256},{1,129},{129,1},{257,385},{385... | collective-permute-start | bytes 3538952 | tf_op jit(solution)/shard_map/ppermute | solution.py:53
  52.6 19.3 %collective-permute-start = (bf16[40,4096]{1,0:T(8,128)(2,1)S(1)}, bf16[40,4096]{1,0:T(8,128)(2,1)S(1)}, u32[]{:S(2)}, u32[]{:S(2)}) collective-permute-start(bf16[40,4096]{1,0:T(8,128)(2,1)S(1)} %bitcast.77), channel_id=1, source_target_pairs={{0,32},{32,64},{64,96},{96,112},{112,80},{80,48},{48,16},{16,0},{1... | collective-permute-start | bytes 983048 | tf_op jit(solution)/shard_map/ppermute | solution.py:63
  71.9 10.2 %collective-permute-start.1 = (bf16[40,4096]{1,0:T(8,128)(2,1)S(1)}, bf16[40,4096]{1,0:T(8,128)(2,1)S(1)}, u32[]{:S(2)}, u32[]{:S(2)}) collective-permute-start(bf16[40,4096]{1,0:T(8,128)(2,1)S(1)} %collective-permute-done), channel_id=1, source_target_pairs={{0,32},{32,64},{64,96},{96,112},{112,80},{80,48},{48,16},{16,0},{1... | collective-permute-start | bytes 983048 | tf_op jit(solution)/shard_map/ppermute | solution.py:63
  82.0 9.6 %collective-permute-start.2 = (bf16[40,4096]{1,0:T(8,128)(2,1)S(1)}, bf16[40,4096]{1,0:T(8,128)(2,1)S(1)}, u32[]{:S(2)}, u32[]{:S(2)}) collective-permute-start(bf16[40,4096]{1,0:T(8,128)(2,1)S(1)} %collective-permute-done.1), channel_id=1, source_target_pairs={{0,32},{32,64},{64,96},{96,112},{112,80},{80,48},{48,16},{16,0},{1... | collective-permute-start | bytes 983048 | tf_op jit(solution)/shard_map/ppermute | solution.py:63
  91.6 0.7 copy-start.4
  93.4 7.1 %copy-start = (bf16[80,4096]{1,0:T(8,128)(2,1)S(1)}, bf16[80,4096]{1,0:T(8,128)(2,1)}, u32[]{:S(2)}) copy-start(bf16[80,4096]{1,0:T(8,128)(2,1)} %reshape.148) | copy-start | bytes 1966084
  93.4 89.1 %collective-permute-start.5 = (bf16[80,4096]{1,0:T(8,128)(2,1)}, bf16[80,4096]{1,0:T(8,128)(2,1)}, u32[]{:S(2)}, u32[]{:S(2)}) collective-permute-start(bf16[80,4096]{1,0:T(8,128)(2,1)} %reshape.148), channel_id=1, source_target_pairs={{0,384},{128,256},{256,128},{384,0},{1,385},{129,257},{257,129},{3... | collective-permute-start | bytes 1966088 | tf_op jit(solution)/shard_map/ppermute | solution.py:53
  96.9 83.6 %collective-permute-start.4 = (bf16[80,4096]{1,0:T(8,128)(2,1)}, bf16[80,4096]{1,0:T(8,128)(2,1)}, u32[]{:S(2)}, u32[]{:S(2)}) collective-permute-start(bf16[80,4096]{1,0:T(8,128)(2,1)} %reshape.148), channel_id=1, source_target_pairs={{0,256},{128,384},{256,0},{384,128},{1,257},{129,385},{257,1},{385... | collective-permute-start | bytes 1966088 | tf_op jit(solution)/shard_map/ppermute | solution.py:53
  100.5 5.4 %copy-start.5 = (bf16[40,4096]{1,0:T(8,128)(2,1)S(1)}, bf16[40,4096]{1,0:T(8,128)(2,1)}, u32[]{:S(2)}) copy-start(bf16[40,4096]{1,0:T(8,128)(2,1)} %copy-done.4) | copy-start | bytes 983044
  100.5 78.0 %collective-permute-start.3 = (bf16[80,4096]{1,0:T(8,128)(2,1)S(1)}, bf16[80,4096]{1,0:T(8,128)(2,1)}, u32[]{:S(2)}, u32[]{:S(2)}) collective-permute-start(bf16[80,4096]{1,0:T(8,128)(2,1)S(1)} %copy-done), channel_id=1, source_target_pairs={{0,128},{128,0},{256,384},{384,256},{1,129},{129,1},{257,385},{385... | collective-permute-start | bytes 1966088 | tf_op jit(solution)/shard_map/ppermute | solution.py:53
  105.9 21.1 %collective-permute-start.6 = (bf16[40,4096]{1,0:T(8,128)(2,1)S(1)}, bf16[40,4096]{1,0:T(8,128)(2,1)S(1)}, u32[]{:S(2)}, u32[]{:S(2)}) collective-permute-start(bf16[40,4096]{1,0:T(8,128)(2,1)S(1)} %copy-done.5), channel_id=1, source_target_pairs={{0,32},{32,64},{64,96},{96,112},{112,80},{80,48},{48,16},{16,0},{1... | collective-permute-start | bytes 983048 | tf_op jit(solution)/shard_map/ppermute | solution.py:63
  126.9 12.6 %collective-permute-start.7 = (bf16[40,4096]{1,0:T(8,128)(2,1)S(1)}, bf16[40,4096]{1,0:T(8,128)(2,1)S(1)}, u32[]{:S(2)}, u32[]{:S(2)}) collective-permute-start(bf16[40,4096]{1,0:T(8,128)(2,1)S(1)} %collective-permute-done.6), channel_id=1, source_target_pairs={{0,32},{32,64},{64,96},{96,112},{112,80},{80,48},{48,16},{16,0},{1... | collective-permute-start | bytes 983048 | tf_op jit(solution)/shard_map/ppermute | solution.py:63
  139.5 11.7 %collective-permute-start.8 = (bf16[40,4096]{1,0:T(8,128)(2,1)S(1)}, bf16[40,4096]{1,0:T(8,128)(2,1)S(1)}, u32[]{:S(2)}, u32[]{:S(2)}) collective-permute-start(bf16[40,4096]{1,0:T(8,128)(2,1)S(1)} %collective-permute-done.7), channel_id=1, source_target_pairs={{0,32},{32,64},{64,96},{96,112},{112,80},{80,48},{48,16},{16,0},{1... | collective-permute-start | bytes 983048 | tf_op jit(solution)/shard_map/ppermute | solution.py:63
  151.3 9.9 %collective-permute-start.9 = (bf16[40,4096]{1,0:T(8,128)(2,1)S(1)}, bf16[40,4096]{1,0:T(8,128)(2,1)S(1)}, u32[]{:S(2)}, u32[]{:S(2)}) collective-permute-start(bf16[40,4096]{1,0:T(8,128)(2,1)S(1)} %collective-permute-done.8), channel_id=1, source_target_pairs={{0,32},{32,64},{64,96},{96,112},{112,80},{80,48},{48,16},{16,0},{1... | collective-permute-start | bytes 983048 | tf_op jit(solution)/shard_map/ppermute | solution.py:63
  168.6 25.9 %all-to-all-start.1 = ((bf16[8,80,384]{2,1,0:T(8,128)(2,1)}), bf16[8,80,384]{2,1,0:T(8,128)(2,1)}, u32[]{:S(2)}, u32[]{:S(2)}) async-start(bf16[8,80,384]{2,1,0:T(8,128)(2,1)} %broadcast_in_dim.13), calls=%async_computation.1 | async-start | bytes 983040 | tf_op jit(solution)/shard_map/all_to_all | solution.py:98
  184.7 23.8 %collective-permute-start.15 = (bf16[80,4096]{1,0:T(8,128)(2,1)S(1)}, bf16[80,4096]{1,0:T(8,128)(2,1)S(1)}, u32[]{:S(2)}, u32[]{:S(2)}) collective-permute-start(bf16[80,4096]{1,0:T(8,128)(2,1)S(1)} %reshape.150), channel_id=1, source_target_pairs={{0,384},{128,256},{256,128},{384,0},{1,385},{129,257},{257,129},{3... | collective-permute-start | bytes 1966088 | tf_op jit(solution)/shard_map/ppermute | solution.py:53
  186.6 21.9 %collective-permute-start.14 = (bf16[80,4096]{1,0:T(8,128)(2,1)S(1)}, bf16[80,4096]{1,0:T(8,128)(2,1)}, u32[]{:S(2)}, u32[]{:S(2)}) collective-permute-start(bf16[80,4096]{1,0:T(8,128)(2,1)S(1)} %reshape.150), channel_id=1, source_target_pairs={{0,256},{128,384},{256,0},{384,128},{1,257},{129,385},{257,1},{385... | collective-permute-start | bytes 1966088 | tf_op jit(solution)/shard_map/ppermute | solution.py:53
  190.7 21.7 %collective-permute-start.13 = (bf16[80,4096]{1,0:T(8,128)(2,1)S(1)}, bf16[80,4096]{1,0:T(8,128)(2,1)}, u32[]{:S(2)}, u32[]{:S(2)}) collective-permute-start(bf16[80,4096]{1,0:T(8,128)(2,1)S(1)} %reshape.150), channel_id=1, source_target_pairs={{0,128},{128,0},{256,384},{384,256},{1,129},{129,1},{257,385},{385... | collective-permute-start | bytes 1966088 | tf_op jit(solution)/shard_map/ppermute | solution.py:53
  199.7 18.8 %all-to-all-start.2 = ((bf16[4,48,1536]{2,1,0:T(8,128)(2,1)}), bf16[4,48,1536]{2,1,0:T(8,128)(2,1)S(1)}, u32[]{:S(2)}, u32[]{:S(2)}) async-start(bf16[4,48,1536]{2,1,0:T(8,128)(2,1)} %bitcast.21), calls=%async_computation.2 | async-start | bytes 1179648 | tf_op jit(solution)/shard_map/all_to_all | solution.py:102
where the time goes:
time: 221 us; the launch traced here: 219 us
  starting transfers between devices  104 us (47%)
  waiting for transfers between devices  72.8 us (33%)
  matrix products  20.2 us (9%)
  local copies, waits for them, and re-layouts  14.6 us (7%)
  other arithmetic  5.54 us (3%)
  between operations  2.54 us (1%)
    ppermute x7, waiting for transfers between devices, body(): parts.append(lax.ppermute(parts[-1], 'zl', pairs))  46.5 us
    ppermute x7, starting transfers between devices, body(): parts.append(lax.ppermute(parts[-1], 'zl', pairs))  43.5 us
    ppermute x9, starting transfers between devices, swap_x(): return lax.ppermute(v, 'x', [(i, i ^ k) for i in range(nx)])  29.7 us
    all_to_all x1, waiting for transfers between devices, body(): lax.all_to_all(packed, ('y', 'zh', 'c'), split_axis=0, concat_axis=0, til...  17.9 us
    all_to_all x1, starting transfers between devices, body(): lax.all_to_all(packed, ('y', 'zh', 'c'), split_axis=0, concat_axis=0, til...  17.8 us
    dot_general x9, matrix products, dot_nt(): lax.dot_general(a, b, (((1,), (1,)), ((), ())), preferred_element_type=F32)  12 us
    all_to_all x1, starting transfers between devices, body(): lax.all_to_all(spread, 'zl', split_axis=0, concat_axis=0, tiled=True)  8.97 us
    ppermute x9, waiting for transfers between devices, swap_x(): return lax.ppermute(v, 'x', [(i, i ^ k) for i in range(nx)])  8.43 us
  transfers between devices with their start and end apart: 19, of which 10 were waited for; matrix products, arithmetic and copies ran while one was open for 15% of the time, Pallas kernels for 0%

commit v1 on v0

--- a/solution.py
+++ b/solution.py
@@ -52,9 +52,8 @@
     def swap_x(v, k):
         return lax.ppermute(v, "x", [(i, i ^ k) for i in range(nx)])
 
-    zero = (recv[0, :1, :1] * 0).reshape(1, 1)
-    w_own = jnp.concatenate([gate_w[0], up_w[0], down_w[0]], axis=0) + zero
-    weights = [w_own] + [swap_x(w_own, k) for k in range(1, nx)]
+    w_own = jnp.concatenate([gate_w[0], up_w[0], down_w[0]], axis=0)
+    w_others = [swap_x(w_own, k) for k in range(1, nx)]
 
     order = list(range(0, nz, 2)) + list(range(nz - 1, 0, -2))
     pairs = [(order[i], order[(i + 1) % nz]) for i in range(nz)]
@@ -63,6 +62,11 @@
         parts.append(lax.ppermute(parts[-1], "zl", pairs))
 
     half = nz // 2
+
+    late = [(parts[half + i][:1, :1] * 0).reshape(1, 1) for i in range(2)]
+    stacked = [w_own, w_others[0] + late[0], w_others[1] + late[1]] + w_others[2:]
+    weights = jnp.concatenate(stacked, axis=0)
+
     group = nx * hid
     slots = nz * capacity
     place = jnp.where(zi % 2 == 0, zi // 2, nz - 1 - zi // 2)
@@ -79,10 +83,7 @@
         x_half.append(
             rows.reshape(half, 2 * capacity, full_width)[:, :capacity].reshape(half * capacity, full_width)
         )
-        pre = []
-        for w in weights:
-            pre.append(dot_nt(w, rows))
-        pre = jnp.stack(pre)
+        pre = dot_nt(weights, rows).reshape(nx, 3 * hid, -1)
         gate_pre, up_pre = pre[:, :hid], pre[:, hid : 2 * hid]
         hidden_grad = jnp.roll(pre[:, 2 * hid :], -capacity, axis=2)
         gate_grad = (hidden_grad * up_pre * silu_slope(gate_pre)).astype(BF16).reshape(group, -1)
@@ -96,6 +97,7 @@
     wide = jnp.concatenate([g_sorted[: slots // 2], g_sorted[slots // 2 :]], axis=1)
     spread = jnp.broadcast_to(wide[None], (nz,) + wide.shape)
     spread = lax.all_to_all(spread, "zl", split_axis=0, concat_axis=0, tiled=True)
+    later = (spread[0, :1, :1] * 0).reshape(1, 1)
     spread = spread.reshape(nz, slots // 2, 2, nx, hid).transpose(2, 1, 3, 0, 4)
     spread = spread.reshape(slots, nx * nz * hid)
     part_sent = dot_tn(g_sorted, spread).astype(BF16).reshape(nx, hid, nx * nz * hid)
@@ -103,10 +105,9 @@
     grad_rows = jnp.sum(part.astype(F32), axis=0) / float(slot_count)
 
     strip_width = full_width // (nx * nz)
-    late = (part_sent[0, :1, :1] * 0).reshape(1, 1)
     input_rows = 0.0
     for name, piece in zip(("xa", "xb"), x_half):
-        own_piece = piece if name == "xa" else piece + late
+        own_piece = piece if name == "xa" else piece + later
         gathered = [own_piece] + [swap_x(piece, k) for k in range(1, nx)]
         rows = jnp.concatenate(gathered, axis=0)
         strip = lax.dynamic_slice_in_dim(rows, (xi * nz + zi) * strip_width, strip_width, 1)

time: 221 us -> 224 us (1.014)
  the two profiles are of different devices: /device:TPU:2 before, /device:TPU:8 now
where the time goes in v1:
time: 224 us; the launch traced here: 223 us
  starting transfers between devices  92.4 us (41%)
  waiting for transfers between devices  83.3 us (37%)
  local copies, waits for them, and re-layouts  18.2 us (8%)
  matrix products  13.7 us (6%)
  other arithmetic  12.3 us (5%)
  between operations  3.17 us (1%)
    ppermute x7, waiting for transfers between devices, body(): parts.append(lax.ppermute(parts[-1], 'zl', pairs))  48.7 us
    ppermute x7, starting transfers between devices, body(): parts.append(lax.ppermute(parts[-1], 'zl', pairs))  31.9 us
    ppermute x9, starting transfers between devices, swap_x(): return lax.ppermute(v, 'x', [(i, i ^ k) for i in range(nx)])  29.9 us
    ppermute x9, waiting for transfers between devices, swap_x(): return lax.ppermute(v, 'x', [(i, i ^ k) for i in range(nx)])  21.7 us
    all_to_all x1, starting transfers between devices, body(): lax.all_to_all(packed, ('y', 'zh', 'c'), split_axis=0, concat_axis=0, til...  18.2 us
    all_to_all x1, waiting for transfers between devices, body(): lax.all_to_all(packed, ('y', 'zh', 'c'), split_axis=0, concat_axis=0, til...  12.9 us
    all_to_all x1, starting transfers between devices, body(): lax.all_to_all(spread, 'zl', split_axis=0, concat_axis=0, tiled=True)  8.96 us
    reshape x2, matrix products, body(): pre = dot_nt(weights, rows).reshape(nx, 3 * hid, -1)  7.94 us
  transfers between devices with their start and end apart: 19, of which 11 were waited for; matrix products, arithmetic and copies ran while one was open for 18% of the time, Pallas kernels for 0%

profile of v1, /device:TPU:8, one launch (start us, length us, event | category | flops | bytes accessed | tf_op | source)
XLA Modules:
  0.0 223.1 jit_solution(16767610040831828919)
XLA Ops:
  0.7 2.4 %pad_maximum_fusion.1 = bf16[144,4096]{1,0:T(8,128)(2,1)} fusion(bf16[48,4096]{1,0:T(8,128)(2,1)} %bitcast.55, bf16[48,4096]{1,0:T(8,128)(2,1)} %bitcast.54, bf16[48,4096]{1,0:T(8,128)(2,1)} %bitcast.53), kind=kLoop, calls=%fused_computation.6 | loop fusion | flops 3538944 | bytes 2359296 | tf_op jit(solution)/shard_map/concatenate | solution.py:55
  3.1 3.4 %collective-permute-start.10 = (bf16[144,4096]{1,0:T(8,128)(2,1)}, bf16[144,4096]{1,0:T(8,128)(2,1)}, u32[]{:S(2)}, u32[]{:S(2)}) collective-permute-start(bf16[144,4096]{1,0:T(8,128)(2,1)} %pad_maximum_fusion.1), channel_id=1, source_target_pairs={{0,128},{128,0},{256,384},{384,256},{1,129},{129,1},{257,385},{385... | collective-permute-start | bytes 3538952 | tf_op jit(solution)/shard_map/ppermute | solution.py:53
  6.5 4.6 %collective-permute-start.11 = (bf16[144,4096]{1,0:T(8,128)(2,1)}, bf16[144,4096]{1,0:T(8,128)(2,1)}, u32[]{:S(2)}, u32[]{:S(2)}) collective-permute-start(bf16[144,4096]{1,0:T(8,128)(2,1)} %pad_maximum_fusion.1), channel_id=1, source_target_pairs={{0,256},{128,384},{256,0},{384,128},{1,257},{129,385},{257,1},{385... | collective-permute-start | bytes 3538952 | tf_op jit(solution)/shard_map/ppermute | solution.py:53
  11.2 2.4 %collective-permute-start.12 = (bf16[144,4096]{1,0:T(8,128)(2,1)}, bf16[144,4096]{1,0:T(8,128)(2,1)}, u32[]{:S(2)}, u32[]{:S(2)}) collective-permute-start(bf16[144,4096]{1,0:T(8,128)(2,1)} %pad_maximum_fusion.1), channel_id=1, source_target_pairs={{0,384},{128,256},{256,128},{384,0},{1,385},{129,257},{257,129},{3... | collective-permute-start | bytes 3538952 | tf_op jit(solution)/shard_map/ppermute | solution.py:53
  13.7 0.6 reduce-window.6
  14.2 0.2 slice_reduce_fusion
  14.8 1.1 convolution_convert_fusion.1
  15.9 18.2 %all-to-all-start = ((bf16[16,40,256]{2,1,0:T(8,128)(2,1)}), bf16[16,40,256]{2,1,0:T(8,128)(2,1)S(1)}, u32[]{:S(2)}, u32[]{:S(2)}) async-start(bf16[16,40,256]{2,1,0:T(8,128)(2,1)} %bitcast.1), calls=%async_computation | async-start | bytes 655360 | tf_op jit(solution)/shard_map/all_to_all | solution.py:49
  34.1 0.8 constant_dynamic-update-slice_fusion.15
  34.9 0.8 constant_dynamic-update-slice_fusion.14
  35.7 0.8 constant_dynamic-update-slice_fusion.13
  36.5 12.9 %all-to-all-done = bf16[16,40,256]{2,1,0:T(8,128)(2,1)S(1)} async-done(((bf16[16,40,256]{2,1,0:T(8,128)(2,1)}), bf16[16,40,256]{2,1,0:T(8,128)(2,1)S(1)}, u32[]{:S(2)}, u32[]{:S(2)}) %all-to-all-start) | async-done | bytes 327712 | tf_op jit(solution)/shard_map/all_to_all | solution.py:49
  49.4 9.9 %collective-permute-start = (bf16[40,4096]{1,0:T(8,128)(2,1)S(1)}, bf16[40,4096]{1,0:T(8,128)(2,1)S(1)}, u32[]{:S(2)}, u32[]{:S(2)}) collective-permute-start(bf16[40,4096]{1,0:T(8,128)(2,1)S(1)} %bitcast.57), channel_id=1, source_target_pairs={{0,32},{32,64},{64,96},{96,112},{112,80},{80,48},{48,16},{16,0},{1... | collective-permute-start | bytes 983048 | tf_op jit(solution)/shard_map/ppermute | solution.py:62
  59.4 11.5 %collective-permute-done = bf16[40,4096]{1,0:T(8,128)(2,1)S(1)} collective-permute-done((bf16[40,4096]{1,0:T(8,128)(2,1)S(1)}, bf16[40,4096]{1,0:T(8,128)(2,1)S(1)}, u32[]{:S(2)}, u32[]{:S(2)}) %collective-permute-start) | collective-permute-done | bytes 327712 | tf_op jit(solution)/shard_map/ppermute | solution.py:62
  70.9 1.9 collective-permute-start.1
  72.8 10.2 %collective-permute-done.1 = bf16[40,4096]{1,0:T(8,128)(2,1)S(1)} collective-permute-done((bf16[40,4096]{1,0:T(8,128)(2,1)S(1)}, bf16[40,4096]{1,0:T(8,128)(2,1)S(1)}, u32[]{:S(2)}, u32[]{:S(2)}) %collective-permute-start.1) | collective-permute-done | bytes 327712 | tf_op jit(solution)/shard_map/ppermute | solution.py:62
  83.0 2.5 %collective-permute-start.2 = (bf16[40,4096]{1,0:T(8,128)(2,1)S(1)}, bf16[40,4096]{1,0:T(8,128)(2,1)}, u32[]{:S(2)}, u32[]{:S(2)}) collective-permute-start(bf16[40,4096]{1,0:T(8,128)(2,1)S(1)} %collective-permute-done.1), channel_id=1, source_target_pairs={{0,32},{32,64},{64,96},{96,112},{112,80},{80,48},{48,16},{16,0},{1... | collective-permute-start | bytes 983048 | tf_op jit(solution)/shard_map/ppermute | solution.py:62
  85.5 8.9 %collective-permute-done.2 = bf16[40,4096]{1,0:T(8,128)(2,1)} collective-permute-done((bf16[40,4096]{1,0:T(8,128)(2,1)S(1)}, bf16[40,4096]{1,0:T(8,128)(2,1)}, u32[]{:S(2)}, u32[]{:S(2)}) %collective-permute-start.2) | collective-permute-done | bytes 327712 | tf_op jit(solution)/shard_map/ppermute | solution.py:62
  94.4 3.0 %collective-permute-start.6 = (bf16[40,4096]{1,0:T(8,128)(2,1)}, bf16[40,4096]{1,0:T(8,128)(2,1)S(1)}, u32[]{:S(2)}, u32[]{:S(2)}) collective-permute-start(bf16[40,4096]{1,0:T(8,128)(2,1)} %collective-permute-done.2), channel_id=1, source_target_pairs={{0,32},{32,64},{64,96},{96,112},{112,80},{80,48},{48,16},{16,0},{1... | collective-permute-start | bytes 983048 | tf_op jit(solution)/shard_map/ppermute | solution.py:62
  97.4 1.0 constant_dynamic-update-slice_fusion
  98.5 0.1 reshape.151
  98.6 2.2 collective-permute-start.3
  100.8 4.2 %collective-permute-done.6 = bf16[40,4096]{1,0:T(8,128)(2,1)S(1)} collective-permute-done((bf16[40,4096]{1,0:T(8,128)(2,1)}, bf16[40,4096]{1,0:T(8,128)(2,1)S(1)}, u32[]{:S(2)}, u32[]{:S(2)}) %collective-permute-start.6) | collective-permute-done | bytes 327712 | tf_op jit(solution)/shard_map/ppermute | solution.py:62
  105.0 3.7 %collective-permute-start.4 = (bf16[80,4096]{1,0:T(8,128)(2,1)S(1)}, bf16[80,4096]{1,0:T(8,128)(2,1)}, u32[]{:S(2)}, u32[]{:S(2)}) collective-permute-start(bf16[80,4096]{1,0:T(8,128)(2,1)S(1)} %reshape.151), channel_id=1, source_target_pairs={{0,256},{128,384},{256,0},{384,128},{1,257},{129,385},{257,1},{385... | collective-permute-start | bytes 1966088 | tf_op jit(solution)/shard_map/ppermute | solution.py:53
  108.7 0.5 slice.84
  109.9 4.0 %collective-permute-start.7 = (bf16[40,4096]{1,0:T(8,128)(2,1)S(1)}, bf16[40,4096]{1,0:T(8,128)(2,1)S(1)}, u32[]{:S(2)}, u32[]{:S(2)}) collective-permute-start(bf16[40,4096]{1,0:T(8,128)(2,1)S(1)} %collective-permute-done.6), channel_id=1, source_target_pairs={{0,32},{32,64},{64,96},{96,112},{112,80},{80,48},{48,16},{16,0},{1... | collective-permute-start | bytes 983048 | tf_op jit(solution)/shard_map/ppermute | solution.py:62
  114.0 2.5 %add_dynamic-update-slice_fusion.1 = bf16[576,4096]{1,0:T(8,128)(2,1)} fusion(bf16[576,4096]{1,0:T(8,128)(2,1)} %constant_dynamic-update-slice_fusion.13, bf16[144,4096]{1,0:T(8,128)(2,1)} %collective-permute-done.10, bf16[]{:T(256)} %bitcast.8), kind=kLoop, calls=%fused_computation.9 | loop fusion | flops 2359296 | bytes 2359808
  116.5 3.0 %collective-permute-done.7 = bf16[40,4096]{1,0:T(8,128)(2,1)S(1)} collective-permute-done((bf16[40,4096]{1,0:T(8,128)(2,1)S(1)}, bf16[40,4096]{1,0:T(8,128)(2,1)S(1)}, u32[]{:S(2)}, u32[]{:S(2)}) %collective-permute-start.7) | collective-permute-done | bytes 327712 | tf_op jit(solution)/shard_map/ppermute | solution.py:62
  119.5 0.5 slice.85
  120.7 2.5 %add_dynamic-update-slice_fusion = bf16[576,4096]{1,0:T(8,128)(2,1)} fusion(bf16[576,4096]{1,0:T(8,128)(2,1)} %add_dynamic-update-slice_fusion.1, bf16[144,4096]{1,0:T(8,128)(2,1)} %collective-permute-done.11, bf16[]{:T(256)} %bitcast.9), kind=kLoop, calls=%fused_computation.8 | loop fusion | flops 2359296 | bytes 2359808
  123.2 2.4 %constant_dynamic-update-slice_fusion.12 = bf16[576,4096]{1,0:T(8,128)(2,1)} fusion(bf16[576,4096]{1,0:T(8,128)(2,1)} %add_dynamic-update-slice_fusion, bf16[144,4096]{1,0:T(8,128)(2,1)} %collective-permute-done.12), kind=kLoop, calls=%fused_computation.50 | loop fusion | bytes 2359296 | tf_op jit(solution)/shard_map/concatenate | solution.py:68
  125.6 3.7 %fusion.40 = f32[576,160]{1,0:T(8,128)S(1)} fusion(bf16[576,4096]{1,0:T(8,128)(2,1)} %constant_dynamic-update-slice_fusion.12, bf16[160,4096]{1,0:T(8,128)(2,1)S(1)} %constant_dynamic-update-slice_fusion), kind=kOutput, calls=%fused_computation.106 | convolution fusion | flops 754974720 | bytes 6397952 | tf_op jit(solution)/shard_map/reshape | solution.py:86
  129.5 5.1 %collective-permute-start.8 = (bf16[40,4096]{1,0:T(8,128)(2,1)S(1)}, bf16[40,4096]{1,0:T(8,128)(2,1)S(1)}, u32[]{:S(2)}, u32[]{:S(2)}) collective-permute-start(bf16[40,4096]{1,0:T(8,128)(2,1)S(1)} %collective-permute-done.7), channel_id=1, source_target_pairs={{0,32},{32,64},{64,96},{96,112},{112,80},{80,48},{48,16},{16,0},{1... | collective-permute-start | bytes 983048 | tf_op jit(solution)/shard_map/ppermute | solution.py:62
  134.6 0.1 fusion.7
  134.7 0.2 fusion.11
  134.9 5.3 %collective-permute-done.8 = bf16[40,4096]{1,0:T(8,128)(2,1)S(1)} collective-permute-done((bf16[40,4096]{1,0:T(8,128)(2,1)S(1)}, bf16[40,4096]{1,0:T(8,128)(2,1)S(1)}, u32[]{:S(2)}, u32[]{:S(2)}) %collective-permute-start.8) | collective-permute-done | bytes 327712 | tf_op jit(solution)/shard_map/ppermute | solution.py:62
  140.3 5.4 %collective-permute-start.9 = (bf16[40,4096]{1,0:T(8,128)(2,1)S(1)}, bf16[40,4096]{1,0:T(8,128)(2,1)S(1)}, u32[]{:S(2)}, u32[]{:S(2)}) collective-permute-start(bf16[40,4096]{1,0:T(8,128)(2,1)S(1)} %collective-permute-done.8), channel_id=1, source_target_pairs={{0,32},{32,64},{64,96},{96,112},{112,80},{80,48},{48,16},{16,0},{1... | collective-permute-start | bytes 983048 | tf_op jit(solution)/shard_map/ppermute | solution.py:62
  145.7 5.6 %collective-permute-done.9 = bf16[40,4096]{1,0:T(8,128)(2,1)S(1)} collective-permute-done((bf16[40,4096]{1,0:T(8,128)(2,1)S(1)}, bf16[40,4096]{1,0:T(8,128)(2,1)S(1)}, u32[]{:S(2)}, u32[]{:S(2)}) %collective-permute-start.9) | collective-permute-done | bytes 327712 | tf_op jit(solution)/shard_map/ppermute | solution.py:62
  151.4 4.2 %fusion.41 = f32[576,160]{1,0:T(8,128)S(1)} fusion(bf16[576,4096]{1,0:T(8,128)(2,1)} %constant_dynamic-update-slice_fusion.12, bf16[160,4096]{1,0:T(8,128)(2,1)S(1)} %constant_dynamic-update-slice_fusion.8), kind=kOutput, calls=%fused_computation.107 | convolution fusion | flops 754974720 | bytes 6397952 | tf_op jit(solution)/shard_map/reshape | solution.py:86
  155.7 0.1 fusion.5
  155.8 0.3 convolution_convert_fusion.2
  156.3 0.8 broadcast_in_dim.13
  157.1 9.0 %all-to-all-start.1 = ((bf16[8,80,384]{2,1,0:T(8,128)(2,1)}), bf16[8,80,384]{2,1,0:T(8,128)(2,1)}, u32[]{:S(2)}, u32[]{:S(2)}) async-start(bf16[8,80,384]{2,1,0:T(8,128)(2,1)} %broadcast_in_dim.13), calls=%async_computation.1 | async-start | bytes 983040 | tf_op jit(solution)/shard_map/all_to_all | solution.py:99
  166.1 3.2 %collective-permute-start.5 = (bf16[80,4096]{1,0:T(8,128)(2,1)S(1)}, bf16[80,4096]{1,0:T(8,128)(2,1)S(1)}, u32[]{:S(2)}, u32[]{:S(2)}) collective-permute-start(bf16[80,4096]{1,0:T(8,128)(2,1)S(1)} %reshape.151), channel_id=1, source_target_pairs={{0,384},{128,256},{256,128},{384,0},{1,385},{129,257},{257,129},{3... | collective-permute-start | bytes 1966088 | tf_op jit(solution)/shard_map/ppermute | solution.py:53
  169.3 1.1 constant_dynamic-update-slice_fusion.6
  170.5 1.1 constant_dynamic-update-slice_fusion.5
  171.6 8.3 %collective-permute-done.5 = bf16[80,4096]{1,0:T(8,128)(2,1)S(1)} collective-permute-done((bf16[80,4096]{1,0:T(8,128)(2,1)S(1)}, bf16[80,4096]{1,0:T(8,128)(2,1)S(1)}, u32[]{:S(2)}, u32[]{:S(2)}) %collective-permute-start.5) | collective-permute-done | bytes 655392 | tf_op jit(solution)/shard_map/ppermute | solution.py:53
  180.1 1.0 reshape.153
  181.1 2.5 %collective-permute-start.13 = (bf16[80,4096]{1,0:T(8,128)(2,1)}, bf16[80,4096]{1,0:T(8,128)(2,1)}, u32[]{:S(2)}, u32[]{:S(2)}) collective-permute-start(bf16[80,4096]{1,0:T(8,128)(2,1)} %reshape.153), channel_id=1, source_target_pairs={{0,128},{128,0},{256,384},{384,256},{1,129},{129,1},{257,385},{385... | collective-permute-start | bytes 1966088 | tf_op jit(solution)/shard_map/ppermute | solution.py:53
  183.5 3.9 %collective-permute-start.14 = (bf16[80,4096]{1,0:T(8,128)(2,1)}, bf16[80,4096]{1,0:T(8,128)(2,1)}, u32[]{:S(2)}, u32[]{:S(2)}) collective-permute-start(bf16[80,4096]{1,0:T(8,128)(2,1)} %reshape.153), channel_id=1, source_target_pairs={{0,256},{128,384},{256,0},{384,128},{1,257},{129,385},{257,1},{385... | collective-permute-start | bytes 1966088 | tf_op jit(solution)/shard_map/ppermute | solution.py:53
  187.5 4.0 %collective-permute-start.15 = (bf16[80,4096]{1,0:T(8,128)(2,1)}, bf16[80,4096]{1,0:T(8,128)(2,1)}, u32[]{:S(2)}, u32[]{:S(2)}) collective-permute-start(bf16[80,4096]{1,0:T(8,128)(2,1)} %reshape.153), channel_id=1, source_target_pairs={{0,384},{128,256},{256,128},{384,0},{1,385},{129,257},{257,129},{3... | collective-permute-start | bytes 1966088 | tf_op jit(solution)/shard_map/ppermute | solution.py:53
  191.5 1.4 copy.34
  192.9 1.7 copy.35
  194.6 2.1 reshape.159
  196.7 1.2 convolution_convert_fusion
  198.0 3.5 %all-to-all-start.2 = ((bf16[4,48,1536]{2,1,0:T(8,128)(2,1)}), bf16[4,48,1536]{2,1,0:T(8,128)(2,1)S(1)}, u32[]{:S(2)}, u32[]{:S(2)}) async-start(bf16[4,48,1536]{2,1,0:T(8,128)(2,1)} %bitcast.52), calls=%async_computation.2 | async-start | bytes 1179648 | tf_op jit(solution)/shard_map/all_to_all | solution.py:104
  201.5 1.2 slice.96
  203.3 1.1 broadcast_add_fusion
  204.5 5.4 %collective-permute-done.14 = bf16[80,4096]{1,0:T(8,128)(2,1)} collective-permute-done((bf16[80,4096]{1,0:T(8,128)(2,1)}, bf16[80,4096]{1,0:T(8,128)(2,1)}, u32[]{:S(2)}, u32[]{:S(2)}) %collective-permute-start.14) | collective-permute-done | bytes 655392 | tf_op jit(solution)/shard_map/ppermute | solution.py:53
  209.9 7.9 %collective-permute-done.15 = bf16[80,4096]{1,0:T(8,128)(2,1)} collective-permute-done((bf16[80,4096]{1,0:T(8,128)(2,1)}, bf16[80,4096]{1,0:T(8,128)(2,1)}, u32[]{:S(2)}, u32[]{:S(2)}) %collective-permute-start.15) | collective-permute-done | bytes 655392 | tf_op jit(solution)/shard_map/ppermute | solution.py:53
  217.8 1.6 pad_maximum_fusion
  219.4 0.8 fusion.13
  220.2 2.1 fusion.1
  222.4 0.7 multiply_bitcast_fusion
  (58 shorter events, 1.2 us)
Async XLA Ops:
  0.6 33.5 %copy-start = (bf16[1,48,4096]{2,1,0:T(8,128)(2,1)S(1)}, bf16[1,48,4096]{2,1,0:T(8,128)(2,1)}, u32[]{:S(2)}) copy-start(bf16[1,48,4096]{2,1,0:T(8,128)(2,1)} %param.11) | copy-start | bytes 1179652
  0.6 12.9 %copy-start.6 = (s32[160,8]{0,1:T(8,128)S(1)}, s32[160,8]{0,1:T(8,128)}, u32[]{:S(2)}) copy-start(s32[160,8]{0,1:T(8,128)} %param.10) | copy-start | bytes 15364
  0.7 12.9 %copy-start.7 = (s32[160,8]{0,1:T(8,128)S(1)}, s32[160,8]{0,1:T(8,128)}, u32[]{:S(2)}) copy-start(s32[160,8]{0,1:T(8,128)} %param.9) | copy-start | bytes 15364
  0.7 14.0 %copy-start.5 = (bf16[160,256]{1,0:T(8,128)(2,1)S(1)}, bf16[160,256]{1,0:T(8,128)(2,1)}, u32[]{:S(2)}) copy-start(bf16[160,256]{1,0:T(8,128)(2,1)} %param.8) | copy-start | bytes 245764
  0.7 14.1 %copy-start.8 = (bf16[160,256]{1,0:T(8,128)(2,1)S(1)}, bf16[160,256]{1,0:T(8,128)(2,1)}, u32[]{:S(2)}) copy-start(bf16[160,256]{1,0:T(8,128)(2,1)} %param.7) | copy-start | bytes 245764
  0.7 34.2 %copy-start.1 = (bf16[1,48,4096]{2,1,0:T(8,128)(2,1)S(1)}, bf16[1,48,4096]{2,1,0:T(8,128)(2,1)}, u32[]{:S(2)}) copy-start(bf16[1,48,4096]{2,1,0:T(8,128)(2,1)} %param.12) | copy-start | bytes 1179652
  0.7 35.0 %copy-start.2 = (bf16[1,48,4096]{2,1,0:T(8,128)(2,1)S(1)}, bf16[1,48,4096]{2,1,0:T(8,128)(2,1)}, u32[]{:S(2)}) copy-start(bf16[1,48,4096]{2,1,0:T(8,128)(2,1)} %param.13) | copy-start | bytes 1179652
  3.1 106.7 %collective-permute-start.10 = (bf16[144,4096]{1,0:T(8,128)(2,1)}, bf16[144,4096]{1,0:T(8,128)(2,1)}, u32[]{:S(2)}, u32[]{:S(2)}) collective-permute-start(bf16[144,4096]{1,0:T(8,128)(2,1)} %pad_maximum_fusion.1), channel_id=1, source_target_pairs={{0,128},{128,0},{256,384},{384,256},{1,129},{129,1},{257,385},{385... | collective-permute-start | bytes 3538952 | tf_op jit(solution)/shard_map/ppermute | solution.py:53
  6.5 114.1 %collective-permute-start.11 = (bf16[144,4096]{1,0:T(8,128)(2,1)}, bf16[144,4096]{1,0:T(8,128)(2,1)}, u32[]{:S(2)}, u32[]{:S(2)}) collective-permute-start(bf16[144,4096]{1,0:T(8,128)(2,1)} %pad_maximum_fusion.1), channel_id=1, source_target_pairs={{0,256},{128,384},{256,0},{384,128},{1,257},{129,385},{257,1},{385... | collective-permute-start | bytes 3538952 | tf_op jit(solution)/shard_map/ppermute | solution.py:53
  11.2 112.0 %collective-permute-start.12 = (bf16[144,4096]{1,0:T(8,128)(2,1)}, bf16[144,4096]{1,0:T(8,128)(2,1)}, u32[]{:S(2)}, u32[]{:S(2)}) collective-permute-start(bf16[144,4096]{1,0:T(8,128)(2,1)} %pad_maximum_fusion.1), channel_id=1, source_target_pairs={{0,384},{128,256},{256,128},{384,0},{1,385},{129,257},{257,129},{3... | collective-permute-start | bytes 3538952 | tf_op jit(solution)/shard_map/ppermute | solution.py:53
  15.9 33.4 %all-to-all-start = ((bf16[16,40,256]{2,1,0:T(8,128)(2,1)}), bf16[16,40,256]{2,1,0:T(8,128)(2,1)S(1)}, u32[]{:S(2)}, u32[]{:S(2)}) async-start(bf16[16,40,256]{2,1,0:T(8,128)(2,1)} %bitcast.1), calls=%async_computation | async-start | bytes 655360 | tf_op jit(solution)/shard_map/all_to_all | solution.py:49
  49.4 21.5 %collective-permute-start = (bf16[40,4096]{1,0:T(8,128)(2,1)S(1)}, bf16[40,4096]{1,0:T(8,128)(2,1)S(1)}, u32[]{:S(2)}, u32[]{:S(2)}) collective-permute-start(bf16[40,4096]{1,0:T(8,128)(2,1)S(1)} %bitcast.57), channel_id=1, source_target_pairs={{0,32},{32,64},{64,96},{96,112},{112,80},{80,48},{48,16},{16,0},{1... | collective-permute-start | bytes 983048 | tf_op jit(solution)/shard_map/ppermute | solution.py:62
  70.9 12.1 %collective-permute-start.1 = (bf16[40,4096]{1,0:T(8,128)(2,1)S(1)}, bf16[40,4096]{1,0:T(8,128)(2,1)S(1)}, u32[]{:S(2)}, u32[]{:S(2)}) collective-permute-start(bf16[40,4096]{1,0:T(8,128)(2,1)S(1)} %collective-permute-done), channel_id=1, source_target_pairs={{0,32},{32,64},{64,96},{96,112},{112,80},{80,48},{48,16},{16,0},{1... | collective-permute-start | bytes 983048 | tf_op jit(solution)/shard_map/ppermute | solution.py:62
  83.0 11.4 %collective-permute-start.2 = (bf16[40,4096]{1,0:T(8,128)(2,1)S(1)}, bf16[40,4096]{1,0:T(8,128)(2,1)}, u32[]{:S(2)}, u32[]{:S(2)}) collective-permute-start(bf16[40,4096]{1,0:T(8,128)(2,1)S(1)} %collective-permute-done.1), channel_id=1, source_target_pairs={{0,32},{32,64},{64,96},{96,112},{112,80},{80,48},{48,16},{16,0},{1... | collective-permute-start | bytes 983048 | tf_op jit(solution)/shard_map/ppermute | solution.py:62
  94.4 10.6 %collective-permute-start.6 = (bf16[40,4096]{1,0:T(8,128)(2,1)}, bf16[40,4096]{1,0:T(8,128)(2,1)S(1)}, u32[]{:S(2)}, u32[]{:S(2)}) collective-permute-start(bf16[40,4096]{1,0:T(8,128)(2,1)} %collective-permute-done.2), channel_id=1, source_target_pairs={{0,32},{32,64},{64,96},{96,112},{112,80},{80,48},{48,16},{16,0},{1... | collective-permute-start | bytes 983048 | tf_op jit(solution)/shard_map/ppermute | solution.py:62
  98.6 70.7 %collective-permute-start.3 = (bf16[80,4096]{1,0:T(8,128)(2,1)S(1)}, bf16[80,4096]{1,0:T(8,128)(2,1)}, u32[]{:S(2)}, u32[]{:S(2)}) collective-permute-start(bf16[80,4096]{1,0:T(8,128)(2,1)S(1)} %reshape.151), channel_id=1, source_target_pairs={{0,128},{128,0},{256,384},{384,256},{1,129},{129,1},{257,385},{385... | collective-permute-start | bytes 1966088 | tf_op jit(solution)/shard_map/ppermute | solution.py:53
  105.0 65.5 %collective-permute-start.4 = (bf16[80,4096]{1,0:T(8,128)(2,1)S(1)}, bf16[80,4096]{1,0:T(8,128)(2,1)}, u32[]{:S(2)}, u32[]{:S(2)}) collective-permute-start(bf16[80,4096]{1,0:T(8,128)(2,1)S(1)} %reshape.151), channel_id=1, source_target_pairs={{0,256},{128,384},{256,0},{384,128},{1,257},{129,385},{257,1},{385... | collective-permute-start | bytes 1966088 | tf_op jit(solution)/shard_map/ppermute | solution.py:53
  109.9 9.6 %collective-permute-start.7 = (bf16[40,4096]{1,0:T(8,128)(2,1)S(1)}, bf16[40,4096]{1,0:T(8,128)(2,1)S(1)}, u32[]{:S(2)}, u32[]{:S(2)}) collective-permute-start(bf16[40,4096]{1,0:T(8,128)(2,1)S(1)} %collective-permute-done.6), channel_id=1, source_target_pairs={{0,32},{32,64},{64,96},{96,112},{112,80},{80,48},{48,16},{16,0},{1... | collective-permute-start | bytes 983048 | tf_op jit(solution)/shard_map/ppermute | solution.py:62
  129.5 10.8 %collective-permute-start.8 = (bf16[40,4096]{1,0:T(8,128)(2,1)S(1)}, bf16[40,4096]{1,0:T(8,128)(2,1)S(1)}, u32[]{:S(2)}, u32[]{:S(2)}) collective-permute-start(bf16[40,4096]{1,0:T(8,128)(2,1)S(1)} %collective-permute-done.7), channel_id=1, source_target_pairs={{0,32},{32,64},{64,96},{96,112},{112,80},{80,48},{48,16},{16,0},{1... | collective-permute-start | bytes 983048 | tf_op jit(solution)/shard_map/ppermute | solution.py:62
  140.3 11.1 %collective-permute-start.9 = (bf16[40,4096]{1,0:T(8,128)(2,1)S(1)}, bf16[40,4096]{1,0:T(8,128)(2,1)S(1)}, u32[]{:S(2)}, u32[]{:S(2)}) collective-permute-start(bf16[40,4096]{1,0:T(8,128)(2,1)S(1)} %collective-permute-done.8), channel_id=1, source_target_pairs={{0,32},{32,64},{64,96},{96,112},{112,80},{80,48},{48,16},{16,0},{1... | collective-permute-start | bytes 983048 | tf_op jit(solution)/shard_map/ppermute | solution.py:62
  151.3 4.2 %copy-start.3 = (bf16[160,4096]{1,0:T(8,128)(2,1)}, bf16[160,4096]{1,0:T(8,128)(2,1)S(1)}, u32[]{:S(2)}) copy-start(bf16[160,4096]{1,0:T(8,128)(2,1)S(1)} %constant_dynamic-update-slice_fusion.8) | copy-start | bytes 3932164
  157.1 34.4 %all-to-all-start.1 = ((bf16[8,80,384]{2,1,0:T(8,128)(2,1)}), bf16[8,80,384]{2,1,0:T(8,128)(2,1)}, u32[]{:S(2)}, u32[]{:S(2)}) async-start(bf16[8,80,384]{2,1,0:T(8,128)(2,1)} %broadcast_in_dim.13), calls=%async_computation.1 | async-start | bytes 983040 | tf_op jit(solution)/shard_map/all_to_all | solution.py:99
  166.1 13.9 %copy-start.4 = (bf16[160,4096]{1,0:T(8,128)(2,1)S(1)}, bf16[160,4096]{1,0:T(8,128)(2,1)}, u32[]{:S(2)}) copy-start(bf16[160,4096]{1,0:T(8,128)(2,1)} %copy-done.3) | copy-start | bytes 3932164
  166.1 13.8 %collective-permute-start.5 = (bf16[80,4096]{1,0:T(8,128)(2,1)S(1)}, bf16[80,4096]{1,0:T(8,128)(2,1)S(1)}, u32[]{:S(2)}, u32[]{:S(2)}) collective-permute-start(bf16[80,4096]{1,0:T(8,128)(2,1)S(1)} %reshape.151), channel_id=1, source_target_pairs={{0,384},{128,256},{256,128},{384,0},{1,385},{129,257},{257,129},{3... | collective-permute-start | bytes 1966088 | tf_op jit(solution)/shard_map/ppermute | solution.py:53
  181.1 23.4 %collective-permute-start.13 = (bf16[80,4096]{1,0:T(8,128)(2,1)}, bf16[80,4096]{1,0:T(8,128)(2,1)}, u32[]{:S(2)}, u32[]{:S(2)}) collective-permute-start(bf16[80,4096]{1,0:T(8,128)(2,1)} %reshape.153), channel_id=1, source_target_pairs={{0,128},{128,0},{256,384},{384,256},{1,129},{129,1},{257,385},{385... | collective-permute-start | bytes 1966088 | tf_op jit(solution)/shard_map/ppermute | solution.py:53
  183.5 26.3 %collective-permute-start.14 = (bf16[80,4096]{1,0:T(8,128)(2,1)}, bf16[80,4096]{1,0:T(8,128)(2,1)}, u32[]{:S(2)}, u32[]{:S(2)}) collective-permute-start(bf16[80,4096]{1,0:T(8,128)(2,1)} %reshape.153), channel_id=1, source_target_pairs={{0,256},{128,384},{256,0},{384,128},{1,257},{129,385},{257,1},{385... | collective-permute-start | bytes 1966088 | tf_op jit(solution)/shard_map/ppermute | solution.py:53
  187.5 30.3 %collective-permute-start.15 = (bf16[80,4096]{1,0:T(8,128)(2,1)}, bf16[80,4096]{1,0:T(8,128)(2,1)}, u32[]{:S(2)}, u32[]{:S(2)}) collective-permute-start(bf16[80,4096]{1,0:T(8,128)(2,1)} %reshape.153), channel_id=1, source_target_pairs={{0,384},{128,256},{256,128},{384,0},{1,385},{129,257},{257,129},{3... | collective-permute-start | bytes 1966088 | tf_op jit(solution)/shard_map/ppermute | solution.py:53
  198.0 24.3 %all-to-all-start.2 = ((bf16[4,48,1536]{2,1,0:T(8,128)(2,1)}), bf16[4,48,1536]{2,1,0:T(8,128)(2,1)S(1)}, u32[]{:S(2)}, u32[]{:S(2)}) async-start(bf16[4,48,1536]{2,1,0:T(8,128)(2,1)} %bitcast.52), calls=%async_computation.2 | async-start | bytes 1179648 | tf_op jit(solution)/shard_map/all_to_all | solution.py:104

commit v2 on v1

--- a/solution.py
+++ b/solution.py
@@ -63,18 +63,22 @@
 
     half = nz // 2
 
-    late = [(parts[half + i][:1, :1] * 0).reshape(1, 1) for i in range(2)]
-    stacked = [w_own, w_others[0] + late[0], w_others[1] + late[1]] + w_others[2:]
-    weights = jnp.concatenate(stacked, axis=0)
+    late = [(parts[i][:1, :1] * 0).reshape(1, 1) for i in (2, 4)]
+    weights = jnp.concatenate([w_own, w_others[0] + late[0], w_others[2], w_others[1] + late[1]], axis=0)
 
     group = nx * hid
     slots = nz * capacity
     place = jnp.where(zi % 2 == 0, zi // 2, nz - 1 - zi // 2)
     unit = jnp.arange(group, dtype=jnp.int32)
-    from_unit = ((unit // hid) ^ xi) * hid + unit % hid
+    offset = (unit // hid) ^ xi
+    from_unit = (offset ^ (offset >> 1)) * hid + unit % hid
     unit_perm = (from_unit[:, None] == unit[None, :]).astype(BF16)
     column = jnp.arange(half * 2 * capacity, dtype=jnp.int32)
-    slot = jnp.arange(slots, dtype=jnp.int32)
+    lanes = 128
+    rest = slots - lanes
+    packed_col = jnp.arange((nx + 1) * lanes, dtype=jnp.int32)
+    lane, part_of = packed_col % lanes, packed_col // lanes - 1
+    slot = jnp.where(part_of < 0, lane, jnp.where(lane // rest == part_of, lanes + lane % rest, -2))
 
     sorted_f32 = 0.0
     x_half = []
@@ -90,24 +94,31 @@
         arrival = h * half + column // (2 * capacity)
         within = column % (2 * capacity)
         target = jnp.where(within < capacity, ((place - arrival + nz) % nz) * capacity + within, -1)
-        slot_perm = (slot[:, None] == target[None, :]).astype(BF16)
-        sorted_f32 = sorted_f32 + dot_nt(slot_perm, gate_grad)
-    g_sorted = jnp.dot(sorted_f32.astype(BF16), unit_perm, preferred_element_type=F32).astype(BF16)
+        slot_perm = (target[:, None] == slot[None, :]).astype(BF16)
+        sorted_f32 = sorted_f32 + jnp.dot(gate_grad, slot_perm, preferred_element_type=F32)
+    g_packed = jnp.dot(unit_perm, sorted_f32.astype(BF16), preferred_element_type=F32).astype(BF16)
 
-    wide = jnp.concatenate([g_sorted[: slots // 2], g_sorted[slots // 2 :]], axis=1)
-    spread = jnp.broadcast_to(wide[None], (nz,) + wide.shape)
+    first = g_packed[:, :lanes]
+    lasts = [g_packed[:, (1 + j) * lanes : (2 + j) * lanes] for j in range(nx)]
+    tail = sum(v[j * hid : (j + 1) * hid] for j, v in enumerate(lasts))
+    sent = jnp.concatenate([first, tail], axis=0)
+    spread = jnp.broadcast_to(sent[None], (nz,) + sent.shape)
     spread = lax.all_to_all(spread, "zl", split_axis=0, concat_axis=0, tiled=True)
     later = (spread[0, :1, :1] * 0).reshape(1, 1)
-    spread = spread.reshape(nz, slots // 2, 2, nx, hid).transpose(2, 1, 3, 0, 4)
-    spread = spread.reshape(slots, nx * nz * hid)
-    part_sent = dot_tn(g_sorted, spread).astype(BF16).reshape(nx, hid, nx * nz * hid)
+    tails = spread[:, group:].reshape(nz * hid, lanes)
+    cols = []
+    for j in range(nx):
+        theirs = spread[:, j * hid : (j + 1) * hid].reshape(nz * hid, lanes)
+        both_j = jnp.concatenate([theirs, tails], axis=1)
+        cols.append(dot_nt(jnp.concatenate([first, lasts[j]], axis=1), both_j).astype(BF16))
+    part_sent = jnp.concatenate(cols, axis=1).reshape(nx, hid, nx * nz * hid)
     part = lax.all_to_all(part_sent, "x", split_axis=0, concat_axis=0, tiled=True)
     grad_rows = jnp.sum(part.astype(F32), axis=0) / float(slot_count)
 
     strip_width = full_width // (nx * nz)
     input_rows = 0.0
     for name, piece in zip(("xa", "xb"), x_half):
-        own_piece = piece if name == "xa" else piece + later
+        own_piece = piece + (later if name == "xb" else (sent[:1, :1] * 0))
         gathered = [own_piece] + [swap_x(piece, k) for k in range(1, nx)]
         rows = jnp.concatenate(gathered, axis=0)
         strip = lax.dynamic_slice_in_dim(rows, (xi * nz + zi) * strip_width, strip_width, 1)

time: 224 us -> 236 us (1.054)
  waiting for transfers between devices: 83.3 us -> 93.6 us
  local copies, waits for them, and re-layouts: 18.2 us -> 14 us
    ppermute x9, waiting for transfers between devices: 21.7 us -> 31.1 us  [swap_x(): return lax.ppermute(v, 'x', [(i, i ^ k) for i in range(nx)])]
    unnamed x2 -> x1, other arithmetic: 5.03 us -> 2.49 us
    concatenate x2 -> x0, local copies, waits for them, and re-layouts: 2.45 us -> none  [the longest x1 2.41 us: body(): weights = jnp.concatenate(stacked, axis=0)]
    dot_general x1 -> x4, matrix products: 0.19 us -> 2.58 us  [dot_nt(): lax.dot_general(a, b, (((1,), (1,)), ((), ())), preferred_element_type=F32)]
    unnamed x30 -> x36, local copies, waits for them, and re-layouts: 4.82 us -> 5.53 us
  transfers between devices with their start and end apart: 19 -> 19, of which waited for: 11 -> 12; matrix products, arithmetic and copies ran while one was open for 18% -> 11% of each run, Pallas kernels for 0% -> 0%
where the time goes in v2:
time: 236 us; the launch traced here: 234 us
  starting transfers between devices  94.2 us (40%)
  waiting for transfers between devices  93.6 us (40%)
  matrix products  15.3 us (6%)
  local copies, waits for them, and re-layouts  14 us (6%)
  other arithmetic  13.5 us (6%)
  between operations  3.79 us (2%)
    ppermute x7, waiting for transfers between devices, body(): parts.append(lax.ppermute(parts[-1], 'zl', pairs))  49.6 us
    ppermute x9, starting transfers between devices, swap_x(): return lax.ppermute(v, 'x', [(i, i ^ k) for i in range(nx)])  31.5 us
    ppermute x7, starting transfers between devices, body(): parts.append(lax.ppermute(parts[-1], 'zl', pairs))  31.5 us
    ppermute x9, waiting for transfers between devices, swap_x(): return lax.ppermute(v, 'x', [(i, i ^ k) for i in range(nx)])  31.1 us
    all_to_all x1, starting transfers between devices, body(): lax.all_to_all(packed, ('y', 'zh', 'c'), split_axis=0, concat_axis=0, til...  18.2 us
    all_to_all x1, waiting for transfers between devices, body(): lax.all_to_all(packed, ('y', 'zh', 'c'), split_axis=0, concat_axis=0, til...  12.9 us
    all_to_all x1, starting transfers between devices, body(): lax.all_to_all(spread, 'zl', split_axis=0, concat_axis=0, tiled=True)  8.97 us
    reshape x2, matrix products, body(): pre = dot_nt(weights, rows).reshape(nx, 3 * hid, -1)  7.93 us
  transfers between devices with their start and end apart: 19, of which 12 were waited for; matrix products, arithmetic and copies ran while one was open for 11% of the time, Pallas kernels for 0%

profile of v2, /device:TPU:8, one launch (start us, length us, event | category | flops | bytes accessed | tf_op | source)
XLA Modules:
  0.0 234.4 jit_solution(16628434676614595320)
XLA Ops:
  0.7 2.4 %pad_maximum_fusion.2 = bf16[144,4096]{1,0:T(8,128)(2,1)} fusion(bf16[48,4096]{1,0:T(8,128)(2,1)} %bitcast.53, bf16[48,4096]{1,0:T(8,128)(2,1)} %bitcast.52, bf16[48,4096]{1,0:T(8,128)(2,1)} %bitcast.51), kind=kLoop, calls=%fused_computation.9 | loop fusion | flops 3538944 | bytes 2359296 | tf_op jit(solution)/shard_map/concatenate | solution.py:55
  3.1 3.4 %collective-permute-start.3 = (bf16[144,4096]{1,0:T(8,128)(2,1)}, bf16[144,4096]{1,0:T(8,128)(2,1)}, u32[]{:S(2)}, u32[]{:S(2)}) collective-permute-start(bf16[144,4096]{1,0:T(8,128)(2,1)} %pad_maximum_fusion.2), channel_id=1, source_target_pairs={{0,128},{128,0},{256,384},{384,256},{1,129},{129,1},{257,385},{385... | collective-permute-start | bytes 3538952 | tf_op jit(solution)/shard_map/ppermute | solution.py:53
  6.5 4.0 %collective-permute-start.4 = (bf16[144,4096]{1,0:T(8,128)(2,1)}, bf16[144,4096]{1,0:T(8,128)(2,1)}, u32[]{:S(2)}, u32[]{:S(2)}) collective-permute-start(bf16[144,4096]{1,0:T(8,128)(2,1)} %pad_maximum_fusion.2), channel_id=1, source_target_pairs={{0,384},{128,256},{256,128},{384,0},{1,385},{129,257},{257,129},{3... | collective-permute-start | bytes 3538952 | tf_op jit(solution)/shard_map/ppermute | solution.py:53
  10.6 2.6 %collective-permute-start.5 = (bf16[144,4096]{1,0:T(8,128)(2,1)}, bf16[144,4096]{1,0:T(8,128)(2,1)S(1)}, u32[]{:S(2)}, u32[]{:S(2)}) collective-permute-start(bf16[144,4096]{1,0:T(8,128)(2,1)} %pad_maximum_fusion.2), channel_id=1, source_target_pairs={{0,256},{128,384},{256,0},{384,128},{1,257},{129,385},{257,1},{385... | collective-permute-start | bytes 3538952 | tf_op jit(solution)/shard_map/ppermute | solution.py:53
  13.2 0.6 reduce-window.6
  14.3 1.1 convolution_convert_fusion
  15.4 18.2 %all-to-all-start = ((bf16[16,40,256]{2,1,0:T(8,128)(2,1)}), bf16[16,40,256]{2,1,0:T(8,128)(2,1)S(1)}, u32[]{:S(2)}, u32[]{:S(2)}) async-start(bf16[16,40,256]{2,1,0:T(8,128)(2,1)} %bitcast.1), calls=%async_computation | async-start | bytes 655360 | tf_op jit(solution)/shard_map/all_to_all | solution.py:49
  33.6 0.8 constant_dynamic-update-slice_fusion.7
  34.3 0.8 constant_dynamic-update-slice_fusion.6
  35.1 0.8 constant_dynamic-update-slice_fusion.5
  36.0 12.9 %all-to-all-done = bf16[16,40,256]{2,1,0:T(8,128)(2,1)S(1)} async-done(((bf16[16,40,256]{2,1,0:T(8,128)(2,1)}), bf16[16,40,256]{2,1,0:T(8,128)(2,1)S(1)}, u32[]{:S(2)}, u32[]{:S(2)}) %all-to-all-start) | async-done | bytes 327712 | tf_op jit(solution)/shard_map/all_to_all | solution.py:49
  48.8 9.9 %collective-permute-start = (bf16[40,4096]{1,0:T(8,128)(2,1)S(1)}, bf16[40,4096]{1,0:T(8,128)(2,1)S(1)}, u32[]{:S(2)}, u32[]{:S(2)}) collective-permute-start(bf16[40,4096]{1,0:T(8,128)(2,1)S(1)} %bitcast.55), channel_id=1, source_target_pairs={{0,32},{32,64},{64,96},{96,112},{112,80},{80,48},{48,16},{16,0},{1... | collective-permute-start | bytes 983048 | tf_op jit(solution)/shard_map/ppermute | solution.py:62
  58.8 11.5 %collective-permute-done = bf16[40,4096]{1,0:T(8,128)(2,1)S(1)} collective-permute-done((bf16[40,4096]{1,0:T(8,128)(2,1)S(1)}, bf16[40,4096]{1,0:T(8,128)(2,1)S(1)}, u32[]{:S(2)}, u32[]{:S(2)}) %collective-permute-start) | collective-permute-done | bytes 327712 | tf_op jit(solution)/shard_map/ppermute | solution.py:62
  70.3 1.9 collective-permute-start.1
  72.3 10.2 %collective-permute-done.1 = bf16[40,4096]{1,0:T(8,128)(2,1)S(1)} collective-permute-done((bf16[40,4096]{1,0:T(8,128)(2,1)S(1)}, bf16[40,4096]{1,0:T(8,128)(2,1)S(1)}, u32[]{:S(2)}, u32[]{:S(2)}) %collective-permute-start.1) | collective-permute-done | bytes 327712 | tf_op jit(solution)/shard_map/ppermute | solution.py:62
  82.5 0.5 slice.138
  83.6 2.5 %collective-permute-start.2 = (bf16[40,4096]{1,0:T(8,128)(2,1)S(1)}, bf16[40,4096]{1,0:T(8,128)(2,1)S(1)}, u32[]{:S(2)}, u32[]{:S(2)}) collective-permute-start(bf16[40,4096]{1,0:T(8,128)(2,1)S(1)} %collective-permute-done.1), channel_id=1, source_target_pairs={{0,32},{32,64},{64,96},{96,112},{112,80},{80,48},{48,16},{16,0},{1... | collective-permute-start | bytes 983048 | tf_op jit(solution)/shard_map/ppermute | solution.py:62
  86.1 2.5 %add_dynamic-update-slice_fusion.1 = bf16[576,4096]{1,0:T(8,128)(2,1)} fusion(bf16[576,4096]{1,0:T(8,128)(2,1)} %constant_dynamic-update-slice_fusion.5, bf16[144,4096]{1,0:T(8,128)(2,1)} %collective-permute-done.3, bf16[]{:T(256)} %bitcast.7), kind=kLoop, calls=%fused_computation.12 | loop fusion | flops 2359296 | bytes 2359808
  88.6 2.4 %constant_dynamic-update-slice_fusion.4 = bf16[576,4096]{1,0:T(8,128)(2,1)} fusion(bf16[576,4096]{1,0:T(8,128)(2,1)} %add_dynamic-update-slice_fusion.1, bf16[144,4096]{1,0:T(8,128)(2,1)} %collective-permute-done.4), kind=kLoop, calls=%fused_computation.65 | loop fusion | bytes 2359296
  91.1 3.8 %collective-permute-done.2 = bf16[40,4096]{1,0:T(8,128)(2,1)S(1)} collective-permute-done((bf16[40,4096]{1,0:T(8,128)(2,1)S(1)}, bf16[40,4096]{1,0:T(8,128)(2,1)S(1)}, u32[]{:S(2)}, u32[]{:S(2)}) %collective-permute-start.2) | collective-permute-done | bytes 327712 | tf_op jit(solution)/shard_map/ppermute | solution.py:62
  94.9 3.0 %collective-permute-start.6 = (bf16[40,4096]{1,0:T(8,128)(2,1)S(1)}, bf16[40,4096]{1,0:T(8,128)(2,1)S(1)}, u32[]{:S(2)}, u32[]{:S(2)}) collective-permute-start(bf16[40,4096]{1,0:T(8,128)(2,1)S(1)} %collective-permute-done.2), channel_id=1, source_target_pairs={{0,32},{32,64},{64,96},{96,112},{112,80},{80,48},{48,16},{16,0},{1... | collective-permute-start | bytes 983048 | tf_op jit(solution)/shard_map/ppermute | solution.py:62
  98.0 7.3 %collective-permute-done.6 = bf16[40,4096]{1,0:T(8,128)(2,1)S(1)} collective-permute-done((bf16[40,4096]{1,0:T(8,128)(2,1)S(1)}, bf16[40,4096]{1,0:T(8,128)(2,1)S(1)}, u32[]{:S(2)}, u32[]{:S(2)}) %collective-permute-start.6) | collective-permute-done | bytes 327712 | tf_op jit(solution)/shard_map/ppermute | solution.py:62
  105.3 0.5 slice.139
  106.5 1.2 add_dynamic-update-slice_fusion
  107.8 3.7 %fusion.77 = f32[576,160]{1,0:T(8,128)S(1)} fusion(bf16[576,4096]{1,0:T(8,128)(2,1)} %add_dynamic-update-slice_fusion, bf16[160,4096]{1,0:T(8,128)(2,1)S(1)} %constant_dynamic-update-slice_fusion), kind=kOutput, calls=%fused_computation.161 | convolution fusion | flops 754974720 | bytes 6397952 | tf_op jit(solution)/shard_map/reshape | solution.py:90
  111.6 3.6 %collective-permute-start.7 = (bf16[40,4096]{1,0:T(8,128)(2,1)S(1)}, bf16[40,4096]{1,0:T(8,128)(2,1)S(1)}, u32[]{:S(2)}, u32[]{:S(2)}) collective-permute-start(bf16[40,4096]{1,0:T(8,128)(2,1)S(1)} %collective-permute-done.6), channel_id=1, source_target_pairs={{0,32},{32,64},{64,96},{96,112},{112,80},{80,48},{48,16},{16,0},{1... | collective-permute-start | bytes 983048 | tf_op jit(solution)/shard_map/ppermute | solution.py:62
  115.4 0.3 fusion.6
  115.7 5.5 %collective-permute-done.7 = bf16[40,4096]{1,0:T(8,128)(2,1)S(1)} collective-permute-done((bf16[40,4096]{1,0:T(8,128)(2,1)S(1)}, bf16[40,4096]{1,0:T(8,128)(2,1)S(1)}, u32[]{:S(2)}, u32[]{:S(2)}) %collective-permute-start.7) | collective-permute-done | bytes 327712 | tf_op jit(solution)/shard_map/ppermute | solution.py:62
  121.2 5.1 %collective-permute-start.8 = (bf16[40,4096]{1,0:T(8,128)(2,1)S(1)}, bf16[40,4096]{1,0:T(8,128)(2,1)S(1)}, u32[]{:S(2)}, u32[]{:S(2)}) collective-permute-start(bf16[40,4096]{1,0:T(8,128)(2,1)S(1)} %collective-permute-done.7), channel_id=1, source_target_pairs={{0,32},{32,64},{64,96},{96,112},{112,80},{80,48},{48,16},{16,0},{1... | collective-permute-start | bytes 983048 | tf_op jit(solution)/shard_map/ppermute | solution.py:62
  126.4 5.6 %collective-permute-done.8 = bf16[40,4096]{1,0:T(8,128)(2,1)S(1)} collective-permute-done((bf16[40,4096]{1,0:T(8,128)(2,1)S(1)}, bf16[40,4096]{1,0:T(8,128)(2,1)S(1)}, u32[]{:S(2)}, u32[]{:S(2)}) %collective-permute-start.8) | collective-permute-done | bytes 327712 | tf_op jit(solution)/shard_map/ppermute | solution.py:62
  132.0 5.4 %collective-permute-start.9 = (bf16[40,4096]{1,0:T(8,128)(2,1)S(1)}, bf16[40,4096]{1,0:T(8,128)(2,1)S(1)}, u32[]{:S(2)}, u32[]{:S(2)}) collective-permute-start(bf16[40,4096]{1,0:T(8,128)(2,1)S(1)} %collective-permute-done.8), channel_id=1, source_target_pairs={{0,32},{32,64},{64,96},{96,112},{112,80},{80,48},{48,16},{16,0},{1... | collective-permute-start | bytes 983048 | tf_op jit(solution)/shard_map/ppermute | solution.py:62
  137.4 5.6 %collective-permute-done.9 = bf16[40,4096]{1,0:T(8,128)(2,1)S(1)} collective-permute-done((bf16[40,4096]{1,0:T(8,128)(2,1)S(1)}, bf16[40,4096]{1,0:T(8,128)(2,1)S(1)}, u32[]{:S(2)}, u32[]{:S(2)}) %collective-permute-start.9) | collective-permute-done | bytes 327712 | tf_op jit(solution)/shard_map/ppermute | solution.py:62
  143.1 4.2 %fusion.78 = f32[576,160]{1,0:T(8,128)S(1)} fusion(bf16[576,4096]{1,0:T(8,128)(2,1)} %add_dynamic-update-slice_fusion, bf16[160,4096]{1,0:T(8,128)(2,1)S(1)} %constant_dynamic-update-slice_fusion.8), kind=kOutput, calls=%fused_computation.162 | convolution fusion | flops 754974720 | bytes 6397952 | tf_op jit(solution)/shard_map/reshape | solution.py:90
  147.6 0.5 convolution_convert_fusion.1
  148.1 0.7 fusion.76
  148.8 0.6 copy-done.6
  149.4 0.8 broadcast_in_dim.18
  150.2 9.0 %all-to-all-start.1 = ((bf16[8,240,128]{2,1,0:T(8,128)(2,1)}), bf16[8,240,128]{2,1,0:T(8,128)(2,1)}, u32[]{:S(2)}, u32[]{:S(2)}) async-start(bf16[8,240,128]{2,1,0:T(8,128)(2,1)} %broadcast_in_dim.18), calls=%async_computation.1 | async-start | bytes 983040 | tf_op jit(solution)/shard_map/all_to_all | solution.py:106
  159.2 1.2 slice.137
  160.5 3.2 %collective-permute-start.10 = (bf16[80,4096]{1,0:T(8,128)(2,1)S(1)}, bf16[80,4096]{1,0:T(8,128)(2,1)S(1)}, u32[]{:S(2)}, u32[]{:S(2)}) collective-permute-start(bf16[80,4096]{1,0:T(8,128)(2,1)S(1)} %reshape.214), channel_id=1, source_target_pairs={{0,128},{128,0},{256,384},{384,256},{1,129},{129,1},{257,385},{385... | collective-permute-start | bytes 1966088 | tf_op jit(solution)/shard_map/ppermute | solution.py:53
  163.8 4.7 %collective-permute-start.11 = (bf16[80,4096]{1,0:T(8,128)(2,1)S(1)}, bf16[80,4096]{1,0:T(8,128)(2,1)}, u32[]{:S(2)}, u32[]{:S(2)}) collective-permute-start(bf16[80,4096]{1,0:T(8,128)(2,1)S(1)} %reshape.214), channel_id=1, source_target_pairs={{0,256},{128,384},{256,0},{384,128},{1,257},{129,385},{257,1},{385... | collective-permute-start | bytes 1966088 | tf_op jit(solution)/shard_map/ppermute | solution.py:53
  168.5 2.5 %collective-permute-start.12 = (bf16[80,4096]{1,0:T(8,128)(2,1)S(1)}, bf16[80,4096]{1,0:T(8,128)(2,1)}, u32[]{:S(2)}, u32[]{:S(2)}) collective-permute-start(bf16[80,4096]{1,0:T(8,128)(2,1)S(1)} %reshape.214), channel_id=1, source_target_pairs={{0,384},{128,256},{256,128},{384,0},{1,385},{129,257},{257,129},{3... | collective-permute-start | bytes 1966088 | tf_op jit(solution)/shard_map/ppermute | solution.py:53
  171.0 0.5 slice.148
  171.5 1.2 slice.149
  172.8 2.0 collective-permute-start.13
  174.9 5.9 %collective-permute-start.14 = (bf16[80,4096]{1,0:T(8,128)(2,1)S(1)}, bf16[80,4096]{1,0:T(8,128)(2,1)}, u32[]{:S(2)}, u32[]{:S(2)}) collective-permute-start(bf16[80,4096]{1,0:T(8,128)(2,1)S(1)} %reshape.220), channel_id=1, source_target_pairs={{0,256},{128,384},{256,0},{384,128},{1,257},{129,385},{257,1},{385... | collective-permute-start | bytes 1966088 | tf_op jit(solution)/shard_map/ppermute | solution.py:53
  181.4 3.2 %collective-permute-start.15 = (bf16[80,4096]{1,0:T(8,128)(2,1)S(1)}, bf16[80,4096]{1,0:T(8,128)(2,1)}, u32[]{:S(2)}, u32[]{:S(2)}) collective-permute-start(bf16[80,4096]{1,0:T(8,128)(2,1)S(1)} %reshape.220), channel_id=1, source_target_pairs={{0,384},{128,256},{256,128},{384,0},{1,385},{129,257},{257,129},{3... | collective-permute-start | bytes 1966088 | tf_op jit(solution)/shard_map/ppermute | solution.py:53
  184.6 11.8 %collective-permute-done.11 = bf16[80,4096]{1,0:T(8,128)(2,1)} collective-permute-done((bf16[80,4096]{1,0:T(8,128)(2,1)S(1)}, bf16[80,4096]{1,0:T(8,128)(2,1)}, u32[]{:S(2)}, u32[]{:S(2)}) %collective-permute-start.11) | collective-permute-done | bytes 655392 | tf_op jit(solution)/shard_map/ppermute | solution.py:53
  196.4 6.9 %collective-permute-done.12 = bf16[80,4096]{1,0:T(8,128)(2,1)} collective-permute-done((bf16[80,4096]{1,0:T(8,128)(2,1)S(1)}, bf16[80,4096]{1,0:T(8,128)(2,1)}, u32[]{:S(2)}, u32[]{:S(2)}) %collective-permute-start.12) | collective-permute-done | bytes 655392 | tf_op jit(solution)/shard_map/ppermute | solution.py:53
  203.3 1.6 pad_maximum_fusion
  204.9 1.1 fusion.75
  206.1 0.2 convolution_convert_fusion.5
  206.3 1.1 convolution_convert_fusion.4
  207.4 1.1 convolution_convert_fusion.3
  208.7 0.9 pad_maximum_fusion.3
  209.6 4.1 %all-to-all-start.2 = ((bf16[4,48,1536]{2,1,0:T(8,128)(2,1)}), bf16[4,48,1536]{2,1,0:T(8,128)(2,1)}, u32[]{:S(2)}, u32[]{:S(2)}) async-start(bf16[4,48,1536]{2,1,0:T(8,128)(2,1)} %bitcast.50), calls=%async_computation.2 | async-start | bytes 1179648 | tf_op jit(solution)/shard_map/all_to_all | solution.py:115
  213.7 1.2 slice.155
  215.6 4.4 %collective-permute-done.14 = bf16[80,4096]{1,0:T(8,128)(2,1)} collective-permute-done((bf16[80,4096]{1,0:T(8,128)(2,1)S(1)}, bf16[80,4096]{1,0:T(8,128)(2,1)}, u32[]{:S(2)}, u32[]{:S(2)}) %collective-permute-start.14) | collective-permute-done | bytes 655392 | tf_op jit(solution)/shard_map/ppermute | solution.py:53
  220.1 7.9 %collective-permute-done.15 = bf16[80,4096]{1,0:T(8,128)(2,1)} collective-permute-done((bf16[80,4096]{1,0:T(8,128)(2,1)S(1)}, bf16[80,4096]{1,0:T(8,128)(2,1)}, u32[]{:S(2)}, u32[]{:S(2)}) %collective-permute-start.15) | collective-permute-done | bytes 655392 | tf_op jit(solution)/shard_map/ppermute | solution.py:53
  228.0 1.6 pad_maximum_fusion.1
  229.6 0.8 fusion.30
  230.4 2.1 fusion.1
  232.5 1.2 convert_reduce_fusion
  233.6 0.7 multiply_bitcast_fusion
  (69 shorter events, 1.9 us)
Async XLA Ops:
  0.6 32.9 %copy-start = (bf16[1,48,4096]{2,1,0:T(8,128)(2,1)S(1)}, bf16[1,48,4096]{2,1,0:T(8,128)(2,1)}, u32[]{:S(2)}) copy-start(bf16[1,48,4096]{2,1,0:T(8,128)(2,1)} %param.11) | copy-start | bytes 1179652
  0.6 12.5 %copy-start.10 = (s32[160,8]{0,1:T(8,128)S(1)}, s32[160,8]{0,1:T(8,128)}, u32[]{:S(2)}) copy-start(s32[160,8]{0,1:T(8,128)} %param.10) | copy-start | bytes 15364
  0.7 12.5 %copy-start.11 = (s32[160,8]{0,1:T(8,128)S(1)}, s32[160,8]{0,1:T(8,128)}, u32[]{:S(2)}) copy-start(s32[160,8]{0,1:T(8,128)} %param.9) | copy-start | bytes 15364
  0.7 13.5 %copy-start.8 = (bf16[160,256]{1,0:T(8,128)(2,1)S(1)}, bf16[160,256]{1,0:T(8,128)(2,1)}, u32[]{:S(2)}) copy-start(bf16[160,256]{1,0:T(8,128)(2,1)} %param.8) | copy-start | bytes 245764
  0.7 13.6 %copy-start.12 = (bf16[160,256]{1,0:T(8,128)(2,1)S(1)}, bf16[160,256]{1,0:T(8,128)(2,1)}, u32[]{:S(2)}) copy-start(bf16[160,256]{1,0:T(8,128)(2,1)} %param.7) | copy-start | bytes 245764
  0.7 33.6 %copy-start.1 = (bf16[1,48,4096]{2,1,0:T(8,128)(2,1)S(1)}, bf16[1,48,4096]{2,1,0:T(8,128)(2,1)}, u32[]{:S(2)}) copy-start(bf16[1,48,4096]{2,1,0:T(8,128)(2,1)} %param.12) | copy-start | bytes 1179652
  0.7 34.4 %copy-start.2 = (bf16[1,48,4096]{2,1,0:T(8,128)(2,1)S(1)}, bf16[1,48,4096]{2,1,0:T(8,128)(2,1)}, u32[]{:S(2)}) copy-start(bf16[1,48,4096]{2,1,0:T(8,128)(2,1)} %param.13) | copy-start | bytes 1179652
  3.1 83.0 %collective-permute-start.3 = (bf16[144,4096]{1,0:T(8,128)(2,1)}, bf16[144,4096]{1,0:T(8,128)(2,1)}, u32[]{:S(2)}, u32[]{:S(2)}) collective-permute-start(bf16[144,4096]{1,0:T(8,128)(2,1)} %pad_maximum_fusion.2), channel_id=1, source_target_pairs={{0,128},{128,0},{256,384},{384,256},{1,129},{129,1},{257,385},{385... | collective-permute-start | bytes 3538952 | tf_op jit(solution)/shard_map/ppermute | solution.py:53
  6.5 82.1 %collective-permute-start.4 = (bf16[144,4096]{1,0:T(8,128)(2,1)}, bf16[144,4096]{1,0:T(8,128)(2,1)}, u32[]{:S(2)}, u32[]{:S(2)}) collective-permute-start(bf16[144,4096]{1,0:T(8,128)(2,1)} %pad_maximum_fusion.2), channel_id=1, source_target_pairs={{0,384},{128,256},{256,128},{384,0},{1,385},{129,257},{257,129},{3... | collective-permute-start | bytes 3538952 | tf_op jit(solution)/shard_map/ppermute | solution.py:53
  10.6 95.9 %collective-permute-start.5 = (bf16[144,4096]{1,0:T(8,128)(2,1)}, bf16[144,4096]{1,0:T(8,128)(2,1)S(1)}, u32[]{:S(2)}, u32[]{:S(2)}) collective-permute-start(bf16[144,4096]{1,0:T(8,128)(2,1)} %pad_maximum_fusion.2), channel_id=1, source_target_pairs={{0,256},{128,384},{256,0},{384,128},{1,257},{129,385},{257,1},{385... | collective-permute-start | bytes 3538952 | tf_op jit(solution)/shard_map/ppermute | solution.py:53
  15.4 33.4 %all-to-all-start = ((bf16[16,40,256]{2,1,0:T(8,128)(2,1)}), bf16[16,40,256]{2,1,0:T(8,128)(2,1)S(1)}, u32[]{:S(2)}, u32[]{:S(2)}) async-start(bf16[16,40,256]{2,1,0:T(8,128)(2,1)} %bitcast.1), calls=%async_computation | async-start | bytes 655360 | tf_op jit(solution)/shard_map/all_to_all | solution.py:49
  48.8 21.5 %collective-permute-start = (bf16[40,4096]{1,0:T(8,128)(2,1)S(1)}, bf16[40,4096]{1,0:T(8,128)(2,1)S(1)}, u32[]{:S(2)}, u32[]{:S(2)}) collective-permute-start(bf16[40,4096]{1,0:T(8,128)(2,1)S(1)} %bitcast.55), channel_id=1, source_target_pairs={{0,32},{32,64},{64,96},{96,112},{112,80},{80,48},{48,16},{16,0},{1... | collective-permute-start | bytes 983048 | tf_op jit(solution)/shard_map/ppermute | solution.py:62
  70.3 12.1 %collective-permute-start.1 = (bf16[40,4096]{1,0:T(8,128)(2,1)S(1)}, bf16[40,4096]{1,0:T(8,128)(2,1)S(1)}, u32[]{:S(2)}, u32[]{:S(2)}) collective-permute-start(bf16[40,4096]{1,0:T(8,128)(2,1)S(1)} %collective-permute-done), channel_id=1, source_target_pairs={{0,32},{32,64},{64,96},{96,112},{112,80},{80,48},{48,16},{16,0},{1... | collective-permute-start | bytes 983048 | tf_op jit(solution)/shard_map/ppermute | solution.py:62
  83.6 11.3 %collective-permute-start.2 = (bf16[40,4096]{1,0:T(8,128)(2,1)S(1)}, bf16[40,4096]{1,0:T(8,128)(2,1)S(1)}, u32[]{:S(2)}, u32[]{:S(2)}) collective-permute-start(bf16[40,4096]{1,0:T(8,128)(2,1)S(1)} %collective-permute-done.1), channel_id=1, source_target_pairs={{0,32},{32,64},{64,96},{96,112},{112,80},{80,48},{48,16},{16,0},{1... | collective-permute-start | bytes 983048 | tf_op jit(solution)/shard_map/ppermute | solution.py:62
  94.9 10.4 %collective-permute-start.6 = (bf16[40,4096]{1,0:T(8,128)(2,1)S(1)}, bf16[40,4096]{1,0:T(8,128)(2,1)S(1)}, u32[]{:S(2)}, u32[]{:S(2)}) collective-permute-start(bf16[40,4096]{1,0:T(8,128)(2,1)S(1)} %collective-permute-done.2), channel_id=1, source_target_pairs={{0,32},{32,64},{64,96},{96,112},{112,80},{80,48},{48,16},{16,0},{1... | collective-permute-start | bytes 983048 | tf_op jit(solution)/shard_map/ppermute | solution.py:62
  98.0 13.5 %copy-start.4 = (bf16[160,4096]{1,0:T(8,128)(2,1)}, bf16[160,4096]{1,0:T(8,128)(2,1)S(1)}, u32[]{:S(2)}) copy-start(bf16[160,4096]{1,0:T(8,128)(2,1)S(1)} %constant_dynamic-update-slice_fusion) | copy-start | bytes 3932164
  111.6 9.6 %collective-permute-start.7 = (bf16[40,4096]{1,0:T(8,128)(2,1)S(1)}, bf16[40,4096]{1,0:T(8,128)(2,1)S(1)}, u32[]{:S(2)}, u32[]{:S(2)}) collective-permute-start(bf16[40,4096]{1,0:T(8,128)(2,1)S(1)} %collective-permute-done.6), channel_id=1, source_target_pairs={{0,32},{32,64},{64,96},{96,112},{112,80},{80,48},{48,16},{16,0},{1... | collective-permute-start | bytes 983048 | tf_op jit(solution)/shard_map/ppermute | solution.py:62
  121.2 10.8 %collective-permute-start.8 = (bf16[40,4096]{1,0:T(8,128)(2,1)S(1)}, bf16[40,4096]{1,0:T(8,128)(2,1)S(1)}, u32[]{:S(2)}, u32[]{:S(2)}) collective-permute-start(bf16[40,4096]{1,0:T(8,128)(2,1)S(1)} %collective-permute-done.7), channel_id=1, source_target_pairs={{0,32},{32,64},{64,96},{96,112},{112,80},{80,48},{48,16},{16,0},{1... | collective-permute-start | bytes 983048 | tf_op jit(solution)/shard_map/ppermute | solution.py:62
  132.0 11.1 %collective-permute-start.9 = (bf16[40,4096]{1,0:T(8,128)(2,1)S(1)}, bf16[40,4096]{1,0:T(8,128)(2,1)S(1)}, u32[]{:S(2)}, u32[]{:S(2)}) collective-permute-start(bf16[40,4096]{1,0:T(8,128)(2,1)S(1)} %collective-permute-done.8), channel_id=1, source_target_pairs={{0,32},{32,64},{64,96},{96,112},{112,80},{80,48},{48,16},{16,0},{1... | collective-permute-start | bytes 983048 | tf_op jit(solution)/shard_map/ppermute | solution.py:62
  143.1 4.2 %copy-start.3 = (bf16[160,4096]{1,0:T(8,128)(2,1)}, bf16[160,4096]{1,0:T(8,128)(2,1)S(1)}, u32[]{:S(2)}) copy-start(bf16[160,4096]{1,0:T(8,128)(2,1)S(1)} %constant_dynamic-update-slice_fusion.8) | copy-start | bytes 3932164
  148.8 0.6 copy-start.6
  150.2 54.7 %all-to-all-start.1 = ((bf16[8,240,128]{2,1,0:T(8,128)(2,1)}), bf16[8,240,128]{2,1,0:T(8,128)(2,1)}, u32[]{:S(2)}, u32[]{:S(2)}) async-start(bf16[8,240,128]{2,1,0:T(8,128)(2,1)} %broadcast_in_dim.18), calls=%async_computation.1 | async-start | bytes 983040 | tf_op jit(solution)/shard_map/all_to_all | solution.py:106
  160.5 20.8 %collective-permute-start.10 = (bf16[80,4096]{1,0:T(8,128)(2,1)S(1)}, bf16[80,4096]{1,0:T(8,128)(2,1)S(1)}, u32[]{:S(2)}, u32[]{:S(2)}) collective-permute-start(bf16[80,4096]{1,0:T(8,128)(2,1)S(1)} %reshape.214), channel_id=1, source_target_pairs={{0,128},{128,0},{256,384},{384,256},{1,129},{129,1},{257,385},{385... | collective-permute-start | bytes 1966088 | tf_op jit(solution)/shard_map/ppermute | solution.py:53
  163.8 32.6 %collective-permute-start.11 = (bf16[80,4096]{1,0:T(8,128)(2,1)S(1)}, bf16[80,4096]{1,0:T(8,128)(2,1)}, u32[]{:S(2)}, u32[]{:S(2)}) collective-permute-start(bf16[80,4096]{1,0:T(8,128)(2,1)S(1)} %reshape.214), channel_id=1, source_target_pairs={{0,256},{128,384},{256,0},{384,128},{1,257},{129,385},{257,1},{385... | collective-permute-start | bytes 1966088 | tf_op jit(solution)/shard_map/ppermute | solution.py:53
  168.5 34.8 %collective-permute-start.12 = (bf16[80,4096]{1,0:T(8,128)(2,1)S(1)}, bf16[80,4096]{1,0:T(8,128)(2,1)}, u32[]{:S(2)}, u32[]{:S(2)}) collective-permute-start(bf16[80,4096]{1,0:T(8,128)(2,1)S(1)} %reshape.214), channel_id=1, source_target_pairs={{0,384},{128,256},{256,128},{384,0},{1,385},{129,257},{257,129},{3... | collective-permute-start | bytes 1966088 | tf_op jit(solution)/shard_map/ppermute | solution.py:53
  172.8 42.8 %collective-permute-start.13 = (bf16[80,4096]{1,0:T(8,128)(2,1)S(1)}, bf16[80,4096]{1,0:T(8,128)(2,1)}, u32[]{:S(2)}, u32[]{:S(2)}) collective-permute-start(bf16[80,4096]{1,0:T(8,128)(2,1)S(1)} %reshape.220), channel_id=1, source_target_pairs={{0,128},{128,0},{256,384},{384,256},{1,129},{129,1},{257,385},{385... | collective-permute-start | bytes 1966088 | tf_op jit(solution)/shard_map/ppermute | solution.py:53
  174.9 45.2 %collective-permute-start.14 = (bf16[80,4096]{1,0:T(8,128)(2,1)S(1)}, bf16[80,4096]{1,0:T(8,128)(2,1)}, u32[]{:S(2)}, u32[]{:S(2)}) collective-permute-start(bf16[80,4096]{1,0:T(8,128)(2,1)S(1)} %reshape.220), channel_id=1, source_target_pairs={{0,256},{128,384},{256,0},{384,128},{1,257},{129,385},{257,1},{385... | collective-permute-start | bytes 1966088 | tf_op jit(solution)/shard_map/ppermute | solution.py:53
  181.3 15.0 %copy-start.5 = (bf16[80,4096]{1,0:T(8,128)(2,1)}, bf16[80,4096]{1,0:T(8,128)(2,1)S(1)}, u32[]{:S(2)}) copy-start(bf16[80,4096]{1,0:T(8,128)(2,1)S(1)} %collective-permute-done.10) | copy-start | bytes 1966084
  181.4 46.6 %collective-permute-start.15 = (bf16[80,4096]{1,0:T(8,128)(2,1)S(1)}, bf16[80,4096]{1,0:T(8,128)(2,1)}, u32[]{:S(2)}, u32[]{:S(2)}) collective-permute-start(bf16[80,4096]{1,0:T(8,128)(2,1)S(1)} %reshape.220), channel_id=1, source_target_pairs={{0,384},{128,256},{256,128},{384,0},{1,385},{129,257},{257,129},{3... | collective-permute-start | bytes 1966088 | tf_op jit(solution)/shard_map/ppermute | solution.py:53
  204.9 3.5 %copy-start.7 = (bf16[192,128]{1,0:T(8,128)(2,1)S(1)}, bf16[192,128]{1,0:T(8,128)(2,1)}, u32[]{:S(2)}) copy-start(bf16[192,128]{1,0:T(8,128)(2,1)} %copy-done.6) | copy-start | bytes 147460
  204.9 3.5 %copy-start.9 = (bf16[192,128]{1,0:T(8,128)(2,1)S(1)}, bf16[192,128]{1,0:T(8,128)(2,1)}, u32[]{:S(2)}) copy-start(bf16[192,128]{1,0:T(8,128)(2,1)} %get-tuple-element.12) | copy-start | bytes 147460
  209.6 22.9 %all-to-all-start.2 = ((bf16[4,48,1536]{2,1,0:T(8,128)(2,1)}), bf16[4,48,1536]{2,1,0:T(8,128)(2,1)}, u32[]{:S(2)}, u32[]{:S(2)}) async-start(bf16[4,48,1536]{2,1,0:T(8,128)(2,1)} %bitcast.50), calls=%async_computation.2 | async-start | bytes 1179648 | tf_op jit(solution)/shard_map/all_to_all | solution.py:115

commit v3 on v2

--- a/solution.py
+++ b/solution.py
@@ -57,10 +57,23 @@
 
     order = list(range(0, nz, 2)) + list(range(nz - 1, 0, -2))
     pairs = [(order[i], order[(i + 1) % nz]) for i in range(nz)]
-    parts = [own]
-    for _ in range(1, nz):
-        parts.append(lax.ppermute(parts[-1], "zl", pairs))
+    back = [(j, i) for i, j in pairs]
 
+    def hop(v, way):
+        return lax.ppermute(v, "zl", way)
+
+    fore, aft = [own], [own]
+    for _ in range(1, nz // 2):
+        fore.append(hop(fore[-1], pairs))
+        aft.append(hop(aft[-1], back))
+    mid = full_width // 2
+    far = [hop(fore[-1][:, :mid], pairs), hop(aft[-1][:, mid:], back)]
+    parts, steps = [own], [0]
+    for k in range(1, nz // 2):
+        parts += [fore[k], aft[k]]
+        steps += [k, nz - k]
+    parts.append(jnp.concatenate(far, axis=1))
+    steps.append(nz // 2)
     half = nz // 2
 
     late = [(parts[i][:1, :1] * 0).reshape(1, 1) for i in (2, 4)]
@@ -84,16 +97,15 @@
     x_half = []
     for h in range(2):
         rows = jnp.concatenate(parts[h * half : (h + 1) * half], axis=0)
-        x_half.append(
-            rows.reshape(half, 2 * capacity, full_width)[:, :capacity].reshape(half * capacity, full_width)
-        )
+        x_rows = rows.reshape(half, 2 * capacity, full_width)[:, :capacity]
+        x_half.append(x_rows.reshape(half * capacity, full_width))
         pre = dot_nt(weights, rows).reshape(nx, 3 * hid, -1)
         gate_pre, up_pre = pre[:, :hid], pre[:, hid : 2 * hid]
         hidden_grad = jnp.roll(pre[:, 2 * hid :], -capacity, axis=2)
         gate_grad = (hidden_grad * up_pre * silu_slope(gate_pre)).astype(BF16).reshape(group, -1)
-        arrival = h * half + column // (2 * capacity)
+        went = jnp.repeat(jnp.array(steps[h * half : (h + 1) * half], jnp.int32), 2 * capacity)
         within = column % (2 * capacity)
-        target = jnp.where(within < capacity, ((place - arrival + nz) % nz) * capacity + within, -1)
+        target = jnp.where(within < capacity, ((place - went + nz) % nz) * capacity + within, -1)
         slot_perm = (target[:, None] == slot[None, :]).astype(BF16)
         sorted_f32 = sorted_f32 + jnp.dot(gate_grad, slot_perm, preferred_element_type=F32)
     g_packed = jnp.dot(unit_perm, sorted_f32.astype(BF16), preferred_element_type=F32).astype(BF16)
@@ -110,10 +122,11 @@
     for j in range(nx):
         theirs = spread[:, j * hid : (j + 1) * hid].reshape(nz * hid, lanes)
         both_j = jnp.concatenate([theirs, tails], axis=1)
-        cols.append(dot_nt(jnp.concatenate([first, lasts[j]], axis=1), both_j).astype(BF16))
+        sums = dot_nt(jnp.concatenate([first, lasts[j]], axis=1), both_j) / float(slot_count)
+        cols.append(sums.astype(BF16))
     part_sent = jnp.concatenate(cols, axis=1).reshape(nx, hid, nx * nz * hid)
     part = lax.all_to_all(part_sent, "x", split_axis=0, concat_axis=0, tiled=True)
-    grad_rows = jnp.sum(part.astype(F32), axis=0) / float(slot_count)
+    grad_rows = jnp.sum(part.astype(F32), axis=0)
 
     strip_width = full_width // (nx * nz)
     input_rows = 0.0

time: 236 us -> 200 us (0.85)
  the two profiles are of different devices: /device:TPU:8 before, /device:TPU:40 now
where the time goes in v3:
time: 200 us; the launch traced here: 199 us
  starting transfers between devices  88.7 us (44%)
  waiting for transfers between devices  62 us (31%)
  other arithmetic  16.1 us (8%)
  matrix products  14.9 us (7%)
  local copies, waits for them, and re-layouts  13.1 us (7%)
  between operations  3.84 us (2%)
    ppermute x9, starting transfers between devices, swap_x(): return lax.ppermute(v, 'x', [(i, i ^ k) for i in range(nx)])  30.8 us
    ppermute x8, starting transfers between devices, hop(): return lax.ppermute(v, 'zl', way)  29.8 us
    all_to_all x1, waiting for transfers between devices, body(): lax.all_to_all(packed, ('y', 'zh', 'c'), split_axis=0, concat_axis=0, til...  22.7 us
    ppermute x8, waiting for transfers between devices, hop(): return lax.ppermute(v, 'zl', way)  19.2 us
    all_to_all x1, starting transfers between devices, body(): lax.all_to_all(packed, ('y', 'zh', 'c'), split_axis=0, concat_axis=0, til...  17.3 us
    ppermute x9, waiting for transfers between devices, swap_x(): return lax.ppermute(v, 'x', [(i, i ^ k) for i in range(nx)])  11.4 us
    all_to_all x1, waiting for transfers between devices, body(): lax.all_to_all(spread, 'zl', split_axis=0, concat_axis=0, tiled=True)  8.66 us
    reshape x2, matrix products, body(): pre = dot_nt(weights, rows).reshape(nx, 3 * hid, -1)  7.52 us
  transfers between devices with their start and end apart: 20, of which 8 were waited for; matrix products, arithmetic and copies ran while one was open for 20% of the time, Pallas kernels for 0%

profile of v3, /device:TPU:40, one launch (start us, length us, event | category | flops | bytes accessed | tf_op | source)
XLA Modules:
  0.0 198.7 jit_solution(8770868681845137304)
XLA Ops:
  0.7 2.4 %pad_maximum_fusion.2 = bf16[144,4096]{1,0:T(8,128)(2,1)} fusion(bf16[48,4096]{1,0:T(8,128)(2,1)} %bitcast.52, bf16[48,4096]{1,0:T(8,128)(2,1)} %bitcast.51, bf16[48,4096]{1,0:T(8,128)(2,1)} %bitcast.50), kind=kLoop, calls=%fused_computation.10 | loop fusion | flops 3538944 | bytes 2359296 | tf_op jit(solution)/shard_map/concatenate | solution.py:55
  3.1 3.4 %collective-permute-start.3 = (bf16[144,4096]{1,0:T(8,128)(2,1)}, bf16[144,4096]{1,0:T(8,128)(2,1)}, u32[]{:S(2)}, u32[]{:S(2)}) collective-permute-start(bf16[144,4096]{1,0:T(8,128)(2,1)} %pad_maximum_fusion.2), channel_id=1, source_target_pairs={{0,128},{128,0},{256,384},{384,256},{1,129},{129,1},{257,385},{385... | collective-permute-start | bytes 3538952 | tf_op jit(solution)/shard_map/ppermute | solution.py:53
  6.5 4.0 %collective-permute-start.4 = (bf16[144,4096]{1,0:T(8,128)(2,1)}, bf16[144,4096]{1,0:T(8,128)(2,1)}, u32[]{:S(2)}, u32[]{:S(2)}) collective-permute-start(bf16[144,4096]{1,0:T(8,128)(2,1)} %pad_maximum_fusion.2), channel_id=1, source_target_pairs={{0,384},{128,256},{256,128},{384,0},{1,385},{129,257},{257,129},{3... | collective-permute-start | bytes 3538952 | tf_op jit(solution)/shard_map/ppermute | solution.py:53
  10.5 2.6 %collective-permute-start.5 = (bf16[144,4096]{1,0:T(8,128)(2,1)}, bf16[144,4096]{1,0:T(8,128)(2,1)S(1)}, u32[]{:S(2)}, u32[]{:S(2)}) collective-permute-start(bf16[144,4096]{1,0:T(8,128)(2,1)} %pad_maximum_fusion.2), channel_id=1, source_target_pairs={{0,256},{128,384},{256,0},{384,128},{1,257},{129,385},{257,1},{385... | collective-permute-start | bytes 3538952 | tf_op jit(solution)/shard_map/ppermute | solution.py:53
  13.1 0.7 fusion.39
  13.9 0.6 reduce-window.6
  14.5 0.2 slice_reduce_fusion
  14.9 1.0 multiply_convert_fusion
  15.9 1.1 convolution_convert_fusion
  16.9 17.3 %all-to-all-start = ((bf16[16,40,256]{2,1,0:T(8,128)(2,1)}), bf16[16,40,256]{2,1,0:T(8,128)(2,1)S(1)}, u32[]{:S(2)}, u32[]{:S(2)}) async-start(bf16[16,40,256]{2,1,0:T(8,128)(2,1)} %bitcast.1), calls=%async_computation | async-start | bytes 655360 | tf_op jit(solution)/shard_map/all_to_all | solution.py:49
  34.2 0.8 constant_dynamic-update-slice_fusion.7
  35.0 0.8 constant_dynamic-update-slice_fusion.6
  36.2 0.8 constant_dynamic-update-slice_fusion.5
  37.0 22.7 %all-to-all-done = bf16[16,40,256]{2,1,0:T(8,128)(2,1)S(1)} async-done(((bf16[16,40,256]{2,1,0:T(8,128)(2,1)}), bf16[16,40,256]{2,1,0:T(8,128)(2,1)S(1)}, u32[]{:S(2)}, u32[]{:S(2)}) %all-to-all-start) | async-done | bytes 327712 | tf_op jit(solution)/shard_map/all_to_all | solution.py:49
  59.7 1.9 collective-permute-start.1
  61.7 3.9 %collective-permute-start = (bf16[40,4096]{1,0:T(8,128)(2,1)S(1)}, bf16[40,4096]{1,0:T(8,128)(2,1)S(1)}, u32[]{:S(2)}, u32[]{:S(2)}) collective-permute-start(bf16[40,4096]{1,0:T(8,128)(2,1)S(1)} %bitcast.55), channel_id=1, source_target_pairs={{0,32},{32,64},{64,96},{96,112},{112,80},{80,48},{48,16},{16,0},{1... | collective-permute-start | bytes 983048 | tf_op jit(solution)/shard_map/ppermute | solution.py:63
  65.6 6.6 %collective-permute-done.1 = bf16[40,4096]{1,0:T(8,128)(2,1)S(1)} collective-permute-done((bf16[40,4096]{1,0:T(8,128)(2,1)S(1)}, bf16[40,4096]{1,0:T(8,128)(2,1)S(1)}, u32[]{:S(2)}, u32[]{:S(2)}) %collective-permute-start.1) | collective-permute-done | bytes 327712 | tf_op jit(solution)/shard_map/ppermute | solution.py:63
  72.2 0.5 slice.146
  73.4 2.9 %collective-permute-start.6 = (bf16[40,4096]{1,0:T(8,128)(2,1)S(1)}, bf16[40,4096]{1,0:T(8,128)(2,1)}, u32[]{:S(2)}, u32[]{:S(2)}) collective-permute-start(bf16[40,4096]{1,0:T(8,128)(2,1)S(1)} %collective-permute-done.1), channel_id=1, source_target_pairs={{32,0},{64,32},{96,64},{112,96},{80,112},{48,80},{16,48},{0,16},{3... | collective-permute-start | bytes 983048 | tf_op jit(solution)/shard_map/ppermute | solution.py:63
  76.3 3.8 %collective-permute-done = bf16[40,4096]{1,0:T(8,128)(2,1)S(1)} collective-permute-done((bf16[40,4096]{1,0:T(8,128)(2,1)S(1)}, bf16[40,4096]{1,0:T(8,128)(2,1)S(1)}, u32[]{:S(2)}, u32[]{:S(2)}) %collective-permute-start) | collective-permute-done | bytes 327712 | tf_op jit(solution)/shard_map/ppermute | solution.py:63
  80.1 1.9 collective-permute-start.2
  82.0 2.5 %add_dynamic-update-slice_fusion.1 = bf16[576,4096]{1,0:T(8,128)(2,1)} fusion(bf16[576,4096]{1,0:T(8,128)(2,1)} %constant_dynamic-update-slice_fusion.5, bf16[144,4096]{1,0:T(8,128)(2,1)} %collective-permute-done.3, bf16[]{:T(256)} %bitcast.7), kind=kLoop, calls=%fused_computation.13 | loop fusion | flops 2359296 | bytes 2359808
  84.5 2.4 %constant_dynamic-update-slice_fusion.4 = bf16[576,4096]{1,0:T(8,128)(2,1)} fusion(bf16[576,4096]{1,0:T(8,128)(2,1)} %add_dynamic-update-slice_fusion.1, bf16[144,4096]{1,0:T(8,128)(2,1)} %collective-permute-done.4), kind=kLoop, calls=%fused_computation.69 | loop fusion | bytes 2359296
  87.0 1.2 slice.147
  88.9 5.8 %collective-permute-start.8 = (bf16[40,4096]{1,0:T(8,128)(2,1)}, bf16[40,4096]{1,0:T(8,128)(2,1)S(1)}, u32[]{:S(2)}, u32[]{:S(2)}) collective-permute-start(bf16[40,4096]{1,0:T(8,128)(2,1)} %collective-permute-done.6), channel_id=1, source_target_pairs={{32,0},{64,32},{96,64},{112,96},{80,112},{48,80},{16,48},{0,16},{3... | collective-permute-start | bytes 983048 | tf_op jit(solution)/shard_map/ppermute | solution.py:63
  94.7 0.7 collective-permute-done.2
  95.4 1.9 collective-permute-start.7
  97.3 1.0 constant_dynamic-update-slice_fusion
  98.3 1.3 add_dynamic-update-slice_fusion
  99.6 3.7 %fusion.81 = f32[576,160]{1,0:T(8,128)S(1)} fusion(bf16[576,4096]{1,0:T(8,128)(2,1)} %add_dynamic-update-slice_fusion, bf16[160,4096]{1,0:T(8,128)(2,1)S(1)} %constant_dynamic-update-slice_fusion), kind=kOutput, calls=%fused_computation.159 | convolution fusion | flops 754974720 | bytes 6397952 | tf_op jit(solution)/shard_map/reshape | solution.py:102
  103.6 3.3 %collective-permute-start.11 = (bf16[80,4096]{1,0:T(8,128)(2,1)S(1)}, bf16[80,4096]{1,0:T(8,128)(2,1)}, u32[]{:S(2)}, u32[]{:S(2)}) collective-permute-start(bf16[80,4096]{1,0:T(8,128)(2,1)S(1)} %reshape.214), channel_id=1, source_target_pairs={{0,128},{128,0},{256,384},{384,256},{1,129},{129,1},{257,385},{385... | collective-permute-start | bytes 1966088 | tf_op jit(solution)/shard_map/ppermute | solution.py:53
  106.9 4.6 %collective-permute-start.12 = (bf16[80,4096]{1,0:T(8,128)(2,1)S(1)}, bf16[80,4096]{1,0:T(8,128)(2,1)}, u32[]{:S(2)}, u32[]{:S(2)}) collective-permute-start(bf16[80,4096]{1,0:T(8,128)(2,1)S(1)} %reshape.214), channel_id=1, source_target_pairs={{0,256},{128,384},{256,0},{384,128},{1,257},{129,385},{257,1},{385... | collective-permute-start | bytes 1966088 | tf_op jit(solution)/shard_map/ppermute | solution.py:53
  111.6 2.5 %collective-permute-start.13 = (bf16[80,4096]{1,0:T(8,128)(2,1)S(1)}, bf16[80,4096]{1,0:T(8,128)(2,1)}, u32[]{:S(2)}, u32[]{:S(2)}) collective-permute-start(bf16[80,4096]{1,0:T(8,128)(2,1)S(1)} %reshape.214), channel_id=1, source_target_pairs={{0,384},{128,256},{256,128},{384,0},{1,385},{129,257},{257,129},{3... | collective-permute-start | bytes 1966088 | tf_op jit(solution)/shard_map/ppermute | solution.py:53
  114.2 9.4 %collective-permute-start.10 = (bf16[40,2048]{1,0:T(8,128)(2,1)S(1)}, bf16[40,2048]{1,0:T(8,128)(2,1)S(1)}, u32[]{:S(2)}, u32[]{:S(2)}) collective-permute-start(bf16[40,2048]{1,0:T(8,128)(2,1)S(1)} %slice.153), channel_id=1, source_target_pairs={{32,0},{64,32},{96,64},{112,96},{80,112},{48,80},{16,48},{0,16},{3... | collective-permute-start | bytes 491528 | tf_op jit(solution)/shard_map/ppermute | solution.py:63
  123.7 1.9 collective-permute-start.9
  125.6 0.3 fusion.10
  126.0 0.5 collective-permute-done.10
  126.5 7.6 %collective-permute-done.9 = bf16[40,2048]{1,0:T(8,128)(2,1)S(1)} collective-permute-done((bf16[40,2048]{1,0:T(8,128)(2,1)S(1)}, bf16[40,2048]{1,0:T(8,128)(2,1)S(1)}, u32[]{:S(2)}, u32[]{:S(2)}) %collective-permute-start.9) | collective-permute-done | bytes 163872 | tf_op jit(solution)/shard_map/ppermute | solution.py:63
  134.1 3.8 %fusion.78 = f32[576,160]{1,0:T(8,128)S(1)} fusion(bf16[576,4096]{1,0:T(8,128)(2,1)} %add_dynamic-update-slice_fusion, bf16[40,2048]{1,0:T(8,128)(2,1)S(1)} %collective-permute-done.10, bf16[40,2048]{1,0:T(8,128)(2,1)S(1)} %collective-permute-done.9, bf16[40,4096]{1,0:T(8,128)(2,1)S(1)} %collective-permute-done.8, ...), kind=kOutput, calls=%fused_computation.156 | convolution fusion | flops 761528320 | bytes 6397952 | tf_op jit(solution)/shard_map/reshape | solution.py:102
  138.2 0.5 convolution_convert_fusion.1
  138.7 0.7 fusion.80
  139.4 0.5 slice.158
  140.0 0.8 broadcast_in_dim.45
  140.8 6.7 %all-to-all-start.1 = ((bf16[8,240,128]{2,1,0:T(8,128)(2,1)}), bf16[8,240,128]{2,1,0:T(8,128)(2,1)}, u32[]{:S(2)}, u32[]{:S(2)}) async-start(bf16[8,240,128]{2,1,0:T(8,128)(2,1)} %broadcast_in_dim.45), calls=%async_computation.1 | async-start | bytes 983040 | tf_op jit(solution)/shard_map/all_to_all | solution.py:118
  147.5 1.1 maximum_maximum_fusion
  148.7 0.1 reshape.220
  148.8 2.1 %collective-permute-start.14 = (bf16[80,4096]{1,0:T(8,128)(2,1)S(1)}, bf16[80,4096]{1,0:T(8,128)(2,1)}, u32[]{:S(2)}, u32[]{:S(2)}) collective-permute-start(bf16[80,4096]{1,0:T(8,128)(2,1)S(1)} %reshape.220), channel_id=1, source_target_pairs={{0,128},{128,0},{256,384},{384,256},{1,129},{129,1},{257,385},{385... | collective-permute-start | bytes 1966088 | tf_op jit(solution)/shard_map/ppermute | solution.py:53
  150.9 5.8 %collective-permute-start.15 = (bf16[80,4096]{1,0:T(8,128)(2,1)S(1)}, bf16[80,4096]{1,0:T(8,128)(2,1)}, u32[]{:S(2)}, u32[]{:S(2)}) collective-permute-start(bf16[80,4096]{1,0:T(8,128)(2,1)S(1)} %reshape.220), channel_id=1, source_target_pairs={{0,256},{128,384},{256,0},{384,128},{1,257},{129,385},{257,1},{385... | collective-permute-start | bytes 1966088 | tf_op jit(solution)/shard_map/ppermute | solution.py:53
  157.4 2.5 %collective-permute-start.16 = (bf16[80,4096]{1,0:T(8,128)(2,1)S(1)}, bf16[80,4096]{1,0:T(8,128)(2,1)}, u32[]{:S(2)}, u32[]{:S(2)}) collective-permute-start(bf16[80,4096]{1,0:T(8,128)(2,1)S(1)} %reshape.220), channel_id=1, source_target_pairs={{0,384},{128,256},{256,128},{384,0},{1,385},{129,257},{257,129},{3... | collective-permute-start | bytes 1966088 | tf_op jit(solution)/shard_map/ppermute | solution.py:53
  160.0 1.6 pad_maximum_fusion
  161.6 8.7 %all-to-all-done.1 = bf16[8,240,128]{2,1,0:T(8,128)(2,1)} async-done(((bf16[8,240,128]{2,1,0:T(8,128)(2,1)}), bf16[8,240,128]{2,1,0:T(8,128)(2,1)}, u32[]{:S(2)}, u32[]{:S(2)}) %all-to-all-start.1) | async-done | bytes 491552 | tf_op jit(solution)/shard_map/all_to_all | solution.py:118
  170.3 1.1 fusion.79
  171.4 0.2 fusion.3
  171.6 1.1 fusion.4
  172.7 1.1 fusion.5
  173.8 0.2 fusion.6
  174.0 0.9 pad_maximum_fusion.3
  174.9 4.1 %all-to-all-start.2 = ((bf16[4,48,1536]{2,1,0:T(8,128)(2,1)}), bf16[4,48,1536]{2,1,0:T(8,128)(2,1)}, u32[]{:S(2)}, u32[]{:S(2)}) async-start(bf16[4,48,1536]{2,1,0:T(8,128)(2,1)} %bitcast.49), calls=%async_computation.2 | async-start | bytes 1179648 | tf_op jit(solution)/shard_map/all_to_all | solution.py:128
  179.1 1.2 slice.165
  181.0 11.4 %collective-permute-done.16 = bf16[80,4096]{1,0:T(8,128)(2,1)} collective-permute-done((bf16[80,4096]{1,0:T(8,128)(2,1)S(1)}, bf16[80,4096]{1,0:T(8,128)(2,1)}, u32[]{:S(2)}, u32[]{:S(2)}) %collective-permute-start.16) | collective-permute-done | bytes 655392 | tf_op jit(solution)/shard_map/ppermute | solution.py:53
  192.4 1.6 pad_maximum_fusion.1
  194.0 0.8 fusion.34
  194.7 2.1 %fusion.1 = f32[1,128,4096]{2,1,0:T(8,128)} fusion(f32[128,4096]{1,0:T(8,128)S(1)} %fusion.34, bf16[320,4096]{1,0:T(8,128)(2,1)S(1)} %pad_maximum_fusion, s32[]{:T(128)S(6)} %select_n.176), kind=kOutput, calls=%fused_computation.2 | convolution fusion | flops 336592896 | bytes 6897668 | tf_op jit(solution)/shard_map/dot_general | solution.py:21
  196.8 1.9 convert_reduce_fusion
  (71 shorter events, 1.6 us)
Async XLA Ops:
  0.6 33.6 %copy-start = (bf16[1,48,4096]{2,1,0:T(8,128)(2,1)S(1)}, bf16[1,48,4096]{2,1,0:T(8,128)(2,1)}, u32[]{:S(2)}) copy-start(bf16[1,48,4096]{2,1,0:T(8,128)(2,1)} %param.13) | copy-start | bytes 1179652
  0.6 34.4 %copy-start.1 = (bf16[1,48,4096]{2,1,0:T(8,128)(2,1)S(1)}, bf16[1,48,4096]{2,1,0:T(8,128)(2,1)}, u32[]{:S(2)}) copy-start(bf16[1,48,4096]{2,1,0:T(8,128)(2,1)} %param.14) | copy-start | bytes 1179652
  0.7 15.2 %copy-start.10 = (bf16[160,256]{1,0:T(8,128)(2,1)S(1)}, bf16[160,256]{1,0:T(8,128)(2,1)}, u32[]{:S(2)}) copy-start(bf16[160,256]{1,0:T(8,128)(2,1)} %param.9) | copy-start | bytes 245764
  0.7 35.1 %copy-start.8 = (s32[4]{0:T(128)S(1)}, s32[4]{0:T(128)}, u32[]{:S(2)}) copy-start(s32[4]{0:T(128)} %constant.189) | copy-start | bytes 52
  0.7 35.1 %copy-start.9 = (s32[4]{0:T(128)S(1)}, s32[4]{0:T(128)}, u32[]{:S(2)}) copy-start(s32[4]{0:T(128)} %constant.190) | copy-start | bytes 52
  0.7 35.5 %copy-start.2 = (bf16[1,48,4096]{2,1,0:T(8,128)(2,1)S(1)}, bf16[1,48,4096]{2,1,0:T(8,128)(2,1)}, u32[]{:S(2)}) copy-start(bf16[1,48,4096]{2,1,0:T(8,128)(2,1)} %param.15) | copy-start | bytes 1179652
  3.1 78.9 %collective-permute-start.3 = (bf16[144,4096]{1,0:T(8,128)(2,1)}, bf16[144,4096]{1,0:T(8,128)(2,1)}, u32[]{:S(2)}, u32[]{:S(2)}) collective-permute-start(bf16[144,4096]{1,0:T(8,128)(2,1)} %pad_maximum_fusion.2), channel_id=1, source_target_pairs={{0,128},{128,0},{256,384},{384,256},{1,129},{129,1},{257,385},{385... | collective-permute-start | bytes 3538952 | tf_op jit(solution)/shard_map/ppermute | solution.py:53
  6.5 78.0 %collective-permute-start.4 = (bf16[144,4096]{1,0:T(8,128)(2,1)}, bf16[144,4096]{1,0:T(8,128)(2,1)}, u32[]{:S(2)}, u32[]{:S(2)}) collective-permute-start(bf16[144,4096]{1,0:T(8,128)(2,1)} %pad_maximum_fusion.2), channel_id=1, source_target_pairs={{0,384},{128,256},{256,128},{384,0},{1,385},{129,257},{257,129},{3... | collective-permute-start | bytes 3538952 | tf_op jit(solution)/shard_map/ppermute | solution.py:53
  10.5 87.8 %collective-permute-start.5 = (bf16[144,4096]{1,0:T(8,128)(2,1)}, bf16[144,4096]{1,0:T(8,128)(2,1)S(1)}, u32[]{:S(2)}, u32[]{:S(2)}) collective-permute-start(bf16[144,4096]{1,0:T(8,128)(2,1)} %pad_maximum_fusion.2), channel_id=1, source_target_pairs={{0,256},{128,384},{256,0},{384,128},{1,257},{129,385},{257,1},{385... | collective-permute-start | bytes 3538952 | tf_op jit(solution)/shard_map/ppermute | solution.py:53
  16.9 42.8 %all-to-all-start = ((bf16[16,40,256]{2,1,0:T(8,128)(2,1)}), bf16[16,40,256]{2,1,0:T(8,128)(2,1)S(1)}, u32[]{:S(2)}, u32[]{:S(2)}) async-start(bf16[16,40,256]{2,1,0:T(8,128)(2,1)} %bitcast.1), calls=%async_computation | async-start | bytes 655360 | tf_op jit(solution)/shard_map/all_to_all | solution.py:49
  59.7 12.5 %collective-permute-start.1 = (bf16[40,4096]{1,0:T(8,128)(2,1)S(1)}, bf16[40,4096]{1,0:T(8,128)(2,1)S(1)}, u32[]{:S(2)}, u32[]{:S(2)}) collective-permute-start(bf16[40,4096]{1,0:T(8,128)(2,1)S(1)} %bitcast.54), channel_id=1, source_target_pairs={{32,0},{64,32},{96,64},{112,96},{80,112},{48,80},{16,48},{0,16},{3... | collective-permute-start | bytes 983048 | tf_op jit(solution)/shard_map/ppermute | solution.py:63
  61.7 18.4 %collective-permute-start = (bf16[40,4096]{1,0:T(8,128)(2,1)S(1)}, bf16[40,4096]{1,0:T(8,128)(2,1)S(1)}, u32[]{:S(2)}, u32[]{:S(2)}) collective-permute-start(bf16[40,4096]{1,0:T(8,128)(2,1)S(1)} %bitcast.55), channel_id=1, source_target_pairs={{0,32},{32,64},{64,96},{96,112},{112,80},{80,48},{48,16},{16,0},{1... | collective-permute-start | bytes 983048 | tf_op jit(solution)/shard_map/ppermute | solution.py:63
  73.4 13.6 %collective-permute-start.6 = (bf16[40,4096]{1,0:T(8,128)(2,1)S(1)}, bf16[40,4096]{1,0:T(8,128)(2,1)}, u32[]{:S(2)}, u32[]{:S(2)}) collective-permute-start(bf16[40,4096]{1,0:T(8,128)(2,1)S(1)} %collective-permute-done.1), channel_id=1, source_target_pairs={{32,0},{64,32},{96,64},{112,96},{80,112},{48,80},{16,48},{0,16},{3... | collective-permute-start | bytes 983048 | tf_op jit(solution)/shard_map/ppermute | solution.py:63
  80.1 15.3 %collective-permute-start.2 = (bf16[40,4096]{1,0:T(8,128)(2,1)S(1)}, bf16[40,4096]{1,0:T(8,128)(2,1)}, u32[]{:S(2)}, u32[]{:S(2)}) collective-permute-start(bf16[40,4096]{1,0:T(8,128)(2,1)S(1)} %collective-permute-done), channel_id=1, source_target_pairs={{0,32},{32,64},{64,96},{96,112},{112,80},{80,48},{48,16},{16,0},{1... | collective-permute-start | bytes 983048 | tf_op jit(solution)/shard_map/ppermute | solution.py:63
  88.9 25.4 %collective-permute-start.8 = (bf16[40,4096]{1,0:T(8,128)(2,1)}, bf16[40,4096]{1,0:T(8,128)(2,1)S(1)}, u32[]{:S(2)}, u32[]{:S(2)}) collective-permute-start(bf16[40,4096]{1,0:T(8,128)(2,1)} %collective-permute-done.6), channel_id=1, source_target_pairs={{32,0},{64,32},{96,64},{112,96},{80,112},{48,80},{16,48},{0,16},{3... | collective-permute-start | bytes 983048 | tf_op jit(solution)/shard_map/ppermute | solution.py:63
  95.4 28.3 %collective-permute-start.7 = (bf16[40,4096]{1,0:T(8,128)(2,1)}, bf16[40,4096]{1,0:T(8,128)(2,1)S(1)}, u32[]{:S(2)}, u32[]{:S(2)}) collective-permute-start(bf16[40,4096]{1,0:T(8,128)(2,1)} %collective-permute-done.2), channel_id=1, source_target_pairs={{0,32},{32,64},{64,96},{96,112},{112,80},{80,48},{48,16},{16,0},{1... | collective-permute-start | bytes 983048 | tf_op jit(solution)/shard_map/ppermute | solution.py:63
  103.6 53.8 %collective-permute-start.11 = (bf16[80,4096]{1,0:T(8,128)(2,1)S(1)}, bf16[80,4096]{1,0:T(8,128)(2,1)}, u32[]{:S(2)}, u32[]{:S(2)}) collective-permute-start(bf16[80,4096]{1,0:T(8,128)(2,1)S(1)} %reshape.214), channel_id=1, source_target_pairs={{0,128},{128,0},{256,384},{384,256},{1,129},{129,1},{257,385},{385... | collective-permute-start | bytes 1966088 | tf_op jit(solution)/shard_map/ppermute | solution.py:53
  106.9 53.1 %collective-permute-start.12 = (bf16[80,4096]{1,0:T(8,128)(2,1)S(1)}, bf16[80,4096]{1,0:T(8,128)(2,1)}, u32[]{:S(2)}, u32[]{:S(2)}) collective-permute-start(bf16[80,4096]{1,0:T(8,128)(2,1)S(1)} %reshape.214), channel_id=1, source_target_pairs={{0,256},{128,384},{256,0},{384,128},{1,257},{129,385},{257,1},{385... | collective-permute-start | bytes 1966088 | tf_op jit(solution)/shard_map/ppermute | solution.py:53
  111.6 48.4 %collective-permute-start.13 = (bf16[80,4096]{1,0:T(8,128)(2,1)S(1)}, bf16[80,4096]{1,0:T(8,128)(2,1)}, u32[]{:S(2)}, u32[]{:S(2)}) collective-permute-start(bf16[80,4096]{1,0:T(8,128)(2,1)S(1)} %reshape.214), channel_id=1, source_target_pairs={{0,384},{128,256},{256,128},{384,0},{1,385},{129,257},{257,129},{3... | collective-permute-start | bytes 1966088 | tf_op jit(solution)/shard_map/ppermute | solution.py:53
  114.2 12.2 %collective-permute-start.10 = (bf16[40,2048]{1,0:T(8,128)(2,1)S(1)}, bf16[40,2048]{1,0:T(8,128)(2,1)S(1)}, u32[]{:S(2)}, u32[]{:S(2)}) collective-permute-start(bf16[40,2048]{1,0:T(8,128)(2,1)S(1)} %slice.153), channel_id=1, source_target_pairs={{32,0},{64,32},{96,64},{112,96},{80,112},{48,80},{16,48},{0,16},{3... | collective-permute-start | bytes 491528 | tf_op jit(solution)/shard_map/ppermute | solution.py:63
  123.7 14.2 %copy-start.3 = (bf16[40,4096]{1,0:T(8,128)(2,1)}, bf16[40,4096]{1,0:T(8,128)(2,1)S(1)}, u32[]{:S(2)}) copy-start(bf16[40,4096]{1,0:T(8,128)(2,1)S(1)} %collective-permute-done.7) | copy-start | bytes 983044
  123.7 10.4 %collective-permute-start.9 = (bf16[40,2048]{1,0:T(8,128)(2,1)S(1)}, bf16[40,2048]{1,0:T(8,128)(2,1)S(1)}, u32[]{:S(2)}, u32[]{:S(2)}) collective-permute-start(bf16[40,2048]{1,0:T(8,128)(2,1)S(1)} %slice.152), channel_id=1, source_target_pairs={{0,32},{32,64},{64,96},{96,112},{112,80},{80,48},{48,16},{16,0},{1... | collective-permute-start | bytes 491528 | tf_op jit(solution)/shard_map/ppermute | solution.py:63
  137.9 9.6 %copy-start.4 = (bf16[40,4096]{1,0:T(8,128)(2,1)S(1)}, bf16[40,4096]{1,0:T(8,128)(2,1)}, u32[]{:S(2)}) copy-start(bf16[40,4096]{1,0:T(8,128)(2,1)} %copy-done.3) | copy-start | bytes 983044
  139.4 9.2 %copy-start.5 = (bf16[192,128]{1,0:T(8,128)(2,1)}, bf16[192,128]{1,0:T(8,128)(2,1)S(1)}, u32[]{:S(2)}) copy-start(bf16[192,128]{1,0:T(8,128)(2,1)S(1)} %get-tuple-element.14) | copy-start | bytes 147460
  140.8 29.5 %all-to-all-start.1 = ((bf16[8,240,128]{2,1,0:T(8,128)(2,1)}), bf16[8,240,128]{2,1,0:T(8,128)(2,1)}, u32[]{:S(2)}, u32[]{:S(2)}) async-start(bf16[8,240,128]{2,1,0:T(8,128)(2,1)} %broadcast_in_dim.45), calls=%async_computation.1 | async-start | bytes 983040 | tf_op jit(solution)/shard_map/all_to_all | solution.py:118
  148.8 32.1 %collective-permute-start.14 = (bf16[80,4096]{1,0:T(8,128)(2,1)S(1)}, bf16[80,4096]{1,0:T(8,128)(2,1)}, u32[]{:S(2)}, u32[]{:S(2)}) collective-permute-start(bf16[80,4096]{1,0:T(8,128)(2,1)S(1)} %reshape.220), channel_id=1, source_target_pairs={{0,128},{128,0},{256,384},{384,256},{1,129},{129,1},{257,385},{385... | collective-permute-start | bytes 1966088 | tf_op jit(solution)/shard_map/ppermute | solution.py:53
  150.9 30.1 %collective-permute-start.15 = (bf16[80,4096]{1,0:T(8,128)(2,1)S(1)}, bf16[80,4096]{1,0:T(8,128)(2,1)}, u32[]{:S(2)}, u32[]{:S(2)}) collective-permute-start(bf16[80,4096]{1,0:T(8,128)(2,1)S(1)} %reshape.220), channel_id=1, source_target_pairs={{0,256},{128,384},{256,0},{384,128},{1,257},{129,385},{257,1},{385... | collective-permute-start | bytes 1966088 | tf_op jit(solution)/shard_map/ppermute | solution.py:53
  157.4 34.9 %collective-permute-start.16 = (bf16[80,4096]{1,0:T(8,128)(2,1)S(1)}, bf16[80,4096]{1,0:T(8,128)(2,1)}, u32[]{:S(2)}, u32[]{:S(2)}) collective-permute-start(bf16[80,4096]{1,0:T(8,128)(2,1)S(1)} %reshape.220), channel_id=1, source_target_pairs={{0,384},{128,256},{256,128},{384,0},{1,385},{129,257},{257,129},{3... | collective-permute-start | bytes 1966088 | tf_op jit(solution)/shard_map/ppermute | solution.py:53
  170.3 3.5 %copy-start.6 = (bf16[192,128]{1,0:T(8,128)(2,1)S(1)}, bf16[192,128]{1,0:T(8,128)(2,1)}, u32[]{:S(2)}) copy-start(bf16[192,128]{1,0:T(8,128)(2,1)} %copy-done.5) | copy-start | bytes 147460
  170.3 3.5 %copy-start.7 = (bf16[192,128]{1,0:T(8,128)(2,1)S(1)}, bf16[192,128]{1,0:T(8,128)(2,1)}, u32[]{:S(2)}) copy-start(bf16[192,128]{1,0:T(8,128)(2,1)} %get-tuple-element.12) | copy-start | bytes 147460
  174.9 21.9 %all-to-all-start.2 = ((bf16[4,48,1536]{2,1,0:T(8,128)(2,1)}), bf16[4,48,1536]{2,1,0:T(8,128)(2,1)}, u32[]{:S(2)}, u32[]{:S(2)}) async-start(bf16[4,48,1536]{2,1,0:T(8,128)(2,1)} %bitcast.49), calls=%async_computation.2 | async-start | bytes 1179648 | tf_op jit(solution)/shard_map/all_to_all | solution.py:128

commit v4 on v3

--- a/solution.py
+++ b/solution.py
@@ -76,7 +76,10 @@
     steps.append(nz // 2)
     half = nz // 2
 
-    late = [(parts[i][:1, :1] * 0).reshape(1, 1) for i in (2, 4)]
+    def anchor(v):
+        return v[:1, :1] * 0
+
+    late = [anchor(parts[2]), anchor(parts[4])]
     weights = jnp.concatenate([w_own, w_others[0] + late[0], w_others[2], w_others[1] + late[1]], axis=0)
 
     group = nx * hid
@@ -131,7 +134,7 @@
     strip_width = full_width // (nx * nz)
     input_rows = 0.0
     for name, piece in zip(("xa", "xb"), x_half):
-        own_piece = piece + (later if name == "xb" else (sent[:1, :1] * 0))
+        own_piece = piece + (later if name == "xb" else anchor(sent))
         gathered = [own_piece] + [swap_x(piece, k) for k in range(1, nx)]
         rows = jnp.concatenate(gathered, axis=0)
         strip = lax.dynamic_slice_in_dim(rows, (xi * nz + zi) * strip_width, strip_width, 1)

time: 200 us -> 200 us (level)
  no operation moved by 1% of the time
where the time goes in v4:
time: 200 us; the launch traced here: 199 us
  starting transfers between devices  88.7 us (44%)
  waiting for transfers between devices  62 us (31%)
  other arithmetic  16.1 us (8%)
  matrix products  14.9 us (7%)
  local copies, waits for them, and re-layouts  13.1 us (7%)
  between operations  3.84 us (2%)
    ppermute x9, starting transfers between devices, swap_x(): return lax.ppermute(v, 'x', [(i, i ^ k) for i in range(nx)])  30.8 us
    ppermute x8, starting transfers between devices, hop(): return lax.ppermute(v, 'zl', way)  29.8 us
    all_to_all x1, waiting for transfers between devices, body(): lax.all_to_all(packed, ('y', 'zh', 'c'), split_axis=0, concat_axis=0, til...  22.7 us
    ppermute x8, waiting for transfers between devices, hop(): return lax.ppermute(v, 'zl', way)  19.2 us
    all_to_all x1, starting transfers between devices, body(): lax.all_to_all(packed, ('y', 'zh', 'c'), split_axis=0, concat_axis=0, til...  17.3 us
    ppermute x9, waiting for transfers between devices, swap_x(): return lax.ppermute(v, 'x', [(i, i ^ k) for i in range(nx)])  11.4 us
    all_to_all x1, waiting for transfers between devices, body(): lax.all_to_all(spread, 'zl', split_axis=0, concat_axis=0, tiled=True)  8.66 us
    reshape x2, matrix products, body(): pre = dot_nt(weights, rows).reshape(nx, 3 * hid, -1)  7.52 us
  transfers between devices with their start and end apart: 20, of which 8 were waited for; matrix products, arithmetic and copies ran while one was open for 20% of the time, Pallas kernels for 0%

profile of v4, /device:TPU:40, one launch (start us, length us, event | category | flops | bytes accessed | tf_op | source)
XLA Modules:
  0.0 198.7 jit_solution(8770868681845137304)
XLA Ops:
  0.7 2.4 %pad_maximum_fusion.2 = bf16[144,4096]{1,0:T(8,128)(2,1)} fusion(bf16[48,4096]{1,0:T(8,128)(2,1)} %bitcast.52, bf16[48,4096]{1,0:T(8,128)(2,1)} %bitcast.51, bf16[48,4096]{1,0:T(8,128)(2,1)} %bitcast.50), kind=kLoop, calls=%fused_computation.10 | loop fusion | flops 3538944 | bytes 2359296 | tf_op jit(solution)/shard_map/concatenate | solution.py:55
  3.1 3.4 %collective-permute-start.3 = (bf16[144,4096]{1,0:T(8,128)(2,1)}, bf16[144,4096]{1,0:T(8,128)(2,1)}, u32[]{:S(2)}, u32[]{:S(2)}) collective-permute-start(bf16[144,4096]{1,0:T(8,128)(2,1)} %pad_maximum_fusion.2), channel_id=1, source_target_pairs={{0,128},{128,0},{256,384},{384,256},{1,129},{129,1},{257,385},{385... | collective-permute-start | bytes 3538952 | tf_op jit(solution)/shard_map/ppermute | solution.py:53
  6.5 4.0 %collective-permute-start.4 = (bf16[144,4096]{1,0:T(8,128)(2,1)}, bf16[144,4096]{1,0:T(8,128)(2,1)}, u32[]{:S(2)}, u32[]{:S(2)}) collective-permute-start(bf16[144,4096]{1,0:T(8,128)(2,1)} %pad_maximum_fusion.2), channel_id=1, source_target_pairs={{0,384},{128,256},{256,128},{384,0},{1,385},{129,257},{257,129},{3... | collective-permute-start | bytes 3538952 | tf_op jit(solution)/shard_map/ppermute | solution.py:53
  10.5 2.6 %collective-permute-start.5 = (bf16[144,4096]{1,0:T(8,128)(2,1)}, bf16[144,4096]{1,0:T(8,128)(2,1)S(1)}, u32[]{:S(2)}, u32[]{:S(2)}) collective-permute-start(bf16[144,4096]{1,0:T(8,128)(2,1)} %pad_maximum_fusion.2), channel_id=1, source_target_pairs={{0,256},{128,384},{256,0},{384,128},{1,257},{129,385},{257,1},{385... | collective-permute-start | bytes 3538952 | tf_op jit(solution)/shard_map/ppermute | solution.py:53
  13.1 0.7 fusion.39
  13.9 0.6 reduce-window.6
  14.5 0.2 slice_reduce_fusion
  14.9 1.0 multiply_convert_fusion
  15.9 1.1 convolution_convert_fusion
  16.9 17.3 %all-to-all-start = ((bf16[16,40,256]{2,1,0:T(8,128)(2,1)}), bf16[16,40,256]{2,1,0:T(8,128)(2,1)S(1)}, u32[]{:S(2)}, u32[]{:S(2)}) async-start(bf16[16,40,256]{2,1,0:T(8,128)(2,1)} %bitcast.1), calls=%async_computation | async-start | bytes 655360 | tf_op jit(solution)/shard_map/all_to_all | solution.py:49
  34.2 0.8 constant_dynamic-update-slice_fusion.7
  35.0 0.8 constant_dynamic-update-slice_fusion.6
  36.2 0.8 constant_dynamic-update-slice_fusion.5
  37.0 22.7 %all-to-all-done = bf16[16,40,256]{2,1,0:T(8,128)(2,1)S(1)} async-done(((bf16[16,40,256]{2,1,0:T(8,128)(2,1)}), bf16[16,40,256]{2,1,0:T(8,128)(2,1)S(1)}, u32[]{:S(2)}, u32[]{:S(2)}) %all-to-all-start) | async-done | bytes 327712 | tf_op jit(solution)/shard_map/all_to_all | solution.py:49
  59.7 1.9 collective-permute-start.1
  61.7 3.9 %collective-permute-start = (bf16[40,4096]{1,0:T(8,128)(2,1)S(1)}, bf16[40,4096]{1,0:T(8,128)(2,1)S(1)}, u32[]{:S(2)}, u32[]{:S(2)}) collective-permute-start(bf16[40,4096]{1,0:T(8,128)(2,1)S(1)} %bitcast.55), channel_id=1, source_target_pairs={{0,32},{32,64},{64,96},{96,112},{112,80},{80,48},{48,16},{16,0},{1... | collective-permute-start | bytes 983048 | tf_op jit(solution)/shard_map/ppermute | solution.py:63
  65.6 6.6 %collective-permute-done.1 = bf16[40,4096]{1,0:T(8,128)(2,1)S(1)} collective-permute-done((bf16[40,4096]{1,0:T(8,128)(2,1)S(1)}, bf16[40,4096]{1,0:T(8,128)(2,1)S(1)}, u32[]{:S(2)}, u32[]{:S(2)}) %collective-permute-start.1) | collective-permute-done | bytes 327712 | tf_op jit(solution)/shard_map/ppermute | solution.py:63
  72.2 0.5 slice.146
  73.4 2.9 %collective-permute-start.6 = (bf16[40,4096]{1,0:T(8,128)(2,1)S(1)}, bf16[40,4096]{1,0:T(8,128)(2,1)}, u32[]{:S(2)}, u32[]{:S(2)}) collective-permute-start(bf16[40,4096]{1,0:T(8,128)(2,1)S(1)} %collective-permute-done.1), channel_id=1, source_target_pairs={{32,0},{64,32},{96,64},{112,96},{80,112},{48,80},{16,48},{0,16},{3... | collective-permute-start | bytes 983048 | tf_op jit(solution)/shard_map/ppermute | solution.py:63
  76.3 3.8 %collective-permute-done = bf16[40,4096]{1,0:T(8,128)(2,1)S(1)} collective-permute-done((bf16[40,4096]{1,0:T(8,128)(2,1)S(1)}, bf16[40,4096]{1,0:T(8,128)(2,1)S(1)}, u32[]{:S(2)}, u32[]{:S(2)}) %collective-permute-start) | collective-permute-done | bytes 327712 | tf_op jit(solution)/shard_map/ppermute | solution.py:63
  80.1 1.9 collective-permute-start.2
  82.0 2.5 %add_dynamic-update-slice_fusion.1 = bf16[576,4096]{1,0:T(8,128)(2,1)} fusion(bf16[576,4096]{1,0:T(8,128)(2,1)} %constant_dynamic-update-slice_fusion.5, bf16[144,4096]{1,0:T(8,128)(2,1)} %collective-permute-done.3, bf16[]{:T(256)} %bitcast.7), kind=kLoop, calls=%fused_computation.13 | loop fusion | flops 2359296 | bytes 2359808
  84.5 2.4 %constant_dynamic-update-slice_fusion.4 = bf16[576,4096]{1,0:T(8,128)(2,1)} fusion(bf16[576,4096]{1,0:T(8,128)(2,1)} %add_dynamic-update-slice_fusion.1, bf16[144,4096]{1,0:T(8,128)(2,1)} %collective-permute-done.4), kind=kLoop, calls=%fused_computation.69 | loop fusion | bytes 2359296
  87.0 1.2 slice.147
  88.9 5.8 %collective-permute-start.8 = (bf16[40,4096]{1,0:T(8,128)(2,1)}, bf16[40,4096]{1,0:T(8,128)(2,1)S(1)}, u32[]{:S(2)}, u32[]{:S(2)}) collective-permute-start(bf16[40,4096]{1,0:T(8,128)(2,1)} %collective-permute-done.6), channel_id=1, source_target_pairs={{32,0},{64,32},{96,64},{112,96},{80,112},{48,80},{16,48},{0,16},{3... | collective-permute-start | bytes 983048 | tf_op jit(solution)/shard_map/ppermute | solution.py:63
  94.7 0.7 collective-permute-done.2
  95.4 1.9 collective-permute-start.7
  97.3 1.0 constant_dynamic-update-slice_fusion
  98.3 1.3 add_dynamic-update-slice_fusion
  99.6 3.7 %fusion.81 = f32[576,160]{1,0:T(8,128)S(1)} fusion(bf16[576,4096]{1,0:T(8,128)(2,1)} %add_dynamic-update-slice_fusion, bf16[160,4096]{1,0:T(8,128)(2,1)S(1)} %constant_dynamic-update-slice_fusion), kind=kOutput, calls=%fused_computation.159 | convolution fusion | flops 754974720 | bytes 6397952 | tf_op jit(solution)/shard_map/reshape | solution.py:105
  103.6 3.3 %collective-permute-start.11 = (bf16[80,4096]{1,0:T(8,128)(2,1)S(1)}, bf16[80,4096]{1,0:T(8,128)(2,1)}, u32[]{:S(2)}, u32[]{:S(2)}) collective-permute-start(bf16[80,4096]{1,0:T(8,128)(2,1)S(1)} %reshape.214), channel_id=1, source_target_pairs={{0,128},{128,0},{256,384},{384,256},{1,129},{129,1},{257,385},{385... | collective-permute-start | bytes 1966088 | tf_op jit(solution)/shard_map/ppermute | solution.py:53
  106.9 4.6 %collective-permute-start.12 = (bf16[80,4096]{1,0:T(8,128)(2,1)S(1)}, bf16[80,4096]{1,0:T(8,128)(2,1)}, u32[]{:S(2)}, u32[]{:S(2)}) collective-permute-start(bf16[80,4096]{1,0:T(8,128)(2,1)S(1)} %reshape.214), channel_id=1, source_target_pairs={{0,256},{128,384},{256,0},{384,128},{1,257},{129,385},{257,1},{385... | collective-permute-start | bytes 1966088 | tf_op jit(solution)/shard_map/ppermute | solution.py:53
  111.6 2.5 %collective-permute-start.13 = (bf16[80,4096]{1,0:T(8,128)(2,1)S(1)}, bf16[80,4096]{1,0:T(8,128)(2,1)}, u32[]{:S(2)}, u32[]{:S(2)}) collective-permute-start(bf16[80,4096]{1,0:T(8,128)(2,1)S(1)} %reshape.214), channel_id=1, source_target_pairs={{0,384},{128,256},{256,128},{384,0},{1,385},{129,257},{257,129},{3... | collective-permute-start | bytes 1966088 | tf_op jit(solution)/shard_map/ppermute | solution.py:53
  114.2 9.4 %collective-permute-start.10 = (bf16[40,2048]{1,0:T(8,128)(2,1)S(1)}, bf16[40,2048]{1,0:T(8,128)(2,1)S(1)}, u32[]{:S(2)}, u32[]{:S(2)}) collective-permute-start(bf16[40,2048]{1,0:T(8,128)(2,1)S(1)} %slice.153), channel_id=1, source_target_pairs={{32,0},{64,32},{96,64},{112,96},{80,112},{48,80},{16,48},{0,16},{3... | collective-permute-start | bytes 491528 | tf_op jit(solution)/shard_map/ppermute | solution.py:63
  123.7 1.9 collective-permute-start.9
  125.6 0.3 fusion.10
  126.0 0.5 collective-permute-done.10
  126.5 7.6 %collective-permute-done.9 = bf16[40,2048]{1,0:T(8,128)(2,1)S(1)} collective-permute-done((bf16[40,2048]{1,0:T(8,128)(2,1)S(1)}, bf16[40,2048]{1,0:T(8,128)(2,1)S(1)}, u32[]{:S(2)}, u32[]{:S(2)}) %collective-permute-start.9) | collective-permute-done | bytes 163872 | tf_op jit(solution)/shard_map/ppermute | solution.py:63
  134.1 3.8 %fusion.78 = f32[576,160]{1,0:T(8,128)S(1)} fusion(bf16[576,4096]{1,0:T(8,128)(2,1)} %add_dynamic-update-slice_fusion, bf16[40,2048]{1,0:T(8,128)(2,1)S(1)} %collective-permute-done.10, bf16[40,2048]{1,0:T(8,128)(2,1)S(1)} %collective-permute-done.9, bf16[40,4096]{1,0:T(8,128)(2,1)S(1)} %collective-permute-done.8, ...), kind=kOutput, calls=%fused_computation.156 | convolution fusion | flops 761528320 | bytes 6397952 | tf_op jit(solution)/shard_map/reshape | solution.py:105
  138.2 0.5 convolution_convert_fusion.1
  138.7 0.7 fusion.80
  139.4 0.5 slice.158
  140.0 0.8 broadcast_in_dim.45
  140.8 6.7 %all-to-all-start.1 = ((bf16[8,240,128]{2,1,0:T(8,128)(2,1)}), bf16[8,240,128]{2,1,0:T(8,128)(2,1)}, u32[]{:S(2)}, u32[]{:S(2)}) async-start(bf16[8,240,128]{2,1,0:T(8,128)(2,1)} %broadcast_in_dim.45), calls=%async_computation.1 | async-start | bytes 983040 | tf_op jit(solution)/shard_map/all_to_all | solution.py:121
  147.5 1.1 maximum_maximum_fusion
  148.7 0.1 reshape.220
  148.8 2.1 %collective-permute-start.14 = (bf16[80,4096]{1,0:T(8,128)(2,1)S(1)}, bf16[80,4096]{1,0:T(8,128)(2,1)}, u32[]{:S(2)}, u32[]{:S(2)}) collective-permute-start(bf16[80,4096]{1,0:T(8,128)(2,1)S(1)} %reshape.220), channel_id=1, source_target_pairs={{0,128},{128,0},{256,384},{384,256},{1,129},{129,1},{257,385},{385... | collective-permute-start | bytes 1966088 | tf_op jit(solution)/shard_map/ppermute | solution.py:53
  150.9 5.8 %collective-permute-start.15 = (bf16[80,4096]{1,0:T(8,128)(2,1)S(1)}, bf16[80,4096]{1,0:T(8,128)(2,1)}, u32[]{:S(2)}, u32[]{:S(2)}) collective-permute-start(bf16[80,4096]{1,0:T(8,128)(2,1)S(1)} %reshape.220), channel_id=1, source_target_pairs={{0,256},{128,384},{256,0},{384,128},{1,257},{129,385},{257,1},{385... | collective-permute-start | bytes 1966088 | tf_op jit(solution)/shard_map/ppermute | solution.py:53
  157.4 2.5 %collective-permute-start.16 = (bf16[80,4096]{1,0:T(8,128)(2,1)S(1)}, bf16[80,4096]{1,0:T(8,128)(2,1)}, u32[]{:S(2)}, u32[]{:S(2)}) collective-permute-start(bf16[80,4096]{1,0:T(8,128)(2,1)S(1)} %reshape.220), channel_id=1, source_target_pairs={{0,384},{128,256},{256,128},{384,0},{1,385},{129,257},{257,129},{3... | collective-permute-start | bytes 1966088 | tf_op jit(solution)/shard_map/ppermute | solution.py:53
  160.0 1.6 pad_maximum_fusion
  161.6 8.7 %all-to-all-done.1 = bf16[8,240,128]{2,1,0:T(8,128)(2,1)} async-done(((bf16[8,240,128]{2,1,0:T(8,128)(2,1)}), bf16[8,240,128]{2,1,0:T(8,128)(2,1)}, u32[]{:S(2)}, u32[]{:S(2)}) %all-to-all-start.1) | async-done | bytes 491552 | tf_op jit(solution)/shard_map/all_to_all | solution.py:121
  170.3 1.1 fusion.79
  171.4 0.2 fusion.3
  171.6 1.1 fusion.4
  172.7 1.1 fusion.5
  173.8 0.2 fusion.6
  174.0 0.9 pad_maximum_fusion.3
  174.9 4.1 %all-to-all-start.2 = ((bf16[4,48,1536]{2,1,0:T(8,128)(2,1)}), bf16[4,48,1536]{2,1,0:T(8,128)(2,1)}, u32[]{:S(2)}, u32[]{:S(2)}) async-start(bf16[4,48,1536]{2,1,0:T(8,128)(2,1)} %bitcast.49), calls=%async_computation.2 | async-start | bytes 1179648 | tf_op jit(solution)/shard_map/all_to_all | solution.py:131
  179.1 1.2 slice.165
  181.0 11.4 %collective-permute-done.16 = bf16[80,4096]{1,0:T(8,128)(2,1)} collective-permute-done((bf16[80,4096]{1,0:T(8,128)(2,1)S(1)}, bf16[80,4096]{1,0:T(8,128)(2,1)}, u32[]{:S(2)}, u32[]{:S(2)}) %collective-permute-start.16) | collective-permute-done | bytes 655392 | tf_op jit(solution)/shard_map/ppermute | solution.py:53
  192.4 1.6 pad_maximum_fusion.1
  194.0 0.8 fusion.34
  194.7 2.1 %fusion.1 = f32[1,128,4096]{2,1,0:T(8,128)} fusion(f32[128,4096]{1,0:T(8,128)S(1)} %fusion.34, bf16[320,4096]{1,0:T(8,128)(2,1)S(1)} %pad_maximum_fusion, s32[]{:T(128)S(6)} %select_n.176), kind=kOutput, calls=%fused_computation.2 | convolution fusion | flops 336592896 | bytes 6897668 | tf_op jit(solution)/shard_map/dot_general | solution.py:21
  196.8 1.9 convert_reduce_fusion
  (71 shorter events, 1.6 us)
Async XLA Ops:
  0.6 33.6 %copy-start = (bf16[1,48,4096]{2,1,0:T(8,128)(2,1)S(1)}, bf16[1,48,4096]{2,1,0:T(8,128)(2,1)}, u32[]{:S(2)}) copy-start(bf16[1,48,4096]{2,1,0:T(8,128)(2,1)} %param.13) | copy-start | bytes 1179652
  0.6 34.4 %copy-start.1 = (bf16[1,48,4096]{2,1,0:T(8,128)(2,1)S(1)}, bf16[1,48,4096]{2,1,0:T(8,128)(2,1)}, u32[]{:S(2)}) copy-start(bf16[1,48,4096]{2,1,0:T(8,128)(2,1)} %param.14) | copy-start | bytes 1179652
  0.7 15.2 %copy-start.10 = (bf16[160,256]{1,0:T(8,128)(2,1)S(1)}, bf16[160,256]{1,0:T(8,128)(2,1)}, u32[]{:S(2)}) copy-start(bf16[160,256]{1,0:T(8,128)(2,1)} %param.9) | copy-start | bytes 245764
  0.7 35.1 %copy-start.8 = (s32[4]{0:T(128)S(1)}, s32[4]{0:T(128)}, u32[]{:S(2)}) copy-start(s32[4]{0:T(128)} %constant.189) | copy-start | bytes 52
  0.7 35.1 %copy-start.9 = (s32[4]{0:T(128)S(1)}, s32[4]{0:T(128)}, u32[]{:S(2)}) copy-start(s32[4]{0:T(128)} %constant.190) | copy-start | bytes 52
  0.7 35.5 %copy-start.2 = (bf16[1,48,4096]{2,1,0:T(8,128)(2,1)S(1)}, bf16[1,48,4096]{2,1,0:T(8,128)(2,1)}, u32[]{:S(2)}) copy-start(bf16[1,48,4096]{2,1,0:T(8,128)(2,1)} %param.15) | copy-start | bytes 1179652
  3.1 78.9 %collective-permute-start.3 = (bf16[144,4096]{1,0:T(8,128)(2,1)}, bf16[144,4096]{1,0:T(8,128)(2,1)}, u32[]{:S(2)}, u32[]{:S(2)}) collective-permute-start(bf16[144,4096]{1,0:T(8,128)(2,1)} %pad_maximum_fusion.2), channel_id=1, source_target_pairs={{0,128},{128,0},{256,384},{384,256},{1,129},{129,1},{257,385},{385... | collective-permute-start | bytes 3538952 | tf_op jit(solution)/shard_map/ppermute | solution.py:53
  6.5 78.0 %collective-permute-start.4 = (bf16[144,4096]{1,0:T(8,128)(2,1)}, bf16[144,4096]{1,0:T(8,128)(2,1)}, u32[]{:S(2)}, u32[]{:S(2)}) collective-permute-start(bf16[144,4096]{1,0:T(8,128)(2,1)} %pad_maximum_fusion.2), channel_id=1, source_target_pairs={{0,384},{128,256},{256,128},{384,0},{1,385},{129,257},{257,129},{3... | collective-permute-start | bytes 3538952 | tf_op jit(solution)/shard_map/ppermute | solution.py:53
  10.5 87.8 %collective-permute-start.5 = (bf16[144,4096]{1,0:T(8,128)(2,1)}, bf16[144,4096]{1,0:T(8,128)(2,1)S(1)}, u32[]{:S(2)}, u32[]{:S(2)}) collective-permute-start(bf16[144,4096]{1,0:T(8,128)(2,1)} %pad_maximum_fusion.2), channel_id=1, source_target_pairs={{0,256},{128,384},{256,0},{384,128},{1,257},{129,385},{257,1},{385... | collective-permute-start | bytes 3538952 | tf_op jit(solution)/shard_map/ppermute | solution.py:53
  16.9 42.8 %all-to-all-start = ((bf16[16,40,256]{2,1,0:T(8,128)(2,1)}), bf16[16,40,256]{2,1,0:T(8,128)(2,1)S(1)}, u32[]{:S(2)}, u32[]{:S(2)}) async-start(bf16[16,40,256]{2,1,0:T(8,128)(2,1)} %bitcast.1), calls=%async_computation | async-start | bytes 655360 | tf_op jit(solution)/shard_map/all_to_all | solution.py:49
  59.7 12.5 %collective-permute-start.1 = (bf16[40,4096]{1,0:T(8,128)(2,1)S(1)}, bf16[40,4096]{1,0:T(8,128)(2,1)S(1)}, u32[]{:S(2)}, u32[]{:S(2)}) collective-permute-start(bf16[40,4096]{1,0:T(8,128)(2,1)S(1)} %bitcast.54), channel_id=1, source_target_pairs={{32,0},{64,32},{96,64},{112,96},{80,112},{48,80},{16,48},{0,16},{3... | collective-permute-start | bytes 983048 | tf_op jit(solution)/shard_map/ppermute | solution.py:63
  61.7 18.4 %collective-permute-start = (bf16[40,4096]{1,0:T(8,128)(2,1)S(1)}, bf16[40,4096]{1,0:T(8,128)(2,1)S(1)}, u32[]{:S(2)}, u32[]{:S(2)}) collective-permute-start(bf16[40,4096]{1,0:T(8,128)(2,1)S(1)} %bitcast.55), channel_id=1, source_target_pairs={{0,32},{32,64},{64,96},{96,112},{112,80},{80,48},{48,16},{16,0},{1... | collective-permute-start | bytes 983048 | tf_op jit(solution)/shard_map/ppermute | solution.py:63
  73.4 13.6 %collective-permute-start.6 = (bf16[40,4096]{1,0:T(8,128)(2,1)S(1)}, bf16[40,4096]{1,0:T(8,128)(2,1)}, u32[]{:S(2)}, u32[]{:S(2)}) collective-permute-start(bf16[40,4096]{1,0:T(8,128)(2,1)S(1)} %collective-permute-done.1), channel_id=1, source_target_pairs={{32,0},{64,32},{96,64},{112,96},{80,112},{48,80},{16,48},{0,16},{3... | collective-permute-start | bytes 983048 | tf_op jit(solution)/shard_map/ppermute | solution.py:63
  80.1 15.3 %collective-permute-start.2 = (bf16[40,4096]{1,0:T(8,128)(2,1)S(1)}, bf16[40,4096]{1,0:T(8,128)(2,1)}, u32[]{:S(2)}, u32[]{:S(2)}) collective-permute-start(bf16[40,4096]{1,0:T(8,128)(2,1)S(1)} %collective-permute-done), channel_id=1, source_target_pairs={{0,32},{32,64},{64,96},{96,112},{112,80},{80,48},{48,16},{16,0},{1... | collective-permute-start | bytes 983048 | tf_op jit(solution)/shard_map/ppermute | solution.py:63
  88.9 25.4 %collective-permute-start.8 = (bf16[40,4096]{1,0:T(8,128)(2,1)}, bf16[40,4096]{1,0:T(8,128)(2,1)S(1)}, u32[]{:S(2)}, u32[]{:S(2)}) collective-permute-start(bf16[40,4096]{1,0:T(8,128)(2,1)} %collective-permute-done.6), channel_id=1, source_target_pairs={{32,0},{64,32},{96,64},{112,96},{80,112},{48,80},{16,48},{0,16},{3... | collective-permute-start | bytes 983048 | tf_op jit(solution)/shard_map/ppermute | solution.py:63
  95.4 28.3 %collective-permute-start.7 = (bf16[40,4096]{1,0:T(8,128)(2,1)}, bf16[40,4096]{1,0:T(8,128)(2,1)S(1)}, u32[]{:S(2)}, u32[]{:S(2)}) collective-permute-start(bf16[40,4096]{1,0:T(8,128)(2,1)} %collective-permute-done.2), channel_id=1, source_target_pairs={{0,32},{32,64},{64,96},{96,112},{112,80},{80,48},{48,16},{16,0},{1... | collective-permute-start | bytes 983048 | tf_op jit(solution)/shard_map/ppermute | solution.py:63
  103.6 53.8 %collective-permute-start.11 = (bf16[80,4096]{1,0:T(8,128)(2,1)S(1)}, bf16[80,4096]{1,0:T(8,128)(2,1)}, u32[]{:S(2)}, u32[]{:S(2)}) collective-permute-start(bf16[80,4096]{1,0:T(8,128)(2,1)S(1)} %reshape.214), channel_id=1, source_target_pairs={{0,128},{128,0},{256,384},{384,256},{1,129},{129,1},{257,385},{385... | collective-permute-start | bytes 1966088 | tf_op jit(solution)/shard_map/ppermute | solution.py:53
  106.9 53.1 %collective-permute-start.12 = (bf16[80,4096]{1,0:T(8,128)(2,1)S(1)}, bf16[80,4096]{1,0:T(8,128)(2,1)}, u32[]{:S(2)}, u32[]{:S(2)}) collective-permute-start(bf16[80,4096]{1,0:T(8,128)(2,1)S(1)} %reshape.214), channel_id=1, source_target_pairs={{0,256},{128,384},{256,0},{384,128},{1,257},{129,385},{257,1},{385... | collective-permute-start | bytes 1966088 | tf_op jit(solution)/shard_map/ppermute | solution.py:53
  111.6 48.4 %collective-permute-start.13 = (bf16[80,4096]{1,0:T(8,128)(2,1)S(1)}, bf16[80,4096]{1,0:T(8,128)(2,1)}, u32[]{:S(2)}, u32[]{:S(2)}) collective-permute-start(bf16[80,4096]{1,0:T(8,128)(2,1)S(1)} %reshape.214), channel_id=1, source_target_pairs={{0,384},{128,256},{256,128},{384,0},{1,385},{129,257},{257,129},{3... | collective-permute-start | bytes 1966088 | tf_op jit(solution)/shard_map/ppermute | solution.py:53
  114.2 12.2 %collective-permute-start.10 = (bf16[40,2048]{1,0:T(8,128)(2,1)S(1)}, bf16[40,2048]{1,0:T(8,128)(2,1)S(1)}, u32[]{:S(2)}, u32[]{:S(2)}) collective-permute-start(bf16[40,2048]{1,0:T(8,128)(2,1)S(1)} %slice.153), channel_id=1, source_target_pairs={{32,0},{64,32},{96,64},{112,96},{80,112},{48,80},{16,48},{0,16},{3... | collective-permute-start | bytes 491528 | tf_op jit(solution)/shard_map/ppermute | solution.py:63
  123.7 14.2 %copy-start.3 = (bf16[40,4096]{1,0:T(8,128)(2,1)}, bf16[40,4096]{1,0:T(8,128)(2,1)S(1)}, u32[]{:S(2)}) copy-start(bf16[40,4096]{1,0:T(8,128)(2,1)S(1)} %collective-permute-done.7) | copy-start | bytes 983044
  123.7 10.4 %collective-permute-start.9 = (bf16[40,2048]{1,0:T(8,128)(2,1)S(1)}, bf16[40,2048]{1,0:T(8,128)(2,1)S(1)}, u32[]{:S(2)}, u32[]{:S(2)}) collective-permute-start(bf16[40,2048]{1,0:T(8,128)(2,1)S(1)} %slice.152), channel_id=1, source_target_pairs={{0,32},{32,64},{64,96},{96,112},{112,80},{80,48},{48,16},{16,0},{1... | collective-permute-start | bytes 491528 | tf_op jit(solution)/shard_map/ppermute | solution.py:63
  137.9 9.6 %copy-start.4 = (bf16[40,4096]{1,0:T(8,128)(2,1)S(1)}, bf16[40,4096]{1,0:T(8,128)(2,1)}, u32[]{:S(2)}) copy-start(bf16[40,4096]{1,0:T(8,128)(2,1)} %copy-done.3) | copy-start | bytes 983044
  139.4 9.2 %copy-start.5 = (bf16[192,128]{1,0:T(8,128)(2,1)}, bf16[192,128]{1,0:T(8,128)(2,1)S(1)}, u32[]{:S(2)}) copy-start(bf16[192,128]{1,0:T(8,128)(2,1)S(1)} %get-tuple-element.14) | copy-start | bytes 147460
  140.8 29.5 %all-to-all-start.1 = ((bf16[8,240,128]{2,1,0:T(8,128)(2,1)}), bf16[8,240,128]{2,1,0:T(8,128)(2,1)}, u32[]{:S(2)}, u32[]{:S(2)}) async-start(bf16[8,240,128]{2,1,0:T(8,128)(2,1)} %broadcast_in_dim.45), calls=%async_computation.1 | async-start | bytes 983040 | tf_op jit(solution)/shard_map/all_to_all | solution.py:121
  148.8 32.1 %collective-permute-start.14 = (bf16[80,4096]{1,0:T(8,128)(2,1)S(1)}, bf16[80,4096]{1,0:T(8,128)(2,1)}, u32[]{:S(2)}, u32[]{:S(2)}) collective-permute-start(bf16[80,4096]{1,0:T(8,128)(2,1)S(1)} %reshape.220), channel_id=1, source_target_pairs={{0,128},{128,0},{256,384},{384,256},{1,129},{129,1},{257,385},{385... | collective-permute-start | bytes 1966088 | tf_op jit(solution)/shard_map/ppermute | solution.py:53
  150.9 30.1 %collective-permute-start.15 = (bf16[80,4096]{1,0:T(8,128)(2,1)S(1)}, bf16[80,4096]{1,0:T(8,128)(2,1)}, u32[]{:S(2)}, u32[]{:S(2)}) collective-permute-start(bf16[80,4096]{1,0:T(8,128)(2,1)S(1)} %reshape.220), channel_id=1, source_target_pairs={{0,256},{128,384},{256,0},{384,128},{1,257},{129,385},{257,1},{385... | collective-permute-start | bytes 1966088 | tf_op jit(solution)/shard_map/ppermute | solution.py:53
  157.4 34.9 %collective-permute-start.16 = (bf16[80,4096]{1,0:T(8,128)(2,1)S(1)}, bf16[80,4096]{1,0:T(8,128)(2,1)}, u32[]{:S(2)}, u32[]{:S(2)}) collective-permute-start(bf16[80,4096]{1,0:T(8,128)(2,1)S(1)} %reshape.220), channel_id=1, source_target_pairs={{0,384},{128,256},{256,128},{384,0},{1,385},{129,257},{257,129},{3... | collective-permute-start | bytes 1966088 | tf_op jit(solution)/shard_map/ppermute | solution.py:53
  170.3 3.5 %copy-start.6 = (bf16[192,128]{1,0:T(8,128)(2,1)S(1)}, bf16[192,128]{1,0:T(8,128)(2,1)}, u32[]{:S(2)}) copy-start(bf16[192,128]{1,0:T(8,128)(2,1)} %copy-done.5) | copy-start | bytes 147460
  170.3 3.5 %copy-start.7 = (bf16[192,128]{1,0:T(8,128)(2,1)S(1)}, bf16[192,128]{1,0:T(8,128)(2,1)}, u32[]{:S(2)}) copy-start(bf16[192,128]{1,0:T(8,128)(2,1)} %get-tuple-element.12) | copy-start | bytes 147460
  174.9 21.9 %all-to-all-start.2 = ((bf16[4,48,1536]{2,1,0:T(8,128)(2,1)}), bf16[4,48,1536]{2,1,0:T(8,128)(2,1)}, u32[]{:S(2)}, u32[]{:S(2)}) async-start(bf16[4,48,1536]{2,1,0:T(8,128)(2,1)} %bitcast.49), calls=%async_computation.2 | async-start | bytes 1179648 | tf_op jit(solution)/shard_map/all_to_all | solution.py:131

commit v5 on v4

--- a/solution.py
+++ b/solution.py
@@ -40,10 +40,11 @@
     running = jnp.cumsum(onehot, axis=0)
     rank_in = jnp.sum(running * onehot, axis=1) - 1
     row_ids = fitted_id * (2 * capacity) + rank_in
-    scaled = (route_weight[:, None] * out_grad.astype(F32)).astype(BF16)
+    entries = jnp.concatenate([jnp.ones_like(route_weight), route_weight]).astype(BF16)
     both_ids = jnp.concatenate([row_ids, row_ids + capacity])
-    packer = (both_ids[None, :] == jnp.arange(owners * 2 * capacity, dtype=jnp.int32)[:, None]).astype(BF16)
-    both = jnp.concatenate([tokens_x, scaled], axis=0)
+    row = jnp.arange(owners * 2 * capacity, dtype=jnp.int32)
+    packer = jnp.where(both_ids[None, :] == row[:, None], entries[None, :], jnp.zeros((), BF16))
+    both = jnp.concatenate([tokens_x, out_grad], axis=0)
     packed = jnp.dot(packer, both, preferred_element_type=F32).astype(BF16)
     packed = packed.reshape(owners, 2 * capacity, local_width)
     recv = lax.all_to_all(packed, ("y", "zh", "c"), split_axis=0, concat_axis=0, tiled=True)
@@ -79,8 +80,8 @@
     def anchor(v):
         return v[:1, :1] * 0
 
-    late = [anchor(parts[2]), anchor(parts[4])]
-    weights = jnp.concatenate([w_own, w_others[0] + late[0], w_others[2], w_others[1] + late[1]], axis=0)
+    first = w_others[0] + anchor(parts[2])
+    weights = jnp.concatenate([w_own, first, w_others[2], w_others[1]], axis=0)
 
     group = nx * hid
     slots = nz * capacity

time: 200 us -> 197 us (0.985)
  the two profiles are of different devices: /device:TPU:40 before, /device:TPU:8 now
where the time goes in v5:
time: 197 us; the launch traced here: 196 us
  starting transfers between devices  105 us (53%)
  waiting for transfers between devices  46 us (23%)
  matrix products  15.7 us (8%)
  local copies, waits for them, and re-layouts  14.4 us (7%)
  other arithmetic  11.7 us (6%)
  between operations  3.17 us (2%)
    ppermute x8, starting transfers between devices, hop(): return lax.ppermute(v, 'zl', way)  42.6 us
    ppermute x9, starting transfers between devices, swap_x(): return lax.ppermute(v, 'x', [(i, i ^ k) for i in range(nx)])  30.8 us
    all_to_all x1, starting transfers between devices, body(): lax.all_to_all(packed, ('y', 'zh', 'c'), split_axis=0, concat_axis=0, til...  18.2 us
    ppermute x8, waiting for transfers between devices, hop(): return lax.ppermute(v, 'zl', way)  13.1 us
    all_to_all x1, waiting for transfers between devices, body(): lax.all_to_all(packed, ('y', 'zh', 'c'), split_axis=0, concat_axis=0, til...  12.5 us
    all_to_all x1, waiting for transfers between devices, body(): lax.all_to_all(spread, 'zl', split_axis=0, concat_axis=0, tiled=True)  12 us
    all_to_all x1, starting transfers between devices, body(): lax.all_to_all(spread, 'zl', split_axis=0, concat_axis=0, tiled=True)  8.95 us
    ppermute x9, waiting for transfers between devices, swap_x(): return lax.ppermute(v, 'x', [(i, i ^ k) for i in range(nx)])  8.39 us
  transfers between devices with their start and end apart: 20, of which 8 were waited for; matrix products, arithmetic and copies ran while one was open for 19% of the time, Pallas kernels for 0%

profile of v5, /device:TPU:8, one launch (start us, length us, event | category | flops | bytes accessed | tf_op | source)
XLA Modules:
  0.0 195.7 jit_solution(12839077258301457393)
XLA Ops:
  0.7 2.4 %pad_maximum_fusion.2 = bf16[144,4096]{1,0:T(8,128)(2,1)} fusion(bf16[48,4096]{1,0:T(8,128)(2,1)} %bitcast.51, bf16[48,4096]{1,0:T(8,128)(2,1)} %bitcast.50, bf16[48,4096]{1,0:T(8,128)(2,1)} %bitcast.49), kind=kLoop, calls=%fused_computation.10 | loop fusion | flops 3538944 | bytes 2359296 | tf_op jit(solution)/shard_map/concatenate | solution.py:56
  3.1 3.4 %collective-permute-start.3 = (bf16[144,4096]{1,0:T(8,128)(2,1)}, bf16[144,4096]{1,0:T(8,128)(2,1)S(1)}, u32[]{:S(2)}, u32[]{:S(2)}) collective-permute-start(bf16[144,4096]{1,0:T(8,128)(2,1)} %pad_maximum_fusion.2), channel_id=1, source_target_pairs={{0,128},{128,0},{256,384},{384,256},{1,129},{129,1},{257,385},{385... | collective-permute-start | bytes 3538952 | tf_op jit(solution)/shard_map/ppermute | solution.py:54
  6.5 4.0 %collective-permute-start.4 = (bf16[144,4096]{1,0:T(8,128)(2,1)}, bf16[144,4096]{1,0:T(8,128)(2,1)}, u32[]{:S(2)}, u32[]{:S(2)}) collective-permute-start(bf16[144,4096]{1,0:T(8,128)(2,1)} %pad_maximum_fusion.2), channel_id=1, source_target_pairs={{0,384},{128,256},{256,128},{384,0},{1,385},{129,257},{257,129},{3... | collective-permute-start | bytes 3538952 | tf_op jit(solution)/shard_map/ppermute | solution.py:54
  10.5 2.6 %collective-permute-start.5 = (bf16[144,4096]{1,0:T(8,128)(2,1)}, bf16[144,4096]{1,0:T(8,128)(2,1)}, u32[]{:S(2)}, u32[]{:S(2)}) collective-permute-start(bf16[144,4096]{1,0:T(8,128)(2,1)} %pad_maximum_fusion.2), channel_id=1, source_target_pairs={{0,256},{128,384},{256,0},{384,128},{1,257},{129,385},{257,1},{385... | collective-permute-start | bytes 3538952 | tf_op jit(solution)/shard_map/ppermute | solution.py:54
  13.1 0.7 fusion.43
  13.9 0.6 reduce-window.6
  14.4 0.2 slice_reduce_fusion
  15.0 2.0 %convolution_convert_fusion = bf16[640,256]{1,0:T(8,128)(2,1)} fusion(s32[320]{0:T(512)S(1)} %pad_add_fusion, bf16[320]{0:T(512)(128)(2,1)S(1)} %concatenate.69, bf16[160,256]{1,0:T(8,128)(2,1)} %param.10, bf16[160,256]{1,0:T(8,128)(2,1)} %param.9), kind=kOutput, calls=%fused_computation.7 | convolution fusion | flops 105758720 | bytes 493440 | tf_op jit(solution)/shard_map/dot_general | solution.py:48
  16.9 18.2 %all-to-all-start = ((bf16[16,40,256]{2,1,0:T(8,128)(2,1)}), bf16[16,40,256]{2,1,0:T(8,128)(2,1)S(1)}, u32[]{:S(2)}, u32[]{:S(2)}) async-start(bf16[16,40,256]{2,1,0:T(8,128)(2,1)} %bitcast.1), calls=%async_computation | async-start | bytes 655360 | tf_op jit(solution)/shard_map/all_to_all | solution.py:50
  35.1 0.8 constant_dynamic-update-slice_fusion.8
  35.9 0.8 constant_dynamic-update-slice_fusion.7
  37.1 0.8 constant_dynamic-update-slice_fusion.6
  37.9 12.5 %all-to-all-done = bf16[16,40,256]{2,1,0:T(8,128)(2,1)S(1)} async-done(((bf16[16,40,256]{2,1,0:T(8,128)(2,1)}), bf16[16,40,256]{2,1,0:T(8,128)(2,1)S(1)}, u32[]{:S(2)}, u32[]{:S(2)}) %all-to-all-start) | async-done | bytes 327712 | tf_op jit(solution)/shard_map/all_to_all | solution.py:50
  50.4 13.1 %collective-permute-start.1 = (bf16[40,4096]{1,0:T(8,128)(2,1)S(1)}, bf16[40,4096]{1,0:T(8,128)(2,1)S(1)}, u32[]{:S(2)}, u32[]{:S(2)}) collective-permute-start(bf16[40,4096]{1,0:T(8,128)(2,1)S(1)} %bitcast.53), channel_id=1, source_target_pairs={{32,0},{64,32},{96,64},{112,96},{80,112},{48,80},{16,48},{0,16},{3... | collective-permute-start | bytes 983048 | tf_op jit(solution)/shard_map/ppermute | solution.py:64
  63.6 1.9 collective-permute-start
  65.5 6.1 %collective-permute-done.1 = bf16[40,4096]{1,0:T(8,128)(2,1)S(1)} collective-permute-done((bf16[40,4096]{1,0:T(8,128)(2,1)S(1)}, bf16[40,4096]{1,0:T(8,128)(2,1)S(1)}, u32[]{:S(2)}, u32[]{:S(2)}) %collective-permute-start.1) | collective-permute-done | bytes 327712 | tf_op jit(solution)/shard_map/ppermute | solution.py:64
  71.6 0.5 slice.142
  72.8 4.4 %collective-permute-start.6 = (bf16[40,4096]{1,0:T(8,128)(2,1)S(1)}, bf16[40,4096]{1,0:T(8,128)(2,1)S(1)}, u32[]{:S(2)}, u32[]{:S(2)}) collective-permute-start(bf16[40,4096]{1,0:T(8,128)(2,1)S(1)} %collective-permute-done.1), channel_id=1, source_target_pairs={{32,0},{64,32},{96,64},{112,96},{80,112},{48,80},{16,48},{0,16},{3... | collective-permute-start | bytes 983048 | tf_op jit(solution)/shard_map/ppermute | solution.py:64
  77.2 1.5 collective-permute-done
  78.7 5.3 %collective-permute-start.2 = (bf16[40,4096]{1,0:T(8,128)(2,1)S(1)}, bf16[40,4096]{1,0:T(8,128)(2,1)}, u32[]{:S(2)}, u32[]{:S(2)}) collective-permute-start(bf16[40,4096]{1,0:T(8,128)(2,1)S(1)} %collective-permute-done), channel_id=1, source_target_pairs={{0,32},{32,64},{64,96},{96,112},{112,80},{80,48},{48,16},{16,0},{1... | collective-permute-start | bytes 983048 | tf_op jit(solution)/shard_map/ppermute | solution.py:64
  84.0 1.2 add_dynamic-update-slice_fusion
  85.2 2.4 %constant_dynamic-update-slice_fusion.5 = bf16[576,4096]{1,0:T(8,128)(2,1)} fusion(bf16[576,4096]{1,0:T(8,128)(2,1)} %add_dynamic-update-slice_fusion, bf16[144,4096]{1,0:T(8,128)(2,1)} %collective-permute-done.4), kind=kLoop, calls=%fused_computation.71 | loop fusion | bytes 2359296
  87.6 2.4 %constant_dynamic-update-slice_fusion.4 = bf16[576,4096]{1,0:T(8,128)(2,1)} fusion(bf16[576,4096]{1,0:T(8,128)(2,1)} %constant_dynamic-update-slice_fusion.5, bf16[144,4096]{1,0:T(8,128)(2,1)} %collective-permute-done.5), kind=kLoop, calls=%fused_computation.70 | loop fusion | bytes 2359296 | tf_op jit(solution)/shard_map/concatenate | solution.py:84
  90.1 1.9 collective-permute-start.8
  92.0 0.7 collective-permute-done.2
  92.7 5.4 %collective-permute-start.7 = (bf16[40,4096]{1,0:T(8,128)(2,1)}, bf16[40,4096]{1,0:T(8,128)(2,1)S(1)}, u32[]{:S(2)}, u32[]{:S(2)}) collective-permute-start(bf16[40,4096]{1,0:T(8,128)(2,1)} %collective-permute-done.2), channel_id=1, source_target_pairs={{0,32},{32,64},{64,96},{96,112},{112,80},{80,48},{48,16},{16,0},{1... | collective-permute-start | bytes 983048 | tf_op jit(solution)/shard_map/ppermute | solution.py:64
  98.1 1.0 constant_dynamic-update-slice_fusion
  99.1 3.7 %fusion.86 = f32[576,160]{1,0:T(8,128)S(1)} fusion(bf16[576,4096]{1,0:T(8,128)(2,1)} %constant_dynamic-update-slice_fusion.4, bf16[160,4096]{1,0:T(8,128)(2,1)S(1)} %constant_dynamic-update-slice_fusion), kind=kOutput, calls=%fused_computation.162 | convolution fusion | flops 754974720 | bytes 6397952 | tf_op jit(solution)/shard_map/reshape | solution.py:106
  103.0 0.1 reshape.211
  103.2 3.3 %collective-permute-start.11 = (bf16[80,4096]{1,0:T(8,128)(2,1)S(1)}, bf16[80,4096]{1,0:T(8,128)(2,1)}, u32[]{:S(2)}, u32[]{:S(2)}) collective-permute-start(bf16[80,4096]{1,0:T(8,128)(2,1)S(1)} %reshape.211), channel_id=1, source_target_pairs={{0,128},{128,0},{256,384},{384,256},{1,129},{129,1},{257,385},{385... | collective-permute-start | bytes 1966088 | tf_op jit(solution)/shard_map/ppermute | solution.py:54
  106.4 4.6 %collective-permute-start.12 = (bf16[80,4096]{1,0:T(8,128)(2,1)S(1)}, bf16[80,4096]{1,0:T(8,128)(2,1)}, u32[]{:S(2)}, u32[]{:S(2)}) collective-permute-start(bf16[80,4096]{1,0:T(8,128)(2,1)S(1)} %reshape.211), channel_id=1, source_target_pairs={{0,256},{128,384},{256,0},{384,128},{1,257},{129,385},{257,1},{385... | collective-permute-start | bytes 1966088 | tf_op jit(solution)/shard_map/ppermute | solution.py:54
  111.1 2.5 %collective-permute-start.13 = (bf16[80,4096]{1,0:T(8,128)(2,1)S(1)}, bf16[80,4096]{1,0:T(8,128)(2,1)}, u32[]{:S(2)}, u32[]{:S(2)}) collective-permute-start(bf16[80,4096]{1,0:T(8,128)(2,1)S(1)} %reshape.211), channel_id=1, source_target_pairs={{0,384},{128,256},{256,128},{384,0},{1,385},{129,257},{257,129},{3... | collective-permute-start | bytes 1966088 | tf_op jit(solution)/shard_map/ppermute | solution.py:54
  113.8 3.0 %collective-permute-start.10 = (bf16[40,2048]{1,0:T(8,128)(2,1)S(1)}, bf16[40,2048]{1,0:T(8,128)(2,1)S(1)}, u32[]{:S(2)}, u32[]{:S(2)}) collective-permute-start(bf16[40,2048]{1,0:T(8,128)(2,1)S(1)} %slice.148), channel_id=1, source_target_pairs={{32,0},{64,32},{96,64},{112,96},{80,112},{48,80},{16,48},{0,16},{3... | collective-permute-start | bytes 491528 | tf_op jit(solution)/shard_map/ppermute | solution.py:64
  116.8 7.5 %collective-permute-start.9 = (bf16[40,2048]{1,0:T(8,128)(2,1)S(1)}, bf16[40,2048]{1,0:T(8,128)(2,1)S(1)}, u32[]{:S(2)}, u32[]{:S(2)}) collective-permute-start(bf16[40,2048]{1,0:T(8,128)(2,1)S(1)} %slice.147), channel_id=1, source_target_pairs={{0,32},{32,64},{64,96},{96,112},{112,80},{80,48},{48,16},{16,0},{1... | collective-permute-start | bytes 491528 | tf_op jit(solution)/shard_map/ppermute | solution.py:64
  124.4 0.3 fusion.12
  124.7 1.0 collective-permute-done.10
  125.7 3.8 %collective-permute-done.9 = bf16[40,2048]{1,0:T(8,128)(2,1)S(1)} collective-permute-done((bf16[40,2048]{1,0:T(8,128)(2,1)S(1)}, bf16[40,2048]{1,0:T(8,128)(2,1)S(1)}, u32[]{:S(2)}, u32[]{:S(2)}) %collective-permute-start.9) | collective-permute-done | bytes 163872 | tf_op jit(solution)/shard_map/ppermute | solution.py:64
  129.6 3.7 %fusion.83 = f32[576,160]{1,0:T(8,128)S(1)} fusion(bf16[576,4096]{1,0:T(8,128)(2,1)} %constant_dynamic-update-slice_fusion.4, bf16[40,2048]{1,0:T(8,128)(2,1)S(1)} %collective-permute-done.10, bf16[40,2048]{1,0:T(8,128)(2,1)S(1)} %collective-permute-done.9, bf16[40,4096]{1,0:T(8,128)(2,1)S(1)} %collective-permute-done.8, ...), kind=kOutput, calls=%fused_computation.159 | convolution fusion | flops 761528320 | bytes 6397952 | tf_op jit(solution)/shard_map/reshape | solution.py:106
  133.4 0.1 fusion.23
  133.5 0.5 convolution_convert_fusion.1
  134.1 0.7 fusion.85
  134.8 0.5 slice.153
  135.3 0.8 broadcast_in_dim.60
  136.2 9.0 %all-to-all-start.1 = ((bf16[8,240,128]{2,1,0:T(8,128)(2,1)}), bf16[8,240,128]{2,1,0:T(8,128)(2,1)}, u32[]{:S(2)}, u32[]{:S(2)}) async-start(bf16[8,240,128]{2,1,0:T(8,128)(2,1)} %broadcast_in_dim.60), calls=%async_computation.1 | async-start | bytes 983040 | tf_op jit(solution)/shard_map/all_to_all | solution.py:122
  145.1 0.1 maximum_maximum_fusion
  145.3 0.1 reshape.217
  145.5 2.0 %collective-permute-start.14 = (bf16[80,4096]{1,0:T(8,128)(2,1)S(1)}, bf16[80,4096]{1,0:T(8,128)(2,1)}, u32[]{:S(2)}, u32[]{:S(2)}) collective-permute-start(bf16[80,4096]{1,0:T(8,128)(2,1)S(1)} %reshape.217), channel_id=1, source_target_pairs={{0,128},{128,0},{256,384},{384,256},{1,129},{129,1},{257,385},{385... | collective-permute-start | bytes 1966088 | tf_op jit(solution)/shard_map/ppermute | solution.py:54
  147.4 5.8 %collective-permute-start.15 = (bf16[80,4096]{1,0:T(8,128)(2,1)S(1)}, bf16[80,4096]{1,0:T(8,128)(2,1)}, u32[]{:S(2)}, u32[]{:S(2)}) collective-permute-start(bf16[80,4096]{1,0:T(8,128)(2,1)S(1)} %reshape.217), channel_id=1, source_target_pairs={{0,256},{128,384},{256,0},{384,128},{1,257},{129,385},{257,1},{385... | collective-permute-start | bytes 1966088 | tf_op jit(solution)/shard_map/ppermute | solution.py:54
  154.0 2.6 %collective-permute-start.16 = (bf16[80,4096]{1,0:T(8,128)(2,1)S(1)}, bf16[80,4096]{1,0:T(8,128)(2,1)}, u32[]{:S(2)}, u32[]{:S(2)}) collective-permute-start(bf16[80,4096]{1,0:T(8,128)(2,1)S(1)} %reshape.217), channel_id=1, source_target_pairs={{0,384},{128,256},{256,128},{384,0},{1,385},{129,257},{257,129},{3... | collective-permute-start | bytes 1966088 | tf_op jit(solution)/shard_map/ppermute | solution.py:54
  156.6 1.6 pad_maximum_fusion
  158.3 12.0 %all-to-all-done.1 = bf16[8,240,128]{2,1,0:T(8,128)(2,1)} async-done(((bf16[8,240,128]{2,1,0:T(8,128)(2,1)}), bf16[8,240,128]{2,1,0:T(8,128)(2,1)}, u32[]{:S(2)}, u32[]{:S(2)}) %all-to-all-start.1) | async-done | bytes 491552 | tf_op jit(solution)/shard_map/all_to_all | solution.py:122
  170.2 1.1 fusion.84
  171.4 0.2 fusion.3
  171.6 1.1 fusion.4
  172.7 1.1 fusion.5
  173.7 0.2 fusion.6
  174.0 0.9 pad_maximum_fusion.3
  174.9 4.1 %all-to-all-start.2 = ((bf16[4,48,1536]{2,1,0:T(8,128)(2,1)}), bf16[4,48,1536]{2,1,0:T(8,128)(2,1)}, u32[]{:S(2)}, u32[]{:S(2)}) async-start(bf16[4,48,1536]{2,1,0:T(8,128)(2,1)} %bitcast.48), calls=%async_computation.2 | async-start | bytes 1179648 | tf_op jit(solution)/shard_map/all_to_all | solution.py:132
  179.0 1.2 slice.160
  180.9 8.4 %collective-permute-done.16 = bf16[80,4096]{1,0:T(8,128)(2,1)} collective-permute-done((bf16[80,4096]{1,0:T(8,128)(2,1)S(1)}, bf16[80,4096]{1,0:T(8,128)(2,1)}, u32[]{:S(2)}, u32[]{:S(2)}) %collective-permute-start.16) | collective-permute-done | bytes 655392 | tf_op jit(solution)/shard_map/ppermute | solution.py:54
  189.3 1.6 pad_maximum_fusion.1
  190.9 0.8 fusion.38
  191.7 2.1 %fusion.1 = f32[1,128,4096]{2,1,0:T(8,128)} fusion(f32[128,4096]{1,0:T(8,128)S(1)} %fusion.38, bf16[320,4096]{1,0:T(8,128)(2,1)S(1)} %pad_maximum_fusion, s32[]{:T(128)S(6)} %select_n.181), kind=kOutput, calls=%fused_computation.2 | convolution fusion | flops 336592896 | bytes 6897668 | tf_op jit(solution)/shard_map/dot_general | solution.py:21
  193.8 1.9 convert_reduce_fusion
  (68 shorter events, 1.4 us)
Async XLA Ops:
  0.6 34.5 %copy-start = (bf16[1,48,4096]{2,1,0:T(8,128)(2,1)S(1)}, bf16[1,48,4096]{2,1,0:T(8,128)(2,1)}, u32[]{:S(2)}) copy-start(bf16[1,48,4096]{2,1,0:T(8,128)(2,1)} %param.13) | copy-start | bytes 1179652
  0.6 35.3 %copy-start.1 = (bf16[1,48,4096]{2,1,0:T(8,128)(2,1)S(1)}, bf16[1,48,4096]{2,1,0:T(8,128)(2,1)}, u32[]{:S(2)}) copy-start(bf16[1,48,4096]{2,1,0:T(8,128)(2,1)} %param.14) | copy-start | bytes 1179652
  0.7 36.0 %copy-start.8 = (s32[4]{0:T(128)S(1)}, s32[4]{0:T(128)}, u32[]{:S(2)}) copy-start(s32[4]{0:T(128)} %constant.196) | copy-start | bytes 52
  0.7 36.0 %copy-start.9 = (s32[4]{0:T(128)S(1)}, s32[4]{0:T(128)}, u32[]{:S(2)}) copy-start(s32[4]{0:T(128)} %constant.197) | copy-start | bytes 52
  0.7 36.4 %copy-start.2 = (bf16[1,48,4096]{2,1,0:T(8,128)(2,1)S(1)}, bf16[1,48,4096]{2,1,0:T(8,128)(2,1)}, u32[]{:S(2)}) copy-start(bf16[1,48,4096]{2,1,0:T(8,128)(2,1)} %param.15) | copy-start | bytes 1179652
  3.1 80.8 %collective-permute-start.3 = (bf16[144,4096]{1,0:T(8,128)(2,1)}, bf16[144,4096]{1,0:T(8,128)(2,1)S(1)}, u32[]{:S(2)}, u32[]{:S(2)}) collective-permute-start(bf16[144,4096]{1,0:T(8,128)(2,1)} %pad_maximum_fusion.2), channel_id=1, source_target_pairs={{0,128},{128,0},{256,384},{384,256},{1,129},{129,1},{257,385},{385... | collective-permute-start | bytes 3538952 | tf_op jit(solution)/shard_map/ppermute | solution.py:54
  6.5 78.7 %collective-permute-start.4 = (bf16[144,4096]{1,0:T(8,128)(2,1)}, bf16[144,4096]{1,0:T(8,128)(2,1)}, u32[]{:S(2)}, u32[]{:S(2)}) collective-permute-start(bf16[144,4096]{1,0:T(8,128)(2,1)} %pad_maximum_fusion.2), channel_id=1, source_target_pairs={{0,384},{128,256},{256,128},{384,0},{1,385},{129,257},{257,129},{3... | collective-permute-start | bytes 3538952 | tf_op jit(solution)/shard_map/ppermute | solution.py:54
  10.5 77.1 %collective-permute-start.5 = (bf16[144,4096]{1,0:T(8,128)(2,1)}, bf16[144,4096]{1,0:T(8,128)(2,1)}, u32[]{:S(2)}, u32[]{:S(2)}) collective-permute-start(bf16[144,4096]{1,0:T(8,128)(2,1)} %pad_maximum_fusion.2), channel_id=1, source_target_pairs={{0,256},{128,384},{256,0},{384,128},{1,257},{129,385},{257,1},{385... | collective-permute-start | bytes 3538952 | tf_op jit(solution)/shard_map/ppermute | solution.py:54
  16.9 33.5 %all-to-all-start = ((bf16[16,40,256]{2,1,0:T(8,128)(2,1)}), bf16[16,40,256]{2,1,0:T(8,128)(2,1)S(1)}, u32[]{:S(2)}, u32[]{:S(2)}) async-start(bf16[16,40,256]{2,1,0:T(8,128)(2,1)} %bitcast.1), calls=%async_computation | async-start | bytes 655360 | tf_op jit(solution)/shard_map/all_to_all | solution.py:50
  50.4 21.2 %collective-permute-start.1 = (bf16[40,4096]{1,0:T(8,128)(2,1)S(1)}, bf16[40,4096]{1,0:T(8,128)(2,1)S(1)}, u32[]{:S(2)}, u32[]{:S(2)}) collective-permute-start(bf16[40,4096]{1,0:T(8,128)(2,1)S(1)} %bitcast.53), channel_id=1, source_target_pairs={{32,0},{64,32},{96,64},{112,96},{80,112},{48,80},{16,48},{0,16},{3... | collective-permute-start | bytes 983048 | tf_op jit(solution)/shard_map/ppermute | solution.py:64
  63.6 15.1 %collective-permute-start = (bf16[40,4096]{1,0:T(8,128)(2,1)S(1)}, bf16[40,4096]{1,0:T(8,128)(2,1)S(1)}, u32[]{:S(2)}, u32[]{:S(2)}) collective-permute-start(bf16[40,4096]{1,0:T(8,128)(2,1)S(1)} %bitcast.54), channel_id=1, source_target_pairs={{0,32},{32,64},{64,96},{96,112},{112,80},{80,48},{48,16},{16,0},{1... | collective-permute-start | bytes 983048 | tf_op jit(solution)/shard_map/ppermute | solution.py:64
  72.8 17.3 %collective-permute-start.6 = (bf16[40,4096]{1,0:T(8,128)(2,1)S(1)}, bf16[40,4096]{1,0:T(8,128)(2,1)S(1)}, u32[]{:S(2)}, u32[]{:S(2)}) collective-permute-start(bf16[40,4096]{1,0:T(8,128)(2,1)S(1)} %collective-permute-done.1), channel_id=1, source_target_pairs={{32,0},{64,32},{96,64},{112,96},{80,112},{48,80},{16,48},{0,16},{3... | collective-permute-start | bytes 983048 | tf_op jit(solution)/shard_map/ppermute | solution.py:64
  78.7 14.0 %collective-permute-start.2 = (bf16[40,4096]{1,0:T(8,128)(2,1)S(1)}, bf16[40,4096]{1,0:T(8,128)(2,1)}, u32[]{:S(2)}, u32[]{:S(2)}) collective-permute-start(bf16[40,4096]{1,0:T(8,128)(2,1)S(1)} %collective-permute-done), channel_id=1, source_target_pairs={{0,32},{32,64},{64,96},{96,112},{112,80},{80,48},{48,16},{16,0},{1... | collective-permute-start | bytes 983048 | tf_op jit(solution)/shard_map/ppermute | solution.py:64
  90.1 39.5 %copy-start.3 = (bf16[40,4096]{1,0:T(8,128)(2,1)}, bf16[40,4096]{1,0:T(8,128)(2,1)S(1)}, u32[]{:S(2)}) copy-start(bf16[40,4096]{1,0:T(8,128)(2,1)S(1)} %collective-permute-done.6) | copy-start | bytes 983044
  90.1 23.7 %collective-permute-start.8 = (bf16[40,4096]{1,0:T(8,128)(2,1)S(1)}, bf16[40,4096]{1,0:T(8,128)(2,1)S(1)}, u32[]{:S(2)}, u32[]{:S(2)}) collective-permute-start(bf16[40,4096]{1,0:T(8,128)(2,1)S(1)} %collective-permute-done.6), channel_id=1, source_target_pairs={{32,0},{64,32},{96,64},{112,96},{80,112},{48,80},{16,48},{0,16},{3... | collective-permute-start | bytes 983048 | tf_op jit(solution)/shard_map/ppermute | solution.py:64
  92.7 24.1 %collective-permute-start.7 = (bf16[40,4096]{1,0:T(8,128)(2,1)}, bf16[40,4096]{1,0:T(8,128)(2,1)S(1)}, u32[]{:S(2)}, u32[]{:S(2)}) collective-permute-start(bf16[40,4096]{1,0:T(8,128)(2,1)} %collective-permute-done.2), channel_id=1, source_target_pairs={{0,32},{32,64},{64,96},{96,112},{112,80},{80,48},{48,16},{16,0},{1... | collective-permute-start | bytes 983048 | tf_op jit(solution)/shard_map/ppermute | solution.py:64
  103.2 50.8 %collective-permute-start.11 = (bf16[80,4096]{1,0:T(8,128)(2,1)S(1)}, bf16[80,4096]{1,0:T(8,128)(2,1)}, u32[]{:S(2)}, u32[]{:S(2)}) collective-permute-start(bf16[80,4096]{1,0:T(8,128)(2,1)S(1)} %reshape.211), channel_id=1, source_target_pairs={{0,128},{128,0},{256,384},{384,256},{1,129},{129,1},{257,385},{385... | collective-permute-start | bytes 1966088 | tf_op jit(solution)/shard_map/ppermute | solution.py:54
  106.4 50.2 %collective-permute-start.12 = (bf16[80,4096]{1,0:T(8,128)(2,1)S(1)}, bf16[80,4096]{1,0:T(8,128)(2,1)}, u32[]{:S(2)}, u32[]{:S(2)}) collective-permute-start(bf16[80,4096]{1,0:T(8,128)(2,1)S(1)} %reshape.211), channel_id=1, source_target_pairs={{0,256},{128,384},{256,0},{384,128},{1,257},{129,385},{257,1},{385... | collective-permute-start | bytes 1966088 | tf_op jit(solution)/shard_map/ppermute | solution.py:54
  111.1 45.5 %collective-permute-start.13 = (bf16[80,4096]{1,0:T(8,128)(2,1)S(1)}, bf16[80,4096]{1,0:T(8,128)(2,1)}, u32[]{:S(2)}, u32[]{:S(2)}) collective-permute-start(bf16[80,4096]{1,0:T(8,128)(2,1)S(1)} %reshape.211), channel_id=1, source_target_pairs={{0,384},{128,256},{256,128},{384,0},{1,385},{129,257},{257,129},{3... | collective-permute-start | bytes 1966088 | tf_op jit(solution)/shard_map/ppermute | solution.py:54
  113.8 11.9 %collective-permute-start.10 = (bf16[40,2048]{1,0:T(8,128)(2,1)S(1)}, bf16[40,2048]{1,0:T(8,128)(2,1)S(1)}, u32[]{:S(2)}, u32[]{:S(2)}) collective-permute-start(bf16[40,2048]{1,0:T(8,128)(2,1)S(1)} %slice.148), channel_id=1, source_target_pairs={{32,0},{64,32},{96,64},{112,96},{80,112},{48,80},{16,48},{0,16},{3... | collective-permute-start | bytes 491528 | tf_op jit(solution)/shard_map/ppermute | solution.py:64
  116.8 12.7 %collective-permute-start.9 = (bf16[40,2048]{1,0:T(8,128)(2,1)S(1)}, bf16[40,2048]{1,0:T(8,128)(2,1)S(1)}, u32[]{:S(2)}, u32[]{:S(2)}) collective-permute-start(bf16[40,2048]{1,0:T(8,128)(2,1)S(1)} %slice.147), channel_id=1, source_target_pairs={{0,32},{32,64},{64,96},{96,112},{112,80},{80,48},{48,16},{16,0},{1... | collective-permute-start | bytes 491528 | tf_op jit(solution)/shard_map/ppermute | solution.py:64
  133.3 11.8 %copy-start.4 = (bf16[40,4096]{1,0:T(8,128)(2,1)S(1)}, bf16[40,4096]{1,0:T(8,128)(2,1)}, u32[]{:S(2)}) copy-start(bf16[40,4096]{1,0:T(8,128)(2,1)} %copy-done.3) | copy-start | bytes 983044
  134.8 21.9 %copy-start.5 = (bf16[192,128]{1,0:T(8,128)(2,1)}, bf16[192,128]{1,0:T(8,128)(2,1)S(1)}, u32[]{:S(2)}) copy-start(bf16[192,128]{1,0:T(8,128)(2,1)S(1)} %get-tuple-element.14) | copy-start | bytes 147460
  136.2 34.1 %all-to-all-start.1 = ((bf16[8,240,128]{2,1,0:T(8,128)(2,1)}), bf16[8,240,128]{2,1,0:T(8,128)(2,1)}, u32[]{:S(2)}, u32[]{:S(2)}) async-start(bf16[8,240,128]{2,1,0:T(8,128)(2,1)} %broadcast_in_dim.60), calls=%async_computation.1 | async-start | bytes 983040 | tf_op jit(solution)/shard_map/all_to_all | solution.py:122
  145.5 35.5 %collective-permute-start.14 = (bf16[80,4096]{1,0:T(8,128)(2,1)S(1)}, bf16[80,4096]{1,0:T(8,128)(2,1)}, u32[]{:S(2)}, u32[]{:S(2)}) collective-permute-start(bf16[80,4096]{1,0:T(8,128)(2,1)S(1)} %reshape.217), channel_id=1, source_target_pairs={{0,128},{128,0},{256,384},{384,256},{1,129},{129,1},{257,385},{385... | collective-permute-start | bytes 1966088 | tf_op jit(solution)/shard_map/ppermute | solution.py:54
  147.4 33.5 %collective-permute-start.15 = (bf16[80,4096]{1,0:T(8,128)(2,1)S(1)}, bf16[80,4096]{1,0:T(8,128)(2,1)}, u32[]{:S(2)}, u32[]{:S(2)}) collective-permute-start(bf16[80,4096]{1,0:T(8,128)(2,1)S(1)} %reshape.217), channel_id=1, source_target_pairs={{0,256},{128,384},{256,0},{384,128},{1,257},{129,385},{257,1},{385... | collective-permute-start | bytes 1966088 | tf_op jit(solution)/shard_map/ppermute | solution.py:54
  154.0 35.3 %collective-permute-start.16 = (bf16[80,4096]{1,0:T(8,128)(2,1)S(1)}, bf16[80,4096]{1,0:T(8,128)(2,1)}, u32[]{:S(2)}, u32[]{:S(2)}) collective-permute-start(bf16[80,4096]{1,0:T(8,128)(2,1)S(1)} %reshape.217), channel_id=1, source_target_pairs={{0,384},{128,256},{256,128},{384,0},{1,385},{129,257},{257,129},{3... | collective-permute-start | bytes 1966088 | tf_op jit(solution)/shard_map/ppermute | solution.py:54
  170.2 3.5 %copy-start.6 = (bf16[192,128]{1,0:T(8,128)(2,1)S(1)}, bf16[192,128]{1,0:T(8,128)(2,1)}, u32[]{:S(2)}) copy-start(bf16[192,128]{1,0:T(8,128)(2,1)} %copy-done.5) | copy-start | bytes 147460
  170.2 3.5 %copy-start.7 = (bf16[192,128]{1,0:T(8,128)(2,1)S(1)}, bf16[192,128]{1,0:T(8,128)(2,1)}, u32[]{:S(2)}) copy-start(bf16[192,128]{1,0:T(8,128)(2,1)} %get-tuple-element.12) | copy-start | bytes 147460
  174.9 18.9 %all-to-all-start.2 = ((bf16[4,48,1536]{2,1,0:T(8,128)(2,1)}), bf16[4,48,1536]{2,1,0:T(8,128)(2,1)}, u32[]{:S(2)}, u32[]{:S(2)}) async-start(bf16[4,48,1536]{2,1,0:T(8,128)(2,1)} %bitcast.48), calls=%async_computation.2 | async-start | bytes 1179648 | tf_op jit(solution)/shard_map/all_to_all | solution.py:132

commit v6 on v5

--- a/solution.py
+++ b/solution.py
@@ -75,7 +75,7 @@
         steps += [k, nz - k]
     parts.append(jnp.concatenate(far, axis=1))
     steps.append(nz // 2)
-    half = nz // 2
+    cuts = (0, 5, nz)
 
     def anchor(v):
         return v[:1, :1] * 0
@@ -90,7 +90,6 @@
     offset = (unit // hid) ^ xi
     from_unit = (offset ^ (offset >> 1)) * hid + unit % hid
     unit_perm = (from_unit[:, None] == unit[None, :]).astype(BF16)
-    column = jnp.arange(half * 2 * capacity, dtype=jnp.int32)
     lanes = 128
     rest = slots - lanes
     packed_col = jnp.arange((nx + 1) * lanes, dtype=jnp.int32)
@@ -100,15 +99,18 @@
     sorted_f32 = 0.0
     x_half = []
     for h in range(2):
-        rows = jnp.concatenate(parts[h * half : (h + 1) * half], axis=0)
-        x_rows = rows.reshape(half, 2 * capacity, full_width)[:, :capacity]
-        x_half.append(x_rows.reshape(half * capacity, full_width))
+        count = cuts[h + 1] - cuts[h]
+        rows = jnp.concatenate(parts[cuts[h] : cuts[h + 1]], axis=0)
+        x_rows = rows.reshape(count, 2 * capacity, full_width)[:, :capacity]
+        x_rows = x_rows.reshape(count * capacity, full_width)
+        x_rows = jnp.pad(x_rows, ((0, -count * capacity % 8), (0, 0)))
+        x_half.append(lax.optimization_barrier(x_rows))
         pre = dot_nt(weights, rows).reshape(nx, 3 * hid, -1)
         gate_pre, up_pre = pre[:, :hid], pre[:, hid : 2 * hid]
         hidden_grad = jnp.roll(pre[:, 2 * hid :], -capacity, axis=2)
         gate_grad = (hidden_grad * up_pre * silu_slope(gate_pre)).astype(BF16).reshape(group, -1)
-        went = jnp.repeat(jnp.array(steps[h * half : (h + 1) * half], jnp.int32), 2 * capacity)
-        within = column % (2 * capacity)
+        went = jnp.repeat(jnp.array(steps[cuts[h] : cuts[h + 1]], jnp.int32), 2 * capacity)
+        within = jnp.arange(count * 2 * capacity, dtype=jnp.int32) % (2 * capacity)
         target = jnp.where(within < capacity, ((place - went + nz) % nz) * capacity + within, -1)
         slot_perm = (target[:, None] == slot[None, :]).astype(BF16)
         sorted_f32 = sorted_f32 + jnp.dot(gate_grad, slot_perm, preferred_element_type=F32)
@@ -130,12 +132,12 @@
         cols.append(sums.astype(BF16))
     part_sent = jnp.concatenate(cols, axis=1).reshape(nx, hid, nx * nz * hid)
     part = lax.all_to_all(part_sent, "x", split_axis=0, concat_axis=0, tiled=True)
-    grad_rows = jnp.sum(part.astype(F32), axis=0)
+    grad_rows = sum(part[j].astype(F32) for j in range(nx))
 
     strip_width = full_width // (nx * nz)
     input_rows = 0.0
     for name, piece in zip(("xa", "xb"), x_half):
-        own_piece = piece + (later if name == "xb" else anchor(sent))
+        own_piece = piece + (later if name == "xb" else anchor(g_packed))
         gathered = [own_piece] + [swap_x(piece, k) for k in range(1, nx)]
         rows = jnp.concatenate(gathered, axis=0)
         strip = lax.dynamic_slice_in_dim(rows, (xi * nz + zi) * strip_width, strip_width, 1)

time: 197 us -> 197 us (level)
  the two profiles are of different devices: /device:TPU:8 before, /device:TPU:64 now
where the time goes in v6:
time: 197 us; the launch traced here: 195 us
  starting transfers between devices  90.5 us (46%)
  waiting for transfers between devices  54.9 us (28%)
  local copies, waits for them, and re-layouts  18.8 us (10%)
  matrix products  14.8 us (8%)
  other arithmetic  13.2 us (7%)
  between operations  3.25 us (2%)
    ppermute x9, starting transfers between devices, swap_x(): return lax.ppermute(v, 'x', [(i, i ^ k) for i in range(nx)])  30.9 us
    ppermute x8, starting transfers between devices, hop(): return lax.ppermute(v, 'zl', way)  30.2 us
    all_to_all x1, waiting for transfers between devices, body(): lax.all_to_all(packed, ('y', 'zh', 'c'), split_axis=0, concat_axis=0, til...  21.8 us
    ppermute x8, waiting for transfers between devices, hop(): return lax.ppermute(v, 'zl', way)  18.9 us
    all_to_all x1, starting transfers between devices, body(): lax.all_to_all(packed, ('y', 'zh', 'c'), split_axis=0, concat_axis=0, til...  16 us
    dot_general x6, matrix products, dot_nt(): lax.dot_general(a, b, (((1,), (1,)), ((), ())), preferred_element_type=F32)  10.3 us
    all_to_all x1, starting transfers between devices, body(): lax.all_to_all(spread, 'zl', split_axis=0, concat_axis=0, tiled=True)  9.14 us
    all_to_all x1, waiting for transfers between devices, body(): lax.all_to_all(spread, 'zl', split_axis=0, concat_axis=0, tiled=True)  7.34 us
  transfers between devices with their start and end apart: 20, of which 7 were waited for; matrix products, arithmetic and copies ran while one was open for 22% of the time, Pallas kernels for 0%

profile of v6, /device:TPU:64, one launch (start us, length us, event | category | flops | bytes accessed | tf_op | source)
XLA Modules:
  0.0 195.4 jit_solution(5968529293685704078)
XLA Ops:
  0.7 2.4 %pad_maximum_fusion.2 = bf16[144,4096]{1,0:T(8,128)(2,1)} fusion(bf16[48,4096]{1,0:T(8,128)(2,1)} %bitcast.50, bf16[48,4096]{1,0:T(8,128)(2,1)} %bitcast.49, bf16[48,4096]{1,0:T(8,128)(2,1)} %bitcast.48), kind=kLoop, calls=%fused_computation.9 | loop fusion | flops 3538944 | bytes 2359296 | tf_op jit(solution)/shard_map/concatenate | solution.py:56
  3.1 3.5 %collective-permute-start.4 = (bf16[144,4096]{1,0:T(8,128)(2,1)}, bf16[144,4096]{1,0:T(8,128)(2,1)S(1)}, u32[]{:S(2)}, u32[]{:S(2)}) collective-permute-start(bf16[144,4096]{1,0:T(8,128)(2,1)} %pad_maximum_fusion.2), channel_id=1, source_target_pairs={{0,128},{128,0},{256,384},{384,256},{1,129},{129,1},{257,385},{385... | collective-permute-start | bytes 3538952 | tf_op jit(solution)/shard_map/ppermute | solution.py:54
  6.6 4.0 %collective-permute-start.5 = (bf16[144,4096]{1,0:T(8,128)(2,1)}, bf16[144,4096]{1,0:T(8,128)(2,1)}, u32[]{:S(2)}, u32[]{:S(2)}) collective-permute-start(bf16[144,4096]{1,0:T(8,128)(2,1)} %pad_maximum_fusion.2), channel_id=1, source_target_pairs={{0,384},{128,256},{256,128},{384,0},{1,385},{129,257},{257,129},{3... | collective-permute-start | bytes 3538952 | tf_op jit(solution)/shard_map/ppermute | solution.py:54
  10.7 2.6 %collective-permute-start.6 = (bf16[144,4096]{1,0:T(8,128)(2,1)}, bf16[144,4096]{1,0:T(8,128)(2,1)}, u32[]{:S(2)}, u32[]{:S(2)}) collective-permute-start(bf16[144,4096]{1,0:T(8,128)(2,1)} %pad_maximum_fusion.2), channel_id=1, source_target_pairs={{0,256},{128,384},{256,0},{384,128},{1,257},{129,385},{257,1},{385... | collective-permute-start | bytes 3538952 | tf_op jit(solution)/shard_map/ppermute | solution.py:54
  13.3 0.6 reduce-window.6
  14.4 1.0 convolution_convert_fusion
  15.4 16.0 %all-to-all-start = ((bf16[16,40,256]{2,1,0:T(8,128)(2,1)}), bf16[16,40,256]{2,1,0:T(8,128)(2,1)S(1)}, u32[]{:S(2)}, u32[]{:S(2)}) async-start(bf16[16,40,256]{2,1,0:T(8,128)(2,1)} %bitcast.1), calls=%async_computation | async-start | bytes 655360 | tf_op jit(solution)/shard_map/all_to_all | solution.py:50
  31.5 0.8 constant_dynamic-update-slice_fusion.9
  32.3 0.8 constant_dynamic-update-slice_fusion.8
  33.4 0.8 constant_dynamic-update-slice_fusion.7
  34.2 21.8 %all-to-all-done = bf16[16,40,256]{2,1,0:T(8,128)(2,1)S(1)} async-done(((bf16[16,40,256]{2,1,0:T(8,128)(2,1)}), bf16[16,40,256]{2,1,0:T(8,128)(2,1)S(1)}, u32[]{:S(2)}, u32[]{:S(2)}) %all-to-all-start) | async-done | bytes 327712 | tf_op jit(solution)/shard_map/all_to_all | solution.py:50
  56.0 4.4 %collective-permute-start = (bf16[40,4096]{1,0:T(8,128)(2,1)S(1)}, bf16[40,4096]{1,0:T(8,128)(2,1)S(1)}, u32[]{:S(2)}, u32[]{:S(2)}) collective-permute-start(bf16[40,4096]{1,0:T(8,128)(2,1)S(1)} %bitcast.52), channel_id=1, source_target_pairs={{0,32},{32,64},{64,96},{96,112},{112,80},{80,48},{48,16},{16,0},{1... | collective-permute-start | bytes 983048 | tf_op jit(solution)/shard_map/ppermute | solution.py:64
  60.4 2.3 %collective-permute-start.1 = (bf16[40,4096]{1,0:T(8,128)(2,1)S(1)}, bf16[40,4096]{1,0:T(8,128)(2,1)S(1)}, u32[]{:S(2)}, u32[]{:S(2)}) collective-permute-start(bf16[40,4096]{1,0:T(8,128)(2,1)S(1)} %bitcast.53), channel_id=1, source_target_pairs={{32,0},{64,32},{96,64},{112,96},{80,112},{48,80},{16,48},{0,16},{3... | collective-permute-start | bytes 983048 | tf_op jit(solution)/shard_map/ppermute | solution.py:64
  62.8 12.5 %collective-permute-done.1 = bf16[40,4096]{1,0:T(8,128)(2,1)S(1)} collective-permute-done((bf16[40,4096]{1,0:T(8,128)(2,1)S(1)}, bf16[40,4096]{1,0:T(8,128)(2,1)S(1)}, u32[]{:S(2)}, u32[]{:S(2)}) %collective-permute-start.1) | collective-permute-done | bytes 327712 | tf_op jit(solution)/shard_map/ppermute | solution.py:64
  75.3 0.5 slice.159
  76.4 3.3 %collective-permute-start.3 = (bf16[40,4096]{1,0:T(8,128)(2,1)S(1)}, bf16[40,4096]{1,0:T(8,128)(2,1)}, u32[]{:S(2)}, u32[]{:S(2)}) collective-permute-start(bf16[40,4096]{1,0:T(8,128)(2,1)S(1)} %collective-permute-done.1), channel_id=1, source_target_pairs={{32,0},{64,32},{96,64},{112,96},{80,112},{48,80},{16,48},{0,16},{3... | collective-permute-start | bytes 983048 | tf_op jit(solution)/shard_map/ppermute | solution.py:64
  79.7 4.7 %collective-permute-start.2 = (bf16[40,4096]{1,0:T(8,128)(2,1)S(1)}, bf16[40,4096]{1,0:T(8,128)(2,1)}, u32[]{:S(2)}, u32[]{:S(2)}) collective-permute-start(bf16[40,4096]{1,0:T(8,128)(2,1)S(1)} %collective-permute-done), channel_id=1, source_target_pairs={{0,32},{32,64},{64,96},{96,112},{112,80},{80,48},{48,16},{16,0},{1... | collective-permute-start | bytes 983048 | tf_op jit(solution)/shard_map/ppermute | solution.py:64
  84.4 1.2 add_dynamic-update-slice_fusion
  85.7 2.4 %constant_dynamic-update-slice_fusion.6 = bf16[576,4096]{1,0:T(8,128)(2,1)} fusion(bf16[576,4096]{1,0:T(8,128)(2,1)} %add_dynamic-update-slice_fusion, bf16[144,4096]{1,0:T(8,128)(2,1)} %collective-permute-done.5), kind=kLoop, calls=%fused_computation.72 | loop fusion | bytes 2359296
  88.1 2.4 %constant_dynamic-update-slice_fusion.5 = bf16[576,4096]{1,0:T(8,128)(2,1)} fusion(bf16[576,4096]{1,0:T(8,128)(2,1)} %constant_dynamic-update-slice_fusion.6, bf16[144,4096]{1,0:T(8,128)(2,1)} %collective-permute-done.6), kind=kLoop, calls=%fused_computation.71 | loop fusion | bytes 2359296 | tf_op jit(solution)/shard_map/concatenate | solution.py:84
  90.5 3.2 %collective-permute-done.2 = bf16[40,4096]{1,0:T(8,128)(2,1)} collective-permute-done((bf16[40,4096]{1,0:T(8,128)(2,1)S(1)}, bf16[40,4096]{1,0:T(8,128)(2,1)}, u32[]{:S(2)}, u32[]{:S(2)}) %collective-permute-start.2) | collective-permute-done | bytes 327712 | tf_op jit(solution)/shard_map/ppermute | solution.py:64
  93.8 5.6 %collective-permute-start.7 = (bf16[40,4096]{1,0:T(8,128)(2,1)}, bf16[40,4096]{1,0:T(8,128)(2,1)}, u32[]{:S(2)}, u32[]{:S(2)}) collective-permute-start(bf16[40,4096]{1,0:T(8,128)(2,1)} %collective-permute-done.2), channel_id=1, source_target_pairs={{0,32},{32,64},{64,96},{96,112},{112,80},{80,48},{48,16},{16,0},{1... | collective-permute-start | bytes 983048 | tf_op jit(solution)/shard_map/ppermute | solution.py:64
  99.4 1.0 constant_dynamic-update-slice_fusion.1
  100.4 1.9 collective-permute-start.8
  102.3 1.0 constant_dynamic-update-slice_fusion
  103.3 3.8 %fusion.84 = f32[576,200]{1,0:T(8,128)S(1)} fusion(bf16[576,4096]{1,0:T(8,128)(2,1)} %constant_dynamic-update-slice_fusion.5, bf16[200,4096]{1,0:T(8,128)(2,1)S(1)} %constant_dynamic-update-slice_fusion), kind=kOutput, calls=%fused_computation.163 | convolution fusion | flops 943718400 | bytes 6817792 | tf_op jit(solution)/shard_map/dot_general | solution.py:17
  107.1 0.8 slice.160
  108.2 3.3 %collective-permute-start.11 = (bf16[104,4096]{1,0:T(8,128)(2,1)S(1)}, bf16[104,4096]{1,0:T(8,128)(2,1)S(1)}, u32[]{:S(2)}, u32[]{:S(2)}) collective-permute-start(bf16[104,4096]{1,0:T(8,128)(2,1)S(1)} %pad.15), channel_id=1, source_target_pairs={{0,128},{128,0},{256,384},{384,256},{1,129},{129,1},{257,385},{385... | collective-permute-start | bytes 2555912 | tf_op jit(solution)/shard_map/ppermute | solution.py:54
  111.5 4.6 %collective-permute-start.12 = (bf16[104,4096]{1,0:T(8,128)(2,1)S(1)}, bf16[104,4096]{1,0:T(8,128)(2,1)}, u32[]{:S(2)}, u32[]{:S(2)}) collective-permute-start(bf16[104,4096]{1,0:T(8,128)(2,1)S(1)} %pad.15), channel_id=1, source_target_pairs={{0,256},{128,384},{256,0},{384,128},{1,257},{129,385},{257,1},{385... | collective-permute-start | bytes 2555912 | tf_op jit(solution)/shard_map/ppermute | solution.py:54
  116.1 2.6 %collective-permute-start.13 = (bf16[104,4096]{1,0:T(8,128)(2,1)S(1)}, bf16[104,4096]{1,0:T(8,128)(2,1)}, u32[]{:S(2)}, u32[]{:S(2)}) collective-permute-start(bf16[104,4096]{1,0:T(8,128)(2,1)S(1)} %pad.15), channel_id=1, source_target_pairs={{0,384},{128,256},{256,128},{384,0},{1,385},{129,257},{257,129},{3... | collective-permute-start | bytes 2555912 | tf_op jit(solution)/shard_map/ppermute | solution.py:54
  118.7 0.9 slice.165
  119.6 2.8 %collective-permute-start.10 = (bf16[40,2048]{1,0:T(8,128)(2,1)S(1)}, bf16[40,2048]{1,0:T(8,128)(2,1)S(1)}, u32[]{:S(2)}, u32[]{:S(2)}) collective-permute-start(bf16[40,2048]{1,0:T(8,128)(2,1)S(1)} %slice.165), channel_id=1, source_target_pairs={{32,0},{64,32},{96,64},{112,96},{80,112},{48,80},{16,48},{0,16},{3... | collective-permute-start | bytes 491528 | tf_op jit(solution)/shard_map/ppermute | solution.py:64
  122.5 0.9 slice.164
  123.4 5.1 %collective-permute-start.9 = (bf16[40,2048]{1,0:T(8,128)(2,1)S(1)}, bf16[40,2048]{1,0:T(8,128)(2,1)S(1)}, u32[]{:S(2)}, u32[]{:S(2)}) collective-permute-start(bf16[40,2048]{1,0:T(8,128)(2,1)S(1)} %slice.164), channel_id=1, source_target_pairs={{0,32},{32,64},{64,96},{96,112},{112,80},{80,48},{48,16},{16,0},{1... | collective-permute-start | bytes 491528 | tf_op jit(solution)/shard_map/ppermute | solution.py:64
  128.7 0.4 collective-permute-done.10
  129.0 2.8 %collective-permute-done.9 = bf16[40,2048]{1,0:T(8,128)(2,1)S(1)} collective-permute-done((bf16[40,2048]{1,0:T(8,128)(2,1)S(1)}, bf16[40,2048]{1,0:T(8,128)(2,1)S(1)}, u32[]{:S(2)}, u32[]{:S(2)}) %collective-permute-start.9) | collective-permute-done | bytes 163872 | tf_op jit(solution)/shard_map/ppermute | solution.py:64
  131.9 3.9 %fusion.81 = f32[576,120]{1,0:T(8,128)S(1)} fusion(bf16[576,4096]{1,0:T(8,128)(2,1)} %constant_dynamic-update-slice_fusion.5, bf16[40,2048]{1,0:T(8,128)(2,1)S(1)} %collective-permute-done.10, bf16[40,2048]{1,0:T(8,128)(2,1)S(1)} %collective-permute-done.9, bf16[40,4096]{1,0:T(8,128)(2,1)} %collective-permute-done.8, ...), kind=kOutput, calls=%fused_computation.160 | convolution fusion | flops 570163200 | bytes 5978112 | tf_op jit(solution)/shard_map/dot_general | solution.py:17
  136.0 0.3 fusion.12
  136.3 0.6 convolution_convert_fusion.1
  136.9 0.7 fusion.83
  137.6 0.6 slice.170
  138.2 0.8 broadcast_in_dim.65
  139.0 9.1 %all-to-all-start.1 = ((bf16[8,240,128]{2,1,0:T(8,128)(2,1)}), bf16[8,240,128]{2,1,0:T(8,128)(2,1)}, u32[]{:S(2)}, u32[]{:S(2)}) async-start(bf16[8,240,128]{2,1,0:T(8,128)(2,1)} %broadcast_in_dim.65), calls=%async_computation.1 | async-start | bytes 983040 | tf_op jit(solution)/shard_map/all_to_all | solution.py:124
  148.2 1.1 maximum_maximum_fusion
  149.5 0.8 pad.16
  150.3 2.1 %collective-permute-start.14 = (bf16[64,4096]{1,0:T(8,128)(2,1)}, bf16[64,4096]{1,0:T(8,128)(2,1)}, u32[]{:S(2)}, u32[]{:S(2)}) collective-permute-start(bf16[64,4096]{1,0:T(8,128)(2,1)} %pad.16), channel_id=1, source_target_pairs={{0,128},{128,0},{256,384},{384,256},{1,129},{129,1},{257,385},{385... | collective-permute-start | bytes 1572872 | tf_op jit(solution)/shard_map/ppermute | solution.py:54
  152.4 5.8 %collective-permute-start.15 = (bf16[64,4096]{1,0:T(8,128)(2,1)}, bf16[64,4096]{1,0:T(8,128)(2,1)}, u32[]{:S(2)}, u32[]{:S(2)}) collective-permute-start(bf16[64,4096]{1,0:T(8,128)(2,1)} %pad.16), channel_id=1, source_target_pairs={{0,256},{128,384},{256,0},{384,128},{1,257},{129,385},{257,1},{385... | collective-permute-start | bytes 1572872 | tf_op jit(solution)/shard_map/ppermute | solution.py:54
  158.9 2.6 %collective-permute-start.16 = (bf16[64,4096]{1,0:T(8,128)(2,1)}, bf16[64,4096]{1,0:T(8,128)(2,1)}, u32[]{:S(2)}, u32[]{:S(2)}) collective-permute-start(bf16[64,4096]{1,0:T(8,128)(2,1)} %pad.16), channel_id=1, source_target_pairs={{0,384},{128,256},{256,128},{384,0},{1,385},{129,257},{257,129},{3... | collective-permute-start | bytes 1572872 | tf_op jit(solution)/shard_map/ppermute | solution.py:54
  161.5 1.8 pad_maximum_fusion
  163.3 7.3 %all-to-all-done.1 = bf16[8,240,128]{2,1,0:T(8,128)(2,1)} async-done(((bf16[8,240,128]{2,1,0:T(8,128)(2,1)}), bf16[8,240,128]{2,1,0:T(8,128)(2,1)}, u32[]{:S(2)}, u32[]{:S(2)}) %all-to-all-start.1) | async-done | bytes 491552 | tf_op jit(solution)/shard_map/all_to_all | solution.py:124
  170.7 1.1 fusion.82
  171.8 1.1 fusion.3
  172.9 1.0 fusion.4
  174.0 0.2 fusion.5
  174.2 0.2 fusion.6
  174.4 0.9 pad_maximum_fusion.3
  175.3 4.2 %all-to-all-start.2 = ((bf16[4,48,1536]{2,1,0:T(8,128)(2,1)}), bf16[4,48,1536]{2,1,0:T(8,128)(2,1)}, u32[]{:S(2)}, u32[]{:S(2)}) async-start(bf16[4,48,1536]{2,1,0:T(8,128)(2,1)} %bitcast.47), calls=%async_computation.2 | async-start | bytes 1179648 | tf_op jit(solution)/shard_map/all_to_all | solution.py:134
  179.5 1.2 slice.177
  181.3 1.1 broadcast_add_fusion.1
  182.4 6.8 %collective-permute-done.16 = bf16[64,4096]{1,0:T(8,128)(2,1)} collective-permute-done((bf16[64,4096]{1,0:T(8,128)(2,1)}, bf16[64,4096]{1,0:T(8,128)(2,1)}, u32[]{:S(2)}, u32[]{:S(2)}) %collective-permute-start.16) | collective-permute-done | bytes 524320 | tf_op jit(solution)/shard_map/ppermute | solution.py:54
  189.3 1.6 pad_maximum_fusion.1
  190.9 0.5 fusion.39
  191.4 2.1 %fusion.1 = f32[1,128,4096]{2,1,0:T(8,128)} fusion(f32[128,4096]{1,0:T(8,128)S(1)} %fusion.39, bf16[416,4096]{1,0:T(8,128)(2,1)S(1)} %pad_maximum_fusion, s32[]{:T(128)S(6)} %select_n.186), kind=kOutput, calls=%fused_computation.2 | convolution fusion | flops 437256192 | bytes 7708676 | tf_op jit(solution)/shard_map/dot_general | solution.py:21
  193.5 1.9 convert_add_fusion
  (84 shorter events, 1.9 us)
Async XLA Ops:
  0.6 12.6 %copy-start.11 = (s32[160,8]{0,1:T(8,128)S(1)}, s32[160,8]{0,1:T(8,128)}, u32[]{:S(2)}) copy-start(s32[160,8]{0,1:T(8,128)} %param.11) | copy-start | bytes 15364
  0.6 12.6 %copy-start.10 = (s32[160,8]{0,1:T(8,128)S(1)}, s32[160,8]{0,1:T(8,128)}, u32[]{:S(2)}) copy-start(s32[160,8]{0,1:T(8,128)} %param.12) | copy-start | bytes 15364
  0.7 13.7 %copy-start.12 = (bf16[160,256]{1,0:T(8,128)(2,1)S(1)}, bf16[160,256]{1,0:T(8,128)(2,1)}, u32[]{:S(2)}) copy-start(bf16[160,256]{1,0:T(8,128)(2,1)} %param.10) | copy-start | bytes 245764
  0.7 13.7 %copy-start.13 = (bf16[160,256]{1,0:T(8,128)(2,1)S(1)}, bf16[160,256]{1,0:T(8,128)(2,1)}, u32[]{:S(2)}) copy-start(bf16[160,256]{1,0:T(8,128)(2,1)} %param.9) | copy-start | bytes 245764
  0.7 30.8 %copy-start = (bf16[1,48,4096]{2,1,0:T(8,128)(2,1)S(1)}, bf16[1,48,4096]{2,1,0:T(8,128)(2,1)}, u32[]{:S(2)}) copy-start(bf16[1,48,4096]{2,1,0:T(8,128)(2,1)} %param.13) | copy-start | bytes 1179652
  3.1 29.2 %copy-start.1 = (bf16[1,48,4096]{2,1,0:T(8,128)(2,1)S(1)}, bf16[1,48,4096]{2,1,0:T(8,128)(2,1)}, u32[]{:S(2)}) copy-start(bf16[1,48,4096]{2,1,0:T(8,128)(2,1)} %param.14) | copy-start | bytes 1179652
  3.1 29.9 %copy-start.15 = (s32[3]{0:T(128)S(1)}, s32[3]{0:T(128)}, u32[]{:S(2)}) copy-start(s32[3]{0:T(128)} %constant.207) | copy-start | bytes 40
  3.1 30.1 %copy-start.14 = (s32[5]{0:T(128)S(1)}, s32[5]{0:T(128)}, u32[]{:S(2)}) copy-start(s32[5]{0:T(128)} %constant.206) | copy-start | bytes 64
  3.1 30.3 %copy-start.2 = (bf16[1,48,4096]{2,1,0:T(8,128)(2,1)S(1)}, bf16[1,48,4096]{2,1,0:T(8,128)(2,1)}, u32[]{:S(2)}) copy-start(bf16[1,48,4096]{2,1,0:T(8,128)(2,1)} %param.15) | copy-start | bytes 1179652
  3.1 81.3 %collective-permute-start.4 = (bf16[144,4096]{1,0:T(8,128)(2,1)}, bf16[144,4096]{1,0:T(8,128)(2,1)S(1)}, u32[]{:S(2)}, u32[]{:S(2)}) collective-permute-start(bf16[144,4096]{1,0:T(8,128)(2,1)} %pad_maximum_fusion.2), channel_id=1, source_target_pairs={{0,128},{128,0},{256,384},{384,256},{1,129},{129,1},{257,385},{385... | collective-permute-start | bytes 3538952 | tf_op jit(solution)/shard_map/ppermute | solution.py:54
  6.6 79.0 %collective-permute-start.5 = (bf16[144,4096]{1,0:T(8,128)(2,1)}, bf16[144,4096]{1,0:T(8,128)(2,1)}, u32[]{:S(2)}, u32[]{:S(2)}) collective-permute-start(bf16[144,4096]{1,0:T(8,128)(2,1)} %pad_maximum_fusion.2), channel_id=1, source_target_pairs={{0,384},{128,256},{256,128},{384,0},{1,385},{129,257},{257,129},{3... | collective-permute-start | bytes 3538952 | tf_op jit(solution)/shard_map/ppermute | solution.py:54
  10.7 77.4 %collective-permute-start.6 = (bf16[144,4096]{1,0:T(8,128)(2,1)}, bf16[144,4096]{1,0:T(8,128)(2,1)}, u32[]{:S(2)}, u32[]{:S(2)}) collective-permute-start(bf16[144,4096]{1,0:T(8,128)(2,1)} %pad_maximum_fusion.2), channel_id=1, source_target_pairs={{0,256},{128,384},{256,0},{384,128},{1,257},{129,385},{257,1},{385... | collective-permute-start | bytes 3538952 | tf_op jit(solution)/shard_map/ppermute | solution.py:54
  15.4 40.6 %all-to-all-start = ((bf16[16,40,256]{2,1,0:T(8,128)(2,1)}), bf16[16,40,256]{2,1,0:T(8,128)(2,1)S(1)}, u32[]{:S(2)}, u32[]{:S(2)}) async-start(bf16[16,40,256]{2,1,0:T(8,128)(2,1)} %bitcast.1), calls=%async_computation | async-start | bytes 655360 | tf_op jit(solution)/shard_map/all_to_all | solution.py:50
  56.0 23.7 %collective-permute-start = (bf16[40,4096]{1,0:T(8,128)(2,1)S(1)}, bf16[40,4096]{1,0:T(8,128)(2,1)S(1)}, u32[]{:S(2)}, u32[]{:S(2)}) collective-permute-start(bf16[40,4096]{1,0:T(8,128)(2,1)S(1)} %bitcast.52), channel_id=1, source_target_pairs={{0,32},{32,64},{64,96},{96,112},{112,80},{80,48},{48,16},{16,0},{1... | collective-permute-start | bytes 983048 | tf_op jit(solution)/shard_map/ppermute | solution.py:64
  60.4 14.8 %collective-permute-start.1 = (bf16[40,4096]{1,0:T(8,128)(2,1)S(1)}, bf16[40,4096]{1,0:T(8,128)(2,1)S(1)}, u32[]{:S(2)}, u32[]{:S(2)}) collective-permute-start(bf16[40,4096]{1,0:T(8,128)(2,1)S(1)} %bitcast.53), channel_id=1, source_target_pairs={{32,0},{64,32},{96,64},{112,96},{80,112},{48,80},{16,48},{0,16},{3... | collective-permute-start | bytes 983048 | tf_op jit(solution)/shard_map/ppermute | solution.py:64
  76.4 24.0 %collective-permute-start.3 = (bf16[40,4096]{1,0:T(8,128)(2,1)S(1)}, bf16[40,4096]{1,0:T(8,128)(2,1)}, u32[]{:S(2)}, u32[]{:S(2)}) collective-permute-start(bf16[40,4096]{1,0:T(8,128)(2,1)S(1)} %collective-permute-done.1), channel_id=1, source_target_pairs={{32,0},{64,32},{96,64},{112,96},{80,112},{48,80},{16,48},{0,16},{3... | collective-permute-start | bytes 983048 | tf_op jit(solution)/shard_map/ppermute | solution.py:64
  79.7 14.0 %collective-permute-start.2 = (bf16[40,4096]{1,0:T(8,128)(2,1)S(1)}, bf16[40,4096]{1,0:T(8,128)(2,1)}, u32[]{:S(2)}, u32[]{:S(2)}) collective-permute-start(bf16[40,4096]{1,0:T(8,128)(2,1)S(1)} %collective-permute-done), channel_id=1, source_target_pairs={{0,32},{32,64},{64,96},{96,112},{112,80},{80,48},{48,16},{16,0},{1... | collective-permute-start | bytes 983048 | tf_op jit(solution)/shard_map/ppermute | solution.py:64
  93.8 28.7 %collective-permute-start.7 = (bf16[40,4096]{1,0:T(8,128)(2,1)}, bf16[40,4096]{1,0:T(8,128)(2,1)}, u32[]{:S(2)}, u32[]{:S(2)}) collective-permute-start(bf16[40,4096]{1,0:T(8,128)(2,1)} %collective-permute-done.2), channel_id=1, source_target_pairs={{0,32},{32,64},{64,96},{96,112},{112,80},{80,48},{48,16},{16,0},{1... | collective-permute-start | bytes 983048 | tf_op jit(solution)/shard_map/ppermute | solution.py:64
  100.4 18.3 %collective-permute-start.8 = (bf16[40,4096]{1,0:T(8,128)(2,1)}, bf16[40,4096]{1,0:T(8,128)(2,1)}, u32[]{:S(2)}, u32[]{:S(2)}) collective-permute-start(bf16[40,4096]{1,0:T(8,128)(2,1)} %collective-permute-done.3), channel_id=1, source_target_pairs={{32,0},{64,32},{96,64},{112,96},{80,112},{48,80},{16,48},{0,16},{3... | collective-permute-start | bytes 983048 | tf_op jit(solution)/shard_map/ppermute | solution.py:64
  108.1 20.4 %copy-start.5 = (f32[4,48,180]{2,1,0:T(8,128)S(1)}, f32[4,48,180]{2,1,0:T(8,128)}, u32[]{:S(2)}) copy-start(f32[4,48,180]{2,1,0:T(8,128)} %slice.160) | copy-start | bytes 414724
  108.2 50.7 %collective-permute-start.11 = (bf16[104,4096]{1,0:T(8,128)(2,1)S(1)}, bf16[104,4096]{1,0:T(8,128)(2,1)S(1)}, u32[]{:S(2)}, u32[]{:S(2)}) collective-permute-start(bf16[104,4096]{1,0:T(8,128)(2,1)S(1)} %pad.15), channel_id=1, source_target_pairs={{0,128},{128,0},{256,384},{384,256},{1,129},{129,1},{257,385},{385... | collective-permute-start | bytes 2555912 | tf_op jit(solution)/shard_map/ppermute | solution.py:54
  111.5 50.0 %collective-permute-start.12 = (bf16[104,4096]{1,0:T(8,128)(2,1)S(1)}, bf16[104,4096]{1,0:T(8,128)(2,1)}, u32[]{:S(2)}, u32[]{:S(2)}) collective-permute-start(bf16[104,4096]{1,0:T(8,128)(2,1)S(1)} %pad.15), channel_id=1, source_target_pairs={{0,256},{128,384},{256,0},{384,128},{1,257},{129,385},{257,1},{385... | collective-permute-start | bytes 2555912 | tf_op jit(solution)/shard_map/ppermute | solution.py:54
  116.1 45.4 %collective-permute-start.13 = (bf16[104,4096]{1,0:T(8,128)(2,1)S(1)}, bf16[104,4096]{1,0:T(8,128)(2,1)}, u32[]{:S(2)}, u32[]{:S(2)}) collective-permute-start(bf16[104,4096]{1,0:T(8,128)(2,1)S(1)} %pad.15), channel_id=1, source_target_pairs={{0,384},{128,256},{256,128},{384,0},{1,385},{129,257},{257,129},{3... | collective-permute-start | bytes 2555912 | tf_op jit(solution)/shard_map/ppermute | solution.py:54
  119.6 9.4 %collective-permute-start.10 = (bf16[40,2048]{1,0:T(8,128)(2,1)S(1)}, bf16[40,2048]{1,0:T(8,128)(2,1)S(1)}, u32[]{:S(2)}, u32[]{:S(2)}) collective-permute-start(bf16[40,2048]{1,0:T(8,128)(2,1)S(1)} %slice.165), channel_id=1, source_target_pairs={{32,0},{64,32},{96,64},{112,96},{80,112},{48,80},{16,48},{0,16},{3... | collective-permute-start | bytes 491528 | tf_op jit(solution)/shard_map/ppermute | solution.py:64
  123.4 8.5 %collective-permute-start.9 = (bf16[40,2048]{1,0:T(8,128)(2,1)S(1)}, bf16[40,2048]{1,0:T(8,128)(2,1)S(1)}, u32[]{:S(2)}, u32[]{:S(2)}) collective-permute-start(bf16[40,2048]{1,0:T(8,128)(2,1)S(1)} %slice.164), channel_id=1, source_target_pairs={{0,32},{32,64},{64,96},{96,112},{112,80},{80,48},{48,16},{16,0},{1... | collective-permute-start | bytes 491528 | tf_op jit(solution)/shard_map/ppermute | solution.py:64
  129.0 6.7 %copy-start.6 = (bf16[40,2048]{1,0:T(8,128)(2,1)}, bf16[40,2048]{1,0:T(8,128)(2,1)S(1)}, u32[]{:S(2)}) copy-start(bf16[40,2048]{1,0:T(8,128)(2,1)S(1)} %collective-permute-done.10) | copy-start | bytes 491524
  131.8 4.0 %copy-start.8 = (bf16[40,2048]{1,0:T(8,128)(2,1)}, bf16[40,2048]{1,0:T(8,128)(2,1)S(1)}, u32[]{:S(2)}) copy-start(bf16[40,2048]{1,0:T(8,128)(2,1)S(1)} %collective-permute-done.9) | copy-start | bytes 491524
  135.9 12.3 %copy-start.7 = (bf16[40,2048]{1,0:T(8,128)(2,1)S(1)}, bf16[40,2048]{1,0:T(8,128)(2,1)}, u32[]{:S(2)}) copy-start(bf16[40,2048]{1,0:T(8,128)(2,1)} %copy-done.6) | copy-start | bytes 491524
  135.9 12.3 %copy-start.9 = (bf16[40,2048]{1,0:T(8,128)(2,1)S(1)}, bf16[40,2048]{1,0:T(8,128)(2,1)}, u32[]{:S(2)}) copy-start(bf16[40,2048]{1,0:T(8,128)(2,1)} %copy-done.8) | copy-start | bytes 491524
  136.9 12.4 %copy-start.3 = (bf16[192,640]{1,0:T(8,128)(2,1)}, bf16[192,640]{1,0:T(8,128)(2,1)S(1)}, u32[]{:S(2)}) copy-start(bf16[192,640]{1,0:T(8,128)(2,1)S(1)} %convolution_convert_fusion.1) | copy-start | bytes 737284
  139.0 31.6 %all-to-all-start.1 = ((bf16[8,240,128]{2,1,0:T(8,128)(2,1)}), bf16[8,240,128]{2,1,0:T(8,128)(2,1)}, u32[]{:S(2)}, u32[]{:S(2)}) async-start(bf16[8,240,128]{2,1,0:T(8,128)(2,1)} %broadcast_in_dim.65), calls=%async_computation.1 | async-start | bytes 983040 | tf_op jit(solution)/shard_map/all_to_all | solution.py:124
  150.3 32.1 %collective-permute-start.14 = (bf16[64,4096]{1,0:T(8,128)(2,1)}, bf16[64,4096]{1,0:T(8,128)(2,1)}, u32[]{:S(2)}, u32[]{:S(2)}) collective-permute-start(bf16[64,4096]{1,0:T(8,128)(2,1)} %pad.16), channel_id=1, source_target_pairs={{0,128},{128,0},{256,384},{384,256},{1,129},{129,1},{257,385},{385... | collective-permute-start | bytes 1572872 | tf_op jit(solution)/shard_map/ppermute | solution.py:54
  152.4 30.0 %collective-permute-start.15 = (bf16[64,4096]{1,0:T(8,128)(2,1)}, bf16[64,4096]{1,0:T(8,128)(2,1)}, u32[]{:S(2)}, u32[]{:S(2)}) collective-permute-start(bf16[64,4096]{1,0:T(8,128)(2,1)} %pad.16), channel_id=1, source_target_pairs={{0,256},{128,384},{256,0},{384,128},{1,257},{129,385},{257,1},{385... | collective-permute-start | bytes 1572872 | tf_op jit(solution)/shard_map/ppermute | solution.py:54
  158.9 2.6 %copy-start.4 = (bf16[104,4096]{1,0:T(8,128)(2,1)}, bf16[104,4096]{1,0:T(8,128)(2,1)S(1)}, u32[]{:S(2)}) copy-start(bf16[104,4096]{1,0:T(8,128)(2,1)S(1)} %collective-permute-done.11) | copy-start | bytes 2555908
  158.9 30.4 %collective-permute-start.16 = (bf16[64,4096]{1,0:T(8,128)(2,1)}, bf16[64,4096]{1,0:T(8,128)(2,1)}, u32[]{:S(2)}, u32[]{:S(2)}) collective-permute-start(bf16[64,4096]{1,0:T(8,128)(2,1)} %pad.16), channel_id=1, source_target_pairs={{0,384},{128,256},{256,128},{384,0},{1,385},{129,257},{257,129},{3... | collective-permute-start | bytes 1572872 | tf_op jit(solution)/shard_map/ppermute | solution.py:54
  175.3 18.1 %all-to-all-start.2 = ((bf16[4,48,1536]{2,1,0:T(8,128)(2,1)}), bf16[4,48,1536]{2,1,0:T(8,128)(2,1)}, u32[]{:S(2)}, u32[]{:S(2)}) async-start(bf16[4,48,1536]{2,1,0:T(8,128)(2,1)} %bitcast.47), calls=%async_computation.2 | async-start | bytes 1179648 | tf_op jit(solution)/shard_map/all_to_all | solution.py:134
